TPU v7x, 512 devices: a whole 4x4x16 slice. The times are simulated.
512 devices in a mesh: seq: 32 (over y_lo, z), head: 16 (over x, y_hi, core).
Axes of the slice: x: 4, y: 4 (y_hi: 2, y_lo: 2; y = y_hi * 2 + y_lo), z: 16, core: 2. Of those that a mesh axis runs over, the one named last changes fastest.
Arguments:
- queries: bfloat16 [4096, 8192], P('seq', 'head'), may hold values from -6 to 6
- vision: bfloat16 [6400, 8192], P('seq'), may hold values from -6 to 6
- kv_weight: bfloat16 [2, 8192, 1024], P(None, None, 'head'), may hold values from -0.75 to 0.75
- out_weight: bfloat16 [8192, 8192], P('head', 'seq'), may hold values from -0.125 to 0.125
- q_gain: float32 [128], replicated, may hold values from 0.1 to 1.9
- k_gain: float32 [128], replicated, may hold values from 0.1 to 1.9
- tile_counts: int32 [4], replicated, may hold values from 800 to 1600, as said below
- spans: int32 [4096, 2], P('seq'), may hold values from 0 to 4, as said below
Outputs:
- output: bfloat16 [4096, 8192], P('seq', 'head')
Inputs may be any that keep to these rules, and one draw needn't show every extreme that they name: `tile_counts`: every tile holds at least 800 vision tokens in its first slots; one tile is full with exactly 1600. For every token spans[t, 0] < spans[t, 1], so each token attends one or more whole tiles.
All inputs are finite; a program needn't handle non-finite values.
Results may differ from a plain program's by a relative error of at most 0.0085.
Values may be sent and summed in bfloat16 or wider, within the bound.
No kernel may reach another device: no remote copies, remote signals or barrier semaphores. Data moves between devices by JAX's collectives and lax.ppermute only.
A program may use at most 64 MiB of HBM per device.

v0:
```python
import math

import jax
import jax.numpy as jnp
from jax import lax
from jax.sharding import PartitionSpec as P

HD = 128
TILES = 4


EPSILON = 1e-05


def swapped(value, axis, apart):
    mask = 2**apart
    pairs = [(source, source ^ mask) for source in range(lax.axis_size(axis))]
    return lax.ppermute(value, axis, pairs)


def rms_scale(field, gain):
    mean_sq = jnp.mean(field * field, axis=-1, keepdims=True)
    return field / jnp.sqrt(mean_sq + EPSILON) * gain


def local(queries, vision, kv_weight, out_weight, q_gain, k_gain, tile_counts, spans):
    row_count = queries.shape[0]
    heads_here = queries.shape[1] // HD
    half_cols = kv_weight.shape[2]
    vis_local = vision.shape[0]
    slot_cap = vis_local * lax.axis_size("seq") // TILES
    factor = 1.0 / math.sqrt(HD)
    query_f = queries.astype(jnp.float32).reshape(row_count, heads_here, HD)
    q_normed = rms_scale(query_f, q_gain).astype(jnp.bfloat16)
    both_weights = jnp.concatenate([kv_weight[0], kv_weight[1]], axis=1)
    projected = jnp.dot(vision, both_weights, preferred_element_type=jnp.float32)
    key_raw = projected[:, :half_cols]
    value_half = projected[:, half_cols:].astype(jnp.bfloat16)
    own_squares = jnp.sum(key_raw * key_raw, axis=1)
    other_squares = swapped(own_squares, "head", 0)
    inverse = 1.0 / jnp.sqrt((own_squares + other_squares) / HD + EPSILON)
    parity = lax.axis_index("head") % 2
    gain_half = lax.dynamic_slice_in_dim(k_gain, parity * half_cols, half_cols)
    key_half = (key_raw * inverse[:, None] * gain_half[None, :]).astype(jnp.bfloat16)
    local_pair = jnp.concatenate([key_half, value_half], axis=1)
    first_tile = spans[:, 0]
    end_tile = spans[:, 1]
    tile_ids = jnp.arange(TILES, dtype=jnp.int32)
    numer = jnp.zeros((row_count, heads_here, HD), jnp.float32)
    totals = jnp.zeros((heads_here, row_count), jnp.float32)
    gathered = lax.all_gather(local_pair, "seq", axis=0, tiled=True)
    partner = swapped(gathered, "head", 0)
    lower_half = jnp.where(parity == 0, gathered, partner)
    upper_half = jnp.where(parity == 0, partner, gathered)
    assemble_key_block = jnp.concatenate(
        [lower_half[:, :half_cols], upper_half[:, :half_cols]], axis=1
    )
    assemble_value_block = jnp.concatenate(
        [lower_half[:, half_cols:], upper_half[:, half_cols:]], axis=1
    )
    for tile_index in range(TILES):
        key_block = assemble_key_block[tile_index * slot_cap : (tile_index + 1) * slot_cap]
        value_block = assemble_value_block[tile_index * slot_cap : (tile_index + 1) * slot_cap]
        key_index = tile_index * slot_cap + jnp.arange(key_block.shape[0], dtype=jnp.int32)
        tile_of = key_index // slot_cap
        slot_of = key_index % slot_cap
        count_of = jnp.sum(
            jnp.where(tile_of[:, None] == tile_ids[None, :], tile_counts[None, :], 0), axis=1
        )
        allowed = (
            (slot_of < count_of)[None, :]
            & (first_tile[:, None] <= tile_of[None, :])
            & (tile_of[None, :] < end_tile[:, None])
        )
        scores = (
            jnp.einsum("rhd,nd->hrn", q_normed, key_block, preferred_element_type=jnp.float32)
            * factor
        )
        weights = jnp.where(allowed[None, :, :], jnp.exp(scores), jnp.zeros_like(scores))
        total_part = jnp.sum(weights, axis=2)
        numer_part = jnp.einsum(
            "hrn,nd->rhd",
            weights.astype(jnp.bfloat16),
            value_block,
            preferred_element_type=jnp.float32,
        )
        numer_part, total_part = (numer_part, total_part)
        numer = numer + numer_part
        totals = totals + total_part
    attended = (
        (numer / jnp.transpose(totals)[:, :, None])
        .astype(jnp.bfloat16)
        .reshape(row_count, heads_here * HD)
    )
    partial_value = jnp.dot(
        attended,
        lax.all_gather(out_weight, "seq", axis=1, tiled=True),
        preferred_element_type=jnp.float32,
    )
    return lax.psum_scatter(partial_value, "head", scatter_dimension=1, tiled=True).astype(
        jnp.bfloat16
    )


def solution(mesh):
    return jax.shard_map(
        local,
        mesh=mesh,
        in_specs=(
            P("seq", "head"),
            P("seq", None),
            P(None, None, "head"),
            P("head", "seq"),
            P(),
            P(),
            P(),
            P("seq", None),
        ),
        out_specs=P("seq", "head"),
        check_vma=False,
    )
```

profile of v0, /device:TPU:6, one launch (start us, length us, event | category | flops | bytes accessed | tf_op | source)
XLA Modules:
  0.0 436.2 jit_solution(855481910128351020)
XLA Ops:
  6.5 1.8 slice_bitcast_fusion.1
  8.4 0.7 copy-done
  9.1 1.1 fusion.30
  10.2 0.1 multiply_reduce_fusion.1
  10.3 1.9 collective-permute-start
  12.3 0.1 slice.158
  12.4 0.1 dynamic_slice.3
  12.5 0.9 collective-permute-done
  13.4 0.1 multiply_convert_fusion.1
  13.5 0.7 pad_maximum_fusion.2
  14.3 0.7 all-gather.5.cloned.1.call-update
  15.0 1.0 copy.20
  16.1 135.8 %all-gather.3.cloned.1.call-done = bf16[6400,128]{1,0:T(8,128)(2,1)} async-done(((bf16[200,128]{1,0:T(8,128)(2,1)}), bf16[6400,128]{1,0:T(8,128)(2,1)}) %all-gather.3.cloned.1.call-update) | async-done | bytes 1638416 | tf_op jit(solution)/shard_map/all_gather | solution.py:51
  151.9 1.9 collective-permute-start.1
  153.8 0.1 select_reduce_fusion
  154.0 0.8 copy.23
  154.9 1.1 multiply_convert_fusion
  156.0 2.1 compare_and_fusion
  158.1 2.1 broadcast_select_fusion
  160.2 1.1 fusion.81
  161.3 1.1 fusion.84
  162.4 1.1 fusion.86
  163.5 1.1 fusion.85
  164.6 1.1 fusion.83
  165.7 0.6 fusion.6
  166.3 0.6 fusion.8
  166.9 0.6 fusion.15
  167.6 0.6 fusion.27
  168.2 154.0 %all-gather.5.cloned.1.call-done = bf16[512,8192]{1,0:T(8,128)(2,1)} async-done(((bf16[512,256]{1,0:T(8,128)(2,1)}), bf16[512,8192]{1,0:T(8,128)(2,1)}) %all-gather.5.cloned.1.call-update) | async-done | bytes 8388624 | tf_op jit(solution)/shard_map/all_gather | solution.py:97
  322.2 6.7 %fusion.87 = f32[128,8192]{1,0:T(8,128)} fusion(bf16[128,512]{0,1:T(8,128)(2,1)S(1)} %bitcast.74, bf16[512,8192]{1,0:T(8,128)(2,1)} %all-gather.5.cloned.1.call-done), kind=kOutput, calls=%fused_computation.131 | convolution fusion | flops 1073741824 | bytes 12713984 | tf_op jit(solution)/shard_map/dot_general | solution.py:95
  328.9 99.1 %reduce-scatter.2.cloned.1.call-done = f32[128,512]{1,0:T(8,128)} async-done(((f32[128,8192]{1,0:T(8,128)}), f32[128,512]{1,0:T(8,128)}) %reduce-scatter.2.cloned.1.call-update) | async-done | bytes 262160 | tf_op jit(solution)/shard_map/reduce_scatter | solution.py:100
  428.1 1.6 convert_element_type.33
  (26 shorter events, 0.3 us)
Async XLA Ops:
  6.5 2.6 copy-start
  6.5 145.4 %all-gather.3.cloned.1.call-start = ((), (), s32[]{:S(2)}) async-start(), calls=%async_computation.1 | async-start | bytes 1689600 | tf_op jit(solution)/shard_map/all_gather | solution.py:51
  9.1 3.3 copy-start.4
  9.1 144.7 %copy-start.2 = (s32[4]{0:T(128)S(1)}, s32[4]{0:T(128)}, u32[]{:S(2)}) copy-start(s32[4]{0:T(128)} %param.14) | copy-start | bytes 52
  10.2 144.6 %copy-start.1 = (s32[128,2]{0,1:T(2,128)S(1)}, s32[128,2]{0,1:T(2,128)}, u32[]{:S(2)}) copy-start(s32[128,2]{0,1:T(2,128)} %param.15) | copy-start | bytes 3076
  10.2 144.6 %copy-start.3 = (f32[128]{0:T(128)S(1)}, f32[128]{0:T(128)}, u32[]{:S(2)}) copy-start(f32[128]{0:T(128)} %param.12) | copy-start | bytes 1540
  10.3 3.0 collective-permute-start
  14.2 308.0 %all-gather.5.cloned.1.call-start = ((), (), s32[]{:S(2)}) async-start(), calls=%async_computation.2 | async-start | bytes 8650752 | tf_op jit(solution)/shard_map/all_gather | solution.py:97
  15.0 413.1 %reduce-scatter.2.cloned.1.call-start = ((), (), s32[]{:S(2)}) async-start(), calls=%async_computation.3 | async-start | bytes 4456448 | tf_op jit(solution)/shard_map/reduce_scatter | solution.py:100
  151.9 6.2 %collective-permute-start.1 = (bf16[6400,128]{1,0:T(8,128)(2,1)}, bf16[6400,128]{1,0:T(8,128)(2,1)}, u32[]{:S(2)}, u32[]{:S(2)}) collective-permute-start(bf16[6400,128]{1,0:T(8,128)(2,1)} %all-gather.3.cloned.1.call-done), channel_id=1, source_target_pairs={{0,1},{1,0},{2,3},{3,2},{4,5},{5,4},{6,7},{7,6},{8,9},{9,8},{10,11... | collective-permute-start | bytes 4915208 | tf_op jit(solution)/shard_map/ppermute | solution.py:18
Sparse Core Ops, SparseCore 0:
  14.3 137.5 all-gather.2
  153.9 168.2 all-gather.4
  329.1 98.9 reduce-scatter.1
where the time goes:
time: 437 us; the launch traced here: 436 us
  waiting for transfers between devices  391 us (89%)
  matrix products  14.6 us (3%)
  between operations  13.3 us (3%)
  other arithmetic  8.11 us (2%)
  local copies, waits for them, and re-layouts  5.67 us (1%)
    all_gather x1, waiting for transfers between devices, local(): lax.all_gather(out_weight, 'seq', axis=1, tiled=True)  154 us
    all_gather x1, waiting for transfers between devices, local(): gathered = lax.all_gather(local_pair, 'seq', axis=0, tiled=True)  136 us
    reduce_scatter x1, waiting for transfers between devices, local(): lax.psum_scatter(partial_value, 'head', scatter_dimension=1, tiled=True)  99.1 us
  transfers between devices with their start and end apart: 5, of which 4 were waited for; matrix products, arithmetic and copies ran while one was open for 4% of the time, Pallas kernels for 0%

commit v1 on v0

v1 whole, which is shorter than its diff:
```python
import math

import jax
import jax.numpy as jnp
from jax import lax
from jax.experimental import pallas as pl
from jax.experimental.pallas import tpu as pltpu
from jax.sharding import Mesh, PartitionSpec as P

HD = 128
TILES = 4
EPSILON = 1e-05
NEG = -1e30
AXES = ("ylo", "z", "x", "yhi", "core")
SIZES = (2, 16, 4, 2, 2)
ROWS = 128
HEADS = 8
LOCAL = 200
TAKE = 112
SHIFT = LOCAL - TAKE
SLOTS = 16 * TAKE
BF = jnp.bfloat16
F32 = jnp.float32


def flat(ylo, z, x, yhi, core):
    return (((ylo * 16 + z) * 4 + x) * 2 + yhi) * 2 + core


def swapped(value, axis):
    return lax.ppermute(value, axis, [(0, 1), (1, 0)])


def moved(value, cross):
    pairs = []
    for ylo in range(2):
        for z in range(16):
            for x in range(4):
                for yhi in range(2):
                    for core in range(2):
                        target = flat(x // 2, z, 2 * ylo + x % 2, yhi, core ^ cross)
                        pairs.append((flat(ylo, z, x, yhi, core), target))
    return lax.ppermute(value, AXES, pairs)


def rms_scale(field, gain):
    mean_sq = jnp.mean(field * field, axis=-1, keepdims=True)
    return field / jnp.sqrt(mean_sq + EPSILON) * gain


def attend_kernel(core_ref, q_ref, qx_ref, kv_ref, kx_ref, numer_ref, total_ref, key_s, value_s):
    step = pl.program_id(0)

    @pl.when(step == 0)
    def _():
        for z in range(16):
            rows = pl.ds(z * TAKE, TAKE)
            key_s[rows, :HD] = kv_ref[z, :TAKE]
            value_s[rows, :HD] = kv_ref[z, TAKE:]
        key_s[:, HD:] = kx_ref[...]
        value_s[:, HD:] = jnp.ones((SLOTS, HD), BF)
        total_ref[...] = jnp.zeros_like(total_ref)

    query = jnp.concatenate([q_ref[...], qx_ref[...]], axis=1)
    scores = lax.dot_general(
        query, key_s[...], (((1,), (1,)), ((), ())), preferred_element_type=F32
    )
    weights = jnp.exp2(scores * (math.log2(math.e) / math.sqrt(HD))).astype(BF)
    result = jnp.dot(weights, value_s[...], preferred_element_type=F32)
    numer_ref[...] = result[:, :HD]
    head = (step + 4 * core_ref[0]) % HEADS
    lane = lax.broadcasted_iota(jnp.int32, (2 * ROWS, HD), 1)
    total_ref[...] += jnp.where(lane == head, result[:, HD:], 0.0)


def attend(core, query, query_ext, gathered, key_ext):
    whole = lambda *dims: pl.BlockSpec(dims, lambda h, c: (0,) * len(dims))
    return pl.pallas_call(
        attend_kernel,
        grid_spec=pltpu.PrefetchScalarGridSpec(
            num_scalar_prefetch=1,
            grid=(HEADS,),
            in_specs=[
                pl.BlockSpec((2 * ROWS, HD), lambda h, c: (0, h)),
                whole(2 * ROWS, HD),
                whole(16, 2 * TAKE, HD),
                whole(SLOTS, HD),
            ],
            out_specs=[
                pl.BlockSpec((2 * ROWS, HD), lambda h, c: (0, (h + 4 * c[0]) % HEADS)),
                whole(2 * ROWS, HD),
            ],
            scratch_shapes=[
                pltpu.VMEM((SLOTS, 2 * HD), BF),
                pltpu.VMEM((SLOTS, 2 * HD), BF),
            ],
        ),
        out_shape=[
            jax.ShapeDtypeStruct((2 * ROWS, HEADS * HD), F32),
            jax.ShapeDtypeStruct((2 * ROWS, HD), F32),
        ],
        compiler_params=pltpu.CompilerParams(
            dimension_semantics=("arbitrary",), vmem_limit_bytes=48 << 20
        ),
        name="attend",
    )(core, query, query_ext, gathered, key_ext)


def project_kernel(a_ref, w_ref, o_ref):
    weight = jnp.concatenate([w_ref[0], w_ref[1]], axis=1)
    result = jnp.dot(a_ref[...], weight, preferred_element_type=F32).astype(BF)
    o_ref[0, 0] = result[:ROWS]
    o_ref[1, 0] = result[ROWS:]


def project(attended, weight):
    depth = HEADS * HD
    return pl.pallas_call(
        project_kernel,
        grid=(8,),
        in_specs=[
            pl.BlockSpec((2 * ROWS, depth), lambda j: (0, 0)),
            pl.BlockSpec((2, depth, 128), lambda j: (j, 0, 0)),
        ],
        out_specs=pl.BlockSpec((2, 1, ROWS, 256), lambda j: (0, j, 0, 0)),
        out_shape=jax.ShapeDtypeStruct((2, 8, ROWS, 256), BF),
        compiler_params=pltpu.CompilerParams(
            dimension_semantics=("arbitrary",), vmem_limit_bytes=48 << 20
        ),
        name="project",
    )(attended, weight)


def local(queries, vision, kv_weight, out_weight, q_gain, k_gain, tile_counts, spans):
    core = lax.axis_index("core")
    ylo = lax.axis_index("ylo")
    first = core == 0

    kept = lax.dynamic_slice_in_dim(out_weight, core * 128, 128, axis=1)
    sent = lax.dynamic_slice_in_dim(out_weight, (1 - core) * 128, 128, axis=1)
    got = swapped(sent, "core")
    upper = jnp.where(first, kept, got)
    lower = jnp.where(first, got, kept)
    weight = lax.all_gather(jnp.concatenate([upper, lower], axis=0), "z", axis=0, tiled=False)

    both = jnp.concatenate([kv_weight[0], kv_weight[1]], axis=1)
    projected = jnp.dot(vision, both, preferred_element_type=F32)
    mine = lax.dynamic_slice_in_dim(projected, core * SHIFT, TAKE, axis=0)
    theirs = swapped(lax.dynamic_slice_in_dim(projected, (1 - core) * SHIFT, TAKE, axis=0), "core")
    half = HD // 2
    left = jnp.where(first, mine, theirs)
    right = jnp.where(first, theirs, mine)
    key = rms_scale(jnp.concatenate([left[:, :half], right[:, :half]], axis=1), k_gain)
    value = jnp.concatenate([left[:, half:], right[:, half:]], axis=1)
    pair = jnp.concatenate([key, value], axis=0).astype(BF)
    gathered = lax.all_gather(pair, "z", axis=0, tiled=False)

    query_f = queries.astype(F32).reshape(ROWS, 4, HD)
    normed = rms_scale(query_f, q_gain).astype(BF).reshape(ROWS, 4 * HD)
    wide = jnp.concatenate([normed, swapped(normed, "core")], axis=1)
    other = swapped(wide, "ylo")
    other_spans = swapped(spans, "ylo")
    below = ylo == 0
    query = jnp.where(
        below, jnp.concatenate([wide, other], axis=0), jnp.concatenate([other, wide], axis=0)
    )
    span = jnp.where(
        below,
        jnp.concatenate([spans, other_spans], axis=0),
        jnp.concatenate([other_spans, spans], axis=0),
    )

    lane = jnp.arange(HD, dtype=jnp.int32)[None, :]
    inside = (span[:, :1] <= lane) & (lane < span[:, 1:])
    query_ext = jnp.where((lane <= TILES) & ~inside, NEG, 0.0).astype(BF)
    row = jnp.arange(SLOTS, dtype=jnp.int32)[:, None]
    block, item = row // TAKE, row % TAKE
    tile = 2 * ylo + block // 8
    slot = (block % 8) * LOCAL + core * SHIFT + item
    count = jnp.sum(jnp.where(tile == jnp.arange(TILES)[None, :], tile_counts[None, :], 0), axis=1)
    absent = (slot >= count[:, None]) | ((core == 1) & (item < 2 * TAKE - LOCAL))
    key_ext = jnp.where((lane == tile) | ((lane == TILES) & absent), 1.0, 0.0).astype(BF)

    numer, total = attend(
        jnp.reshape(core, (1,)).astype(jnp.int32), query, query_ext, gathered, key_ext
    )

    numer = numer + swapped(numer, "core")
    total = total + swapped(total, "core")
    high = lax.reduce_precision(total, 8, 7)
    low = jnp.concatenate([jnp.zeros((2 * ROWS, 8), F32), (total - high)[:, : HD - 8]], axis=1)
    payload = jnp.concatenate([numer, high + low], axis=1).astype(BF)
    rest = swapped(payload, "ylo").astype(F32)
    depth = HEADS * HD
    total = total[:, :HEADS] + (rest[:, depth : depth + 8] + rest[:, depth + 8 : depth + 16])
    attended = (
        ((numer + rest[:, :depth]).reshape(2 * ROWS, HEADS, HD) / total[:, :, None])
        .astype(BF)
        .reshape(2 * ROWS, depth)
    )

    partial = project(attended, weight).reshape(8, 2, ROWS, 256)
    parts = lax.all_to_all(partial, ("x", "yhi"), 0, 0, tiled=True)
    summed = jnp.sum(parts.astype(F32), axis=0).astype(BF)
    own = moved(lax.dynamic_index_in_dim(summed, core, 0, keepdims=False), 0)
    cross = moved(lax.dynamic_index_in_dim(summed, 1 - core, 0, keepdims=False), 1)
    even = jnp.where(first, own, cross)
    odd = jnp.where(first, cross, own)
    return jnp.concatenate([even[:, :128], odd[:, :128], even[:, 128:], odd[:, 128:]], axis=1)


def solution(mesh):
    split = Mesh(mesh.devices.reshape(SIZES), AXES)
    seq, head = ("ylo", "z"), ("x", "yhi", "core")
    return jax.shard_map(
        local,
        mesh=split,
        in_specs=(
            P(seq, head),
            P(seq, None),
            P(None, None, head),
            P(head, seq),
            P(),
            P(),
            P(),
            P(seq, None),
        ),
        out_specs=P(seq, head),
        check_vma=False,
    )
```

time: 437 us -> 172 us (0.39)
  waiting for transfers between devices: 391 us -> 38.2 us
  blocking collectives: 0 us -> 49.9 us
  starting transfers between devices: 3.91 us -> 31.9 us
  matrix products: 14.6 us -> 2.64 us
  Pallas kernels: 0 us -> 9.68 us
  local copies, waits for them, and re-layouts: 5.67 us -> 10.8 us
  other arithmetic: 8.11 us -> 12.7 us
    all_gather x2 -> x1, waiting for transfers between devices: 290 us -> 0.01 us  [local(): lax.all_gather(jnp.concatenate([upper, lower], axis=0), 'z', axis=0, tile...]
    reduce_scatter x1 -> x0, waiting for transfers between devices: 99.1 us -> none  [local(): lax.psum_scatter(partial_value, 'head', scatter_dimension=1, tiled=True)]
    all_gather x0 -> x1, blocking collectives: none -> 49.9 us  [local(): gathered = lax.all_gather(pair, 'z', axis=0, tiled=False)]
    ppermute x2 -> x10, waiting for transfers between devices: 0.92 us -> 23.8 us  [the longest x8 17.7 us: swapped(): return lax.ppermute(value, axis, [(0, 1), (1, 0)])]
    ppermute x2 -> x10, starting transfers between devices: 3.83 us -> 24.3 us  [the longest x8 19.2 us: swapped(): return lax.ppermute(value, axis, [(0, 1), (1, 0)])]
    all_to_all x0 -> x1, waiting for transfers between devices: none -> 14.3 us  [local(): parts = lax.all_to_all(partial, ('x', 'yhi'), 0, 0, tiled=True)]
    dot_general x10 -> x1, matrix products: 14.6 us -> 2.64 us  [local(): projected = jnp.dot(vision, both, preferred_element_type=F32)]
    pallas_call x0 -> x2, Pallas kernels: none -> 9.68 us  [the longest x1 7.11 us: attend(): pl.pallas_call(attend_kernel, grid_spec=pltpu.PrefetchScalarGridSpec(num_...]
  transfers between devices with their start and end apart: 5 -> 12, of which waited for: 4 -> 6; matrix products, arithmetic and copies ran while one was open for 4% -> 10% of each run, Pallas kernels for 0% -> 4%
where the time goes in v1:
time: 172 us; the launch traced here: 170 us
  blocking collectives  49.9 us (29%)
  waiting for transfers between devices  38.2 us (22%)
  starting transfers between devices  31.9 us (19%)
  between operations  13.8 us (8%)
  other arithmetic  12.7 us (7%)
  local copies, waits for them, and re-layouts  10.8 us (6%)
  Pallas kernels  9.68 us (6%)
  matrix products  2.64 us (2%)
    all_gather x1, blocking collectives, local(): gathered = lax.all_gather(pair, 'z', axis=0, tiled=False)  49.9 us
    ppermute x8, starting transfers between devices, swapped(): return lax.ppermute(value, axis, [(0, 1), (1, 0)])  19.2 us
    ppermute x8, waiting for transfers between devices, swapped(): return lax.ppermute(value, axis, [(0, 1), (1, 0)])  17.7 us
    all_to_all x1, waiting for transfers between devices, local(): parts = lax.all_to_all(partial, ('x', 'yhi'), 0, 0, tiled=True)  14.3 us
    all_to_all x1, starting transfers between devices, local(): parts = lax.all_to_all(partial, ('x', 'yhi'), 0, 0, tiled=True)  7.59 us
    pallas_call x1, Pallas kernels, attend(): pl.pallas_call(attend_kernel, grid_spec=pltpu.PrefetchScalarGridSpec(num_...  7.11 us
    ppermute x2, waiting for transfers between devices, moved(): return lax.ppermute(value, AXES, pairs)  6.16 us
    ppermute x2, starting transfers between devices, moved(): return lax.ppermute(value, AXES, pairs)  5.02 us
  transfers between devices with their start and end apart: 12, of which 6 were waited for; matrix products, arithmetic and copies ran while one was open for 10% of the time, Pallas kernels for 4%

profile of v1, /device:TPU:6, one launch (start us, length us, event | category | flops | bytes accessed | tf_op | source)
XLA Modules:
  0.0 169.5 jit_solution(2159243330643070554)
XLA Ops:
  6.5 1.1 constant_dynamic-slice_fusion
  7.6 1.9 %collective-permute-start.7 = (bf16[512,128]{1,0:T(8,128)(2,1)S(1)}, bf16[512,128]{1,0:T(8,128)(2,1)S(1)}, u32[]{:S(2)}, u32[]{:S(2)}) collective-permute-start(bf16[512,128]{1,0:T(8,128)(2,1)S(1)} %constant_dynamic-slice_fusion), channel_id=1, source_target_pairs={{0,1},{1,0},{2,3},{3,2},{4,5},{5,4},{6,7},{7,6},{8,9},{9,8},{10,11... | collective-permute-start | bytes 393224 | tf_op jit(solution)/shard_map/ppermute | solution.py:31
  9.5 1.3 collective-permute-done.7
  10.8 1.0 broadcast_select_fusion.1
  12.6 3.1 %slice_bitcast_fusion.1 = (bf16[8192,64]{0,1:T(8,128)(2,1)}, bf16[8192,64]{0,1:T(8,128)(2,1)}) fusion(bf16[2,8192,64]{1,2,0:T(8,128)(2,1)} %param.10), kind=kLoop, calls=%fused_computation.8 | loop fusion | bytes 4194304 | tf_op jit(solution)/shard_map/squeeze | solution.py:146
  15.6 2.6 %fusion = f32[128,200]{0,1:T(8,128)S(1)} fusion(bf16[200,8192]{1,0:T(8,128)(2,1)S(1)} %copy-done, bf16[8192,64]{0,1:T(8,128)(2,1)} %get-tuple-element.14, bf16[8192,64]{0,1:T(8,128)(2,1)} %get-tuple-element.13), kind=kOutput, calls=%fused_computation | convolution fusion | flops 423624704 | bytes 5476352 | tf_op jit(solution)/shard_map/dot_general | solution.py:147
  19.0 2.0 %collective-permute-start.3 = (f32[112,128]{1,0:T(8,128)}, f32[112,128]{1,0:T(8,128)}, u32[]{:S(2)}, u32[]{:S(2)}) collective-permute-start(f32[112,128]{1,0:T(8,128)} %dynamic-slice_bitcast_fusion.2), channel_id=1, source_target_pairs={{0,1},{1,0},{2,3},{3,2},{4,5},{5,4},{6,7},{7,6},{8,9},{9,8},{10,11... | collective-permute-start | bytes 172040 | tf_op jit(solution)/shard_map/ppermute | solution.py:31
  21.8 1.0 mul.61
  24.7 1.0 fusion.7
  25.7 2.3 %collective-permute-start = (bf16[128,512]{1,0:T(8,128)(2,1)S(1)}, bf16[128,512]{1,0:T(8,128)(2,1)S(1)}, u32[]{:S(2)}, u32[]{:S(2)}) collective-permute-start(bf16[128,512]{1,0:T(8,128)(2,1)S(1)} %fusion.7), channel_id=1, source_target_pairs={{0,1},{1,0},{2,3},{3,2},{4,5},{5,4},{6,7},{7,6},{8,9},{9,8},{10,11... | collective-permute-start | bytes 393224 | tf_op jit(solution)/shard_map/ppermute | solution.py:31
  28.0 3.5 %collective-permute-start.2 = (s32[128,2]{0,1:T(2,128)S(1)}, s32[128,2]{0,1:T(2,128)S(1)}, u32[]{:S(2)}, u32[]{:S(2)}) collective-permute-start(s32[128,2]{0,1:T(2,128)S(1)} %copy-done.7), channel_id=1, source_target_pairs={{0,256},{256,0},{1,257},{257,1},{2,258},{258,2},{3,259},{259,3},{4... | collective-permute-start | bytes 3080 | tf_op jit(solution)/shard_map/ppermute | solution.py:31
  31.6 2.2 %select_convert_fusion.kx_ref = bf16[1792,128]{1,0:T(8,128)(2,1)} fusion(s32[1792]{0:T(1024)S(1)} %fusion.19, pred[128]{0:T(512)(128)(4,1)S(1)} %iota_compare_fusion.4, pred[1792]{0:T(1024)(128)(4,1)S(1)} %fusion.28), kind=kLoop, calls=%fused_computation.9 | loop fusion | flops 1146880 | bytes 467840 | tf_op jit(solution)/shard_map/convert_element_type | solution.py:182
  35.5 3.1 %collective-permute-start.1 = (bf16[128,1024]{1,0:T(8,128)(2,1)S(1)}, bf16[128,1024]{1,0:T(8,128)(2,1)S(1)}, u32[]{:S(2)}, u32[]{:S(2)}) collective-permute-start(bf16[128,1024]{1,0:T(8,128)(2,1)S(1)} %pad_maximum_fusion.1), channel_id=1, source_target_pairs={{0,256},{256,0},{1,257},{257,1},{2,258},{258,2},{3,259},{259,3},{4... | collective-permute-start | bytes 786440 | tf_op jit(solution)/shard_map/ppermute | solution.py:31
  38.6 49.9 %all_gather.10.kv_ref = bf16[16,224,128]{2,1,0:T(8,128)(2,1)S(1)} all-gather(bf16[1,224,128]{2,1,0:T(8,128)(2,1)S(1)} %pad_maximum_fusion.5), channel_id=1, replica_groups=mesh['ylo'=2,'z'=16,'x'=4,'yhi'=2,'core'=2] {'z'}, dimensions={0}, use_global_device_ids=true | all-gather | bytes 974848 | tf_op jit(solution)/shard_map/all_gather | solution.py:156
  88.6 7.1 %attend.1 = (f32[256,1024]{1,0:T(8,128)S(1)}, f32[256,128]{1,0:T(8,128)S(1)}) custom-call(s32[1]{0:T(128)} %bitcast.core_ref, bf16[256,1024]{1,0:T(8,128)(2,1)S(1)} %maximum_select_fusion.q_ref, bf16[256,128]{1,0:T(8,128)(2,1)S(1)} %select_convert_fusion.1.qx_ref, bf16[16,224,128]{2,1,0:T(8,128)(2,1)S(1)} %all_gather.10.kv_ref, bf16[1792,128]{1,0:T(8,128)(2,1)S(1)} %copy-done.4), custom_call_target="tpu_custom_call" | custom-call | tf_op jit(solution)/shard_map/attend/pallas_call | solution.py:78
  95.7 1.9 %collective-permute-start.4 = (f32[256,1024]{1,0:T(8,128)S(1)}, f32[256,1024]{1,0:T(8,128)S(1)}, u32[]{:S(2)}, u32[]{:S(2)}) collective-permute-start(f32[256,1024]{1,0:T(8,128)S(1)} %get-tuple-element.7), channel_id=1, source_target_pairs={{0,1},{1,0},{2,3},{3,2},{4,5},{5,4},{6,7},{7,6},{8,9},{9,8},{10,11... | collective-permute-start | bytes 3145736 | tf_op jit(solution)/shard_map/ppermute | solution.py:31
  97.6 2.4 %collective-permute-start.5 = (f32[256,128]{1,0:T(8,128)S(1)}, f32[256,128]{1,0:T(8,128)S(1)}, u32[]{:S(2)}, u32[]{:S(2)}) collective-permute-start(f32[256,128]{1,0:T(8,128)S(1)} %get-tuple-element.8), channel_id=1, source_target_pairs={{0,1},{1,0},{2,3},{3,2},{4,5},{5,4},{6,7},{7,6},{8,9},{9,8},{10,11... | collective-permute-start | bytes 393224 | tf_op jit(solution)/shard_map/ppermute | solution.py:31
  100.0 1.0 collective-permute-done.5
  101.4 2.1 %collective-permute-start.6 = (bf16[256,1152]{1,0:T(8,128)(2,1)S(1)}, bf16[256,1152]{1,0:T(8,128)(2,1)S(1)}, u32[]{:S(2)}, u32[]{:S(2)}) collective-permute-start(bf16[256,1152]{1,0:T(8,128)(2,1)S(1)} %pad_maximum_fusion), channel_id=1, source_target_pairs={{0,256},{256,0},{1,257},{257,1},{2,258},{258,2},{3,259},{259,3},{4... | collective-permute-start | bytes 1769480 | tf_op jit(solution)/shard_map/ppermute | solution.py:31
  103.6 15.4 %collective-permute-done.6 = bf16[256,1152]{1,0:T(8,128)(2,1)S(1)} collective-permute-done((bf16[256,1152]{1,0:T(8,128)(2,1)S(1)}, bf16[256,1152]{1,0:T(8,128)(2,1)S(1)}, u32[]{:S(2)}, u32[]{:S(2)}) %collective-permute-start.6) | collective-permute-done | bytes 589856 | tf_op jit(solution)/shard_map/ppermute | solution.py:31
  119.5 1.2 fusion.4.a_ref
  120.6 2.2 %copy-done.1 = bf16[16384,128]{1,0:T(8,128)(2,1)S(1)} copy-done((bf16[16384,128]{1,0:T(8,128)(2,1)S(1)}, bf16[16384,128]{1,0:T(8,128)(2,1)}, u32[]{:S(2)}) %copy-start.1) | copy-done | bytes 4194328
  122.8 1.0 copy-done.3
  123.9 2.6 %project.1 = bf16[2,8,128,256]{3,2,1,0:T(8,128)(2,1)S(1)} custom-call(bf16[256,1024]{1,0:T(8,128)(2,1)S(1)} %copy-done.3, bf16[16,1024,128]{2,1,0:T(8,128)(2,1)S(1)} %bitcast.35), custom_call_target="tpu_custom_call" | custom-call | tf_op jit(solution)/shard_map/project/pallas_call | solution.py:118
  126.4 1.0 copy-done.2
  127.4 7.6 %all-to-all-start = ((bf16[8,2,128,256]{3,2,1,0:T(8,128)(2,1)}), bf16[8,2,128,256]{3,2,1,0:T(8,128)(2,1)}, u32[]{:S(2)}, u32[]{:S(2)}) async-start(bf16[8,2,128,256]{3,2,1,0:T(8,128)(2,1)} %bitcast.36), calls=%async_computation | async-start | bytes 2097152 | tf_op jit(solution)/shard_map/all_to_all | solution.py:203
  135.0 14.3 %all-to-all-done = bf16[8,2,128,256]{3,2,1,0:T(8,128)(2,1)} async-done(((bf16[8,2,128,256]{3,2,1,0:T(8,128)(2,1)}), bf16[8,2,128,256]{3,2,1,0:T(8,128)(2,1)}, u32[]{:S(2)}, u32[]{:S(2)}) %all-to-all-start) | async-done | bytes 1048608 | tf_op jit(solution)/shard_map/all_to_all | solution.py:203
  149.3 1.4 reduce_sum.42
  150.7 3.1 %collective-permute-start.8 = (bf16[128,256]{1,0:T(8,128)(2,1)S(1)}, bf16[128,256]{1,0:T(8,128)(2,1)S(1)}, u32[]{:S(2)}, u32[]{:S(2)}) collective-permute-start(bf16[128,256]{1,0:T(8,128)(2,1)S(1)} %get-tuple-element.21), channel_id=1, source_target_pairs={{0,0},{1,1},{2,2},{3,3},{4,4},{5,5},{6,6},{7,7},{8,256},{9,257},{1... | collective-permute-start | bytes 196616 | tf_op jit(solution)/shard_map/ppermute | solution.py:43
  153.9 1.9 %collective-permute-start.9 = (bf16[128,256]{1,0:T(8,128)(2,1)S(1)}, bf16[128,256]{1,0:T(8,128)(2,1)S(1)}, u32[]{:S(2)}, u32[]{:S(2)}) collective-permute-start(bf16[128,256]{1,0:T(8,128)(2,1)S(1)} %get-tuple-element.22), channel_id=1, source_target_pairs={{0,1},{1,0},{2,3},{3,2},{4,5},{5,4},{6,7},{7,6},{8,257},{9,256},{1... | collective-permute-start | bytes 196616 | tf_op jit(solution)/shard_map/ppermute | solution.py:43
  155.8 3.5 %collective-permute-done.8 = bf16[128,256]{1,0:T(8,128)(2,1)S(1)} collective-permute-done((bf16[128,256]{1,0:T(8,128)(2,1)S(1)}, bf16[128,256]{1,0:T(8,128)(2,1)S(1)}, u32[]{:S(2)}, u32[]{:S(2)}) %collective-permute-start.8) | collective-permute-done | bytes 65568 | tf_op jit(solution)/shard_map/ppermute | solution.py:43
  159.3 2.6 %collective-permute-done.9 = bf16[128,256]{1,0:T(8,128)(2,1)S(1)} collective-permute-done((bf16[128,256]{1,0:T(8,128)(2,1)S(1)}, bf16[128,256]{1,0:T(8,128)(2,1)S(1)}, u32[]{:S(2)}, u32[]{:S(2)}) %collective-permute-start.9) | collective-permute-done | bytes 65568 | tf_op jit(solution)/shard_map/ppermute | solution.py:43
  (64 shorter events, 7.6 us)
Async XLA Ops:
  6.5 9.1 %copy-start = (bf16[200,8192]{1,0:T(8,128)(2,1)S(1)}, bf16[200,8192]{1,0:T(8,128)(2,1)}, u32[]{:S(2)}) copy-start(bf16[200,8192]{1,0:T(8,128)(2,1)} %param.9) | copy-start | bytes 9830404
  6.5 114.1 %all-gather.3.cloned.1.call-start = ((), (), s32[]{:S(2)}) async-start(), calls=%async_computation.1 | async-start | bytes 4456448 | tf_op jit(solution)/shard_map/all_gather | solution.py:144
  7.6 3.2 %collective-permute-start.7 = (bf16[512,128]{1,0:T(8,128)(2,1)S(1)}, bf16[512,128]{1,0:T(8,128)(2,1)S(1)}, u32[]{:S(2)}, u32[]{:S(2)}) collective-permute-start(bf16[512,128]{1,0:T(8,128)(2,1)S(1)} %constant_dynamic-slice_fusion), channel_id=1, source_target_pairs={{0,1},{1,0},{2,3},{3,2},{4,5},{5,4},{6,7},{7,6},{8,9},{9,8},{10,11... | collective-permute-start | bytes 393224 | tf_op jit(solution)/shard_map/ppermute | solution.py:31
  15.6 5.4 %copy-start.5 = (bf16[128,512]{1,0:T(8,128)(2,1)S(1)}, bf16[128,512]{1,0:T(8,128)(2,1)}, u32[]{:S(2)}) copy-start(bf16[128,512]{1,0:T(8,128)(2,1)} %param.8) | copy-start | bytes 393220
  15.6 8.0 %copy-start.9 = (f32[128]{0:T(128)S(1)}, f32[128]{0:T(128)}, u32[]{:S(2)}) copy-start(f32[128]{0:T(128)} %param.12) | copy-start | bytes 1540
  18.3 2.7 %copy-start.6 = (f32[128,200]{0,1:T(8,128)}, f32[128,200]{0,1:T(8,128)S(1)}, u32[]{:S(2)}) copy-start(f32[128,200]{0,1:T(8,128)S(1)} %fusion) | copy-start | bytes 307204
  18.3 9.7 %copy-start.7 = (s32[128,2]{0,1:T(2,128)S(1)}, s32[128,2]{0,1:T(2,128)}, u32[]{:S(2)}) copy-start(s32[128,2]{0,1:T(2,128)} %param.15) | copy-start | bytes 3076
  18.3 13.2 %copy-start.10 = (s32[4]{0:T(128)S(1)}, s32[4]{0:T(128)}, u32[]{:S(2)}) copy-start(s32[4]{0:T(128)} %param.14) | copy-start | bytes 52
  18.3 16.9 %copy-start.8 = (f32[128]{0:T(128)S(1)}, f32[128]{0:T(128)}, u32[]{:S(2)}) copy-start(f32[128]{0:T(128)} %param.13) | copy-start | bytes 1540
  19.0 15.0 %collective-permute-start.3 = (f32[112,128]{1,0:T(8,128)}, f32[112,128]{1,0:T(8,128)}, u32[]{:S(2)}, u32[]{:S(2)}) collective-permute-start(f32[112,128]{1,0:T(8,128)} %dynamic-slice_bitcast_fusion.2), channel_id=1, source_target_pairs={{0,1},{1,0},{2,3},{3,2},{4,5},{5,4},{6,7},{7,6},{8,9},{9,8},{10,11... | collective-permute-start | bytes 172040 | tf_op jit(solution)/shard_map/ppermute | solution.py:31
  25.7 9.8 %collective-permute-start = (bf16[128,512]{1,0:T(8,128)(2,1)S(1)}, bf16[128,512]{1,0:T(8,128)(2,1)S(1)}, u32[]{:S(2)}, u32[]{:S(2)}) collective-permute-start(bf16[128,512]{1,0:T(8,128)(2,1)S(1)} %fusion.7), channel_id=1, source_target_pairs={{0,1},{1,0},{2,3},{3,2},{4,5},{5,4},{6,7},{7,6},{8,9},{9,8},{10,11... | collective-permute-start | bytes 393224 | tf_op jit(solution)/shard_map/ppermute | solution.py:31
  28.0 5.9 %collective-permute-start.2 = (s32[128,2]{0,1:T(2,128)S(1)}, s32[128,2]{0,1:T(2,128)S(1)}, u32[]{:S(2)}, u32[]{:S(2)}) collective-permute-start(s32[128,2]{0,1:T(2,128)S(1)} %copy-done.7), channel_id=1, source_target_pairs={{0,256},{256,0},{1,257},{257,1},{2,258},{258,2},{3,259},{259,3},{4... | collective-permute-start | bytes 3080 | tf_op jit(solution)/shard_map/ppermute | solution.py:31
  33.8 54.8 %copy-start.4 = (bf16[1792,128]{1,0:T(8,128)(2,1)S(1)}, bf16[1792,128]{1,0:T(8,128)(2,1)}, u32[]{:S(2)}) copy-start(bf16[1792,128]{1,0:T(8,128)(2,1)} %select_convert_fusion.kx_ref) | copy-start | bytes 1376260
  35.5 52.9 %collective-permute-start.1 = (bf16[128,1024]{1,0:T(8,128)(2,1)S(1)}, bf16[128,1024]{1,0:T(8,128)(2,1)S(1)}, u32[]{:S(2)}, u32[]{:S(2)}) collective-permute-start(bf16[128,1024]{1,0:T(8,128)(2,1)S(1)} %pad_maximum_fusion.1), channel_id=1, source_target_pairs={{0,256},{256,0},{1,257},{257,1},{2,258},{258,2},{3,259},{259,3},{4... | collective-permute-start | bytes 786440 | tf_op jit(solution)/shard_map/ppermute | solution.py:31
  95.7 5.5 %collective-permute-start.4 = (f32[256,1024]{1,0:T(8,128)S(1)}, f32[256,1024]{1,0:T(8,128)S(1)}, u32[]{:S(2)}, u32[]{:S(2)}) collective-permute-start(f32[256,1024]{1,0:T(8,128)S(1)} %get-tuple-element.7), channel_id=1, source_target_pairs={{0,1},{1,0},{2,3},{3,2},{4,5},{5,4},{6,7},{7,6},{8,9},{9,8},{10,11... | collective-permute-start | bytes 3145736 | tf_op jit(solution)/shard_map/ppermute | solution.py:31
  97.6 3.4 %collective-permute-start.5 = (f32[256,128]{1,0:T(8,128)S(1)}, f32[256,128]{1,0:T(8,128)S(1)}, u32[]{:S(2)}, u32[]{:S(2)}) collective-permute-start(f32[256,128]{1,0:T(8,128)S(1)} %get-tuple-element.8), channel_id=1, source_target_pairs={{0,1},{1,0},{2,3},{3,2},{4,5},{5,4},{6,7},{7,6},{8,9},{9,8},{10,11... | collective-permute-start | bytes 393224 | tf_op jit(solution)/shard_map/ppermute | solution.py:31
  101.4 17.5 %collective-permute-start.6 = (bf16[256,1152]{1,0:T(8,128)(2,1)S(1)}, bf16[256,1152]{1,0:T(8,128)(2,1)S(1)}, u32[]{:S(2)}, u32[]{:S(2)}) collective-permute-start(bf16[256,1152]{1,0:T(8,128)(2,1)S(1)} %pad_maximum_fusion), channel_id=1, source_target_pairs={{0,256},{256,0},{1,257},{257,1},{2,258},{258,2},{3,259},{259,3},{4... | collective-permute-start | bytes 1769480 | tf_op jit(solution)/shard_map/ppermute | solution.py:31
  120.6 2.2 %copy-start.1 = (bf16[16384,128]{1,0:T(8,128)(2,1)S(1)}, bf16[16384,128]{1,0:T(8,128)(2,1)}, u32[]{:S(2)}) copy-start(bf16[16384,128]{1,0:T(8,128)(2,1)} %all-gather.3.cloned.1.call-done) | copy-start | bytes 12582916
  122.8 1.0 copy-start.3
  126.4 1.0 copy-start.2
  127.4 21.9 %all-to-all-start = ((bf16[8,2,128,256]{3,2,1,0:T(8,128)(2,1)}), bf16[8,2,128,256]{3,2,1,0:T(8,128)(2,1)}, u32[]{:S(2)}, u32[]{:S(2)}) async-start(bf16[8,2,128,256]{3,2,1,0:T(8,128)(2,1)} %bitcast.36), calls=%async_computation | async-start | bytes 2097152 | tf_op jit(solution)/shard_map/all_to_all | solution.py:203
  150.7 8.6 %collective-permute-start.8 = (bf16[128,256]{1,0:T(8,128)(2,1)S(1)}, bf16[128,256]{1,0:T(8,128)(2,1)S(1)}, u32[]{:S(2)}, u32[]{:S(2)}) collective-permute-start(bf16[128,256]{1,0:T(8,128)(2,1)S(1)} %get-tuple-element.21), channel_id=1, source_target_pairs={{0,0},{1,1},{2,2},{3,3},{4,4},{5,5},{6,6},{7,7},{8,256},{9,257},{1... | collective-permute-start | bytes 196616 | tf_op jit(solution)/shard_map/ppermute | solution.py:43
  153.9 8.1 %collective-permute-start.9 = (bf16[128,256]{1,0:T(8,128)(2,1)S(1)}, bf16[128,256]{1,0:T(8,128)(2,1)S(1)}, u32[]{:S(2)}, u32[]{:S(2)}) collective-permute-start(bf16[128,256]{1,0:T(8,128)(2,1)S(1)} %get-tuple-element.22), channel_id=1, source_target_pairs={{0,1},{1,0},{2,3},{3,2},{4,5},{5,4},{6,7},{7,6},{8,257},{9,256},{1... | collective-permute-start | bytes 196616 | tf_op jit(solution)/shard_map/ppermute | solution.py:43
Sparse Core Ops, SparseCore 0:
  12.7 87.7 all-gather.2

commit v2 on v0

v2 whole, which is shorter than its diff:
```python
import math

import jax
import jax.numpy as jnp
from jax import lax
from jax.experimental import pallas as pl
from jax.experimental.pallas import tpu as pltpu
from jax.sharding import Mesh, PartitionSpec as P

HD = 128
TILES = 4
EPSILON = 1e-05
NEG = -1e30
AXES = ("ylo", "zh", "zl", "x", "yhi", "core")
SIZES = (2, 8, 2, 4, 2, 2)
QUAD = ("ylo", "zl")
ROWS = 128
HEADS = 4
WIDTH = HEADS * HD
LOCAL = 200
BLOCKS = 8
SLOTS = BLOCKS * LOCAL
BF = jnp.bfloat16
F32 = jnp.float32
VMEM_LIMIT = 48 << 20


def flat(ylo, zh, zl, x, yhi, core):
    return ((((ylo * 8 + zh) * 2 + zl) * 4 + x) * 2 + yhi) * 2 + core


def everywhere(target):
    pairs = []
    for source in range(512):
        core, yhi, x = source % 2, source // 2 % 2, source // 4 % 4
        zl, zh, ylo = source // 16 % 2, source // 32 % 8, source // 256
        pairs.append((source, flat(*target(ylo, zh, zl, x, yhi, core))))
    return pairs


def swapped(value, axis):
    return lax.ppermute(value, axis, [(0, 1), (1, 0)])


def crossed(value, flip_y, flip_z):
    pairs = everywhere(
        lambda ylo, zh, zl, x, yhi, core: (ylo ^ flip_y, zh, zl ^ flip_z, x, yhi, core)
    )
    return lax.ppermute(value, AXES, pairs)


def placed(value, flip_z, flip_core):
    pairs = everywhere(
        lambda ylo, zh, zl, x, yhi, core: (
            x // 2,
            zh,
            zl ^ flip_z,
            2 * ylo + x % 2,
            yhi,
            core ^ flip_core,
        )
    )
    return lax.ppermute(value, AXES, pairs)


def vmem():
    return pl.BlockSpec(memory_space=pltpu.VMEM)


def smem():
    return pl.BlockSpec(memory_space=pltpu.SMEM)


def params():
    return pltpu.CompilerParams(vmem_limit_bytes=VMEM_LIMIT)


def prepare_kernel(q_ref, gain_ref, span_ref, o_ref):
    gain = gain_ref[...]
    for head in range(HEADS):
        columns = slice(head * HD, (head + 1) * HD)
        field = q_ref[:, columns].astype(F32)
        mean_sq = jnp.mean(field * field, axis=1, keepdims=True)
        o_ref[:, columns] = (field / jnp.sqrt(mean_sq + EPSILON) * gain).astype(BF)
    row = lax.broadcasted_iota(jnp.int32, (ROWS, HD), 0)
    lane = lax.broadcasted_iota(jnp.int32, (ROWS, HD), 1)
    begin = jnp.sum(jnp.where(row == lane, span_ref[0:1, :], 0), axis=1, keepdims=True)
    end = jnp.sum(jnp.where(row == lane, span_ref[1:2, :], 0), axis=1, keepdims=True)
    inside = (begin <= lane) & (lane < end)
    o_ref[:, WIDTH:] = jnp.where((lane <= TILES) & ~inside, NEG, 0.0).astype(BF)


def prepare(queries, q_gain, spans):
    return pl.pallas_call(
        prepare_kernel,
        in_specs=[vmem(), vmem(), vmem()],
        out_specs=vmem(),
        out_shape=jax.ShapeDtypeStruct((ROWS, WIDTH + HD), BF),
        compiler_params=params(),
        name="prepare",
    )(queries, q_gain.reshape(1, HD), spans.T)


def attend_kernel(place_ref, count_ref, q_ref, mine_ref, theirs_ref, o_ref, key_s, value_s):
    core, ylo, zl = place_ref[0], place_ref[1], place_ref[2]
    half = HD // 2
    lane = lax.broadcasted_iota(jnp.int32, (LOCAL, HD), 1)
    item = lax.broadcasted_iota(jnp.int32, (LOCAL, HD), 0)
    for block in range(BLOCKS):
        rows = slice(block * LOCAL, (block + 1) * LOCAL)
        mine, theirs = mine_ref[block], theirs_ref[block]
        left = jnp.where(core == 0, mine, theirs)
        right = jnp.where(core == 0, theirs, mine)
        key_s[rows, :HD] = jnp.concatenate([left[:, :half], right[:, :half]], axis=1)
        value_s[rows, :HD] = jnp.concatenate([left[:, half:], right[:, half:]], axis=1)
        tile = 2 * ylo + block // 4
        absent = item + ((block % 4) * 2 + zl) * LOCAL >= count_ref[tile]
        key_s[rows, HD:] = jnp.where(
            (lane == tile) | ((lane == TILES) & absent), 1.0, 0.0
        ).astype(BF)
    value_s[:, HD:] = jnp.ones((SLOTS, HD), BF)
    query_ext = q_ref[:, :, WIDTH:].reshape(4 * ROWS, HD)
    wide = lax.broadcasted_iota(jnp.int32, (4 * ROWS, HD), 1)
    totals = jnp.zeros((4 * ROWS, HD), F32)
    for head in range(HEADS):
        columns = slice(head * HD, (head + 1) * HD)
        query = q_ref[:, :, columns].reshape(4 * ROWS, HD)
        scores = lax.dot_general(
            jnp.concatenate([query, query_ext], axis=1),
            key_s[...],
            (((1,), (1,)), ((), ())),
            preferred_element_type=F32,
        )
        weights = jnp.exp2(scores * (math.log2(math.e) / math.sqrt(HD))).astype(BF)
        result = jnp.dot(weights, value_s[...], preferred_element_type=F32)
        numer = result[:, :HD].astype(BF)
        for part in range(4):
            o_ref[part ^ (2 * ylo + zl), :, columns] = numer[part * ROWS : (part + 1) * ROWS]
        totals = jnp.where(wide % HEADS == head, result[:, HD:], totals)
    high = totals.astype(BF)
    low = (totals - high.astype(F32)).astype(BF)
    packed = jnp.where(wide < HEADS, high.astype(F32), low.astype(F32)).astype(BF)
    for part in range(4):
        o_ref[part ^ (2 * ylo + zl), :, WIDTH:] = packed[part * ROWS : (part + 1) * ROWS]


def attend(place, counts, query, mine, theirs):
    return pl.pallas_call(
        attend_kernel,
        in_specs=[smem(), smem(), vmem(), vmem(), vmem()],
        out_specs=vmem(),
        out_shape=jax.ShapeDtypeStruct((4, ROWS, WIDTH + HD), BF),
        scratch_shapes=[pltpu.VMEM((SLOTS, 2 * HD), BF), pltpu.VMEM((SLOTS, 2 * HD), BF)],
        compiler_params=params(),
        name="attend",
    )(place, counts, query, mine, theirs)


def combine_kernel(x_ref, o_ref):
    summed = x_ref[0].astype(F32)
    for source in range(1, 4):
        summed = summed + x_ref[source].astype(F32)
    for head in range(HEADS):
        columns = slice(head * HD, (head + 1) * HD)
        high = summed[:, WIDTH + head : WIDTH + head + 1]
        low = summed[:, WIDTH + HEADS + head : WIDTH + HEADS + head + 1]
        o_ref[:, columns] = (summed[:, columns] / (high + low)).astype(BF)


def combine(parts):
    return pl.pallas_call(
        combine_kernel,
        in_specs=[vmem()],
        out_specs=vmem(),
        out_shape=jax.ShapeDtypeStruct((ROWS, WIDTH), BF),
        compiler_params=params(),
        name="combine",
    )(parts)


def project_kernel(own_ref, other_ref, w_hbm, o_hbm, w_s, o_s, in_sem, out_sem):
    fetch = [
        pltpu.make_async_copy(
            w_hbm.at[pl.ds(2 * step, 2)], w_s.at[pl.ds(2 * step, 2)], in_sem.at[step]
        )
        for step in range(4)
    ]
    for copy in fetch:
        copy.start()
    own = own_ref[...].reshape(4 * ROWS, WIDTH)
    other = other_ref[...].reshape(4 * ROWS, WIDTH)
    drain = []
    for step in range(4):
        fetch[step].wait()
        weight = jnp.concatenate([w_s[2 * step], w_s[2 * step + 1]], axis=1)
        result = jnp.dot(own, weight[:WIDTH], preferred_element_type=F32)
        result = result + jnp.dot(other, weight[WIDTH:], preferred_element_type=F32)
        result = result.astype(BF)
        for upper in range(2):
            for lower in range(2):
                begin = (2 * upper + lower) * ROWS
                rows = slice(begin, begin + ROWS)
                o_s[step, upper, lower, 0] = result[rows, :HD]
                o_s[step, upper, lower, 1] = result[rows, HD:]
        copy = pltpu.make_async_copy(o_s.at[step], o_hbm.at[:, step], out_sem.at[step])
        copy.start()
        drain.append(copy)
    for copy in drain:
        copy.wait()


def project(own, other, weight):
    hbm = pl.BlockSpec(memory_space=pltpu.HBM)
    return pl.pallas_call(
        project_kernel,
        in_specs=[vmem(), vmem(), hbm],
        out_specs=hbm,
        out_shape=jax.ShapeDtypeStruct((2, 4, 2, 2, ROWS, HD), BF),
        scratch_shapes=[
            pltpu.VMEM((BLOCKS, 2 * WIDTH, HD), BF),
            pltpu.VMEM((4, 2, 2, 2, ROWS, HD), BF),
            pltpu.SemaphoreType.DMA((4,)),
            pltpu.SemaphoreType.DMA((4,)),
        ],
        compiler_params=params(),
        name="project",
    )(own, other, weight)


def local(queries, vision, kv_weight, out_weight, q_gain, k_gain, tile_counts, spans):
    core = lax.axis_index("core")
    ylo = lax.axis_index("ylo")
    zl = lax.axis_index("zl")
    half = HD // 2

    kept = lax.dynamic_slice_in_dim(out_weight, core * HD, HD, axis=1)
    sent = lax.dynamic_slice_in_dim(out_weight, (1 - core) * HD, HD, axis=1)
    pair = jnp.concatenate([kept, swapped(sent, "core")], axis=0)
    weight = lax.all_gather(pair, "zh", axis=0, tiled=False)

    both = jnp.transpose(kv_weight, (0, 2, 1)).reshape(HD, vision.shape[1])
    projected = lax.dot_general(
        vision, both, (((1,), (1,)), ((), ())), preferred_element_type=F32
    )
    key_raw = projected[:, :half]
    own_squares = jnp.sum(key_raw * key_raw, axis=1)
    inverse = 1.0 / jnp.sqrt((own_squares + swapped(own_squares, "core")) / HD + EPSILON)
    gain_half = lax.dynamic_slice_in_dim(k_gain, core * half, half)
    key_half = key_raw * inverse[:, None] * gain_half[None, :]
    local_pair = jnp.concatenate([key_half, projected[:, half:]], axis=1).astype(BF)
    mine = lax.all_gather(local_pair, "zh", axis=0, tiled=False)
    theirs = swapped(mine, "core")

    query = prepare(queries, q_gain, spans)
    shared = jnp.stack(
        [query, crossed(query, 0, 1), crossed(query, 1, 0), crossed(query, 1, 1)], axis=0
    )

    place = jnp.stack([core, ylo, zl]).astype(jnp.int32)
    partial = attend(place, tile_counts, shared, mine, theirs)
    attended = combine(lax.all_to_all(partial, QUAD, 0, 0, tiled=True))
    own = lax.all_gather(attended, QUAD, axis=0, tiled=False)
    other = swapped(own, "core")

    product = project(own, other, weight).reshape(8, 2, 2, ROWS, HD)
    parts = lax.all_to_all(product, ("x", "yhi"), 0, 0, tiled=True)
    summed = jnp.sum(parts.astype(F32), axis=0).astype(BF)
    pieces = {}
    for flip_z in range(2):
        row = lax.dynamic_index_in_dim(summed, zl ^ flip_z, 0, keepdims=False)
        for flip_core in range(2):
            piece = lax.dynamic_index_in_dim(row, core ^ flip_core, 0, keepdims=False)
            pieces[flip_z, flip_core] = placed(piece, flip_z, flip_core)
    columns = []
    for side in range(2):
        for lane in range(2):
            near = jnp.where(core == lane, pieces[0, 0], pieces[0, 1])
            far = jnp.where(core == lane, pieces[1, 0], pieces[1, 1])
            columns.append(jnp.where(zl == side, near, far))
    return jnp.concatenate(columns, axis=1)


def solution(mesh):
    split = Mesh(mesh.devices.reshape(SIZES), AXES)
    seq, head = ("ylo", "zh", "zl"), ("x", "yhi", "core")
    return jax.shard_map(
        local,
        mesh=split,
        in_specs=(
            P(seq, head),
            P(seq, None),
            P(None, None, head),
            P(head, seq),
            P(),
            P(),
            P(),
            P(seq, None),
        ),
        out_specs=P(seq, head),
        check_vma=False,
    )
```

time: 437 us -> 196 us (0.45)
  waiting for transfers between devices: 391 us -> 36.2 us
  blocking collectives: 0 us -> 71.6 us
  starting transfers between devices: 3.91 us -> 42.4 us
  matrix products: 14.6 us -> 2.66 us
  Pallas kernels: 0 us -> 9.04 us
  local copies, waits for them, and re-layouts: 5.67 us -> 11.5 us
    all_gather x2 -> x1, waiting for transfers between devices: 290 us -> 0.01 us  [local(): weight = lax.all_gather(pair, 'zh', axis=0, tiled=False)]
    reduce_scatter x1 -> x0, waiting for transfers between devices: 99.1 us -> none  [local(): lax.psum_scatter(partial_value, 'head', scatter_dimension=1, tiled=True)]
    all_gather x0 -> x2, blocking collectives: none -> 56.4 us  [the longest x1 42.3 us: local(): mine = lax.all_gather(local_pair, 'zh', axis=0, tiled=False)]
    ppermute x2 -> x11, starting transfers between devices: 3.83 us -> 34.7 us  [the longest x4 16.8 us: placed(): return lax.ppermute(value, AXES, pairs)]
    ppermute x2 -> x11, waiting for transfers between devices: 0.92 us -> 21.2 us  [the longest x3 16.1 us: crossed(): return lax.ppermute(value, AXES, pairs)]
    all_to_all x0 -> x1, blocking collectives: none -> 15.2 us  [local(): attended = combine(lax.all_to_all(partial, QUAD, 0, 0, tiled=True))]
    all_to_all x0 -> x1, waiting for transfers between devices: none -> 14.9 us  [local(): parts = lax.all_to_all(product, ('x', 'yhi'), 0, 0, tiled=True)]
    dot_general x10 -> x1, matrix products: 14.6 us -> 2.66 us  [local(): lax.dot_general(vision, both, (((1,), (1,)), ((), ())), preferred_element...]
  transfers between devices with their start and end apart: 5 -> 13, of which waited for: 4 -> 6; matrix products, arithmetic and copies ran while one was open for 4% -> 3% of each run, Pallas kernels for 0% -> 3%
where the time goes in v2:
time: 196 us; the launch traced here: 193 us
  blocking collectives  71.6 us (37%)
  starting transfers between devices  42.4 us (22%)
  waiting for transfers between devices  36.2 us (18%)
  between operations  13.7 us (7%)
  local copies, waits for them, and re-layouts  11.5 us (6%)
  Pallas kernels  9.04 us (5%)
  other arithmetic  6.04 us (3%)
  matrix products  2.66 us (1%)
    all_gather x1, blocking collectives, local(): mine = lax.all_gather(local_pair, 'zh', axis=0, tiled=False)  42.3 us
    ppermute x4, starting transfers between devices, placed(): return lax.ppermute(value, AXES, pairs)  16.8 us
    ppermute x3, waiting for transfers between devices, crossed(): return lax.ppermute(value, AXES, pairs)  16.1 us
    all_to_all x1, blocking collectives, local(): attended = combine(lax.all_to_all(partial, QUAD, 0, 0, tiled=True))  15.2 us
    all_to_all x1, waiting for transfers between devices, local(): parts = lax.all_to_all(product, ('x', 'yhi'), 0, 0, tiled=True)  14.9 us
    all_gather x1, blocking collectives, local(): own = lax.all_gather(attended, QUAD, axis=0, tiled=False)  14.1 us
    ppermute x3, starting transfers between devices, crossed(): return lax.ppermute(value, AXES, pairs)  9.72 us
    unnamed x24, local copies, waits for them, and re-layouts  9.08 us
  transfers between devices with their start and end apart: 13, of which 6 were waited for; matrix products, arithmetic and copies ran while one was open for 3% of the time, Pallas kernels for 3%

profile of v2, /device:TPU:6, one launch (start us, length us, event | category | flops | bytes accessed | tf_op | source)
XLA Modules:
  0.0 193.2 jit_solution(14816758501971215179)
XLA Ops:
  6.5 1.9 copy-done
  8.5 2.7 %fusion.2 = f32[200,128]{1,0:T(8,128)S(1)} fusion(bf16[200,8192]{1,0:T(8,128)(2,1)S(1)} %copy-done, bf16[128,8192]{1,0:T(8,128)(2,1)} %bitcast.36), kind=kOutput, calls=%fused_computation.25 | convolution fusion | flops 419430400 | bytes 5476352 | tf_op jit(solution)/shard_map/dot_general | solution.py:242
  11.3 1.9 collective-permute-start.3
  13.2 1.6 constant_dynamic-slice_fusion.1
  14.9 2.4 %collective-permute-start.6 = (bf16[512,128]{1,0:T(8,128)(2,1)}, bf16[512,128]{1,0:T(8,128)(2,1)}, u32[]{:S(2)}, u32[]{:S(2)}) collective-permute-start(bf16[512,128]{1,0:T(8,128)(2,1)} %get-tuple-element.6), channel_id=1, source_target_pairs={{0,1},{1,0},{2,3},{3,2},{4,5},{5,4},{6,7},{7,6},{8,9},{9,8},{10,11... | collective-permute-start | bytes 393224 | tf_op jit(solution)/shard_map/ppermute | solution.py:42
  18.6 1.6 pad_maximum_fusion.1
  21.2 42.3 %all_gather.16.mine_ref = bf16[8,200,128]{2,1,0:T(8,128)(2,1)} all-gather(bf16[1,200,128]{2,1,0:T(8,128)(2,1)S(1)} %pad_maximum_fusion.3), channel_id=1, replica_groups=mesh['ylo'=2,'zh'=8,'zl'=2,'x'=4,'yhi'=2,'core'=2] {'zh'}, dimensions={0}, use_global_device_ids=true | all-gather | bytes 460800 | tf_op jit(solution)/shard_map/all_gather | solution.py:251
  63.6 1.9 collective-permute-start.4
  66.7 3.5 %collective-permute-start = (bf16[128,640]{1,0:T(8,128)(2,1)S(1)}, bf16[128,640]{1,0:T(8,128)(2,1)}, u32[]{:S(2)}, u32[]{:S(2)}) collective-permute-start(bf16[128,640]{1,0:T(8,128)(2,1)S(1)} %prepare.1), channel_id=1, source_target_pairs={{0,16},{1,17},{2,18},{3,19},{4,20},{5,21},{6,22},{7,23},{8,24},{9,... | collective-permute-start | bytes 491528 | tf_op jit(solution)/shard_map/ppermute | solution.py:49
  70.2 3.0 %collective-permute-start.1 = (bf16[128,640]{1,0:T(8,128)(2,1)S(1)}, bf16[128,640]{1,0:T(8,128)(2,1)}, u32[]{:S(2)}, u32[]{:S(2)}) collective-permute-start(bf16[128,640]{1,0:T(8,128)(2,1)S(1)} %prepare.1), channel_id=1, source_target_pairs={{0,256},{1,257},{2,258},{3,259},{4,260},{5,261},{6,262},{7,263},{8... | collective-permute-start | bytes 491528 | tf_op jit(solution)/shard_map/ppermute | solution.py:49
  73.2 3.2 %collective-permute-start.2 = (bf16[128,640]{1,0:T(8,128)(2,1)S(1)}, bf16[128,640]{1,0:T(8,128)(2,1)}, u32[]{:S(2)}, u32[]{:S(2)}) collective-permute-start(bf16[128,640]{1,0:T(8,128)(2,1)S(1)} %prepare.1), channel_id=1, source_target_pairs={{0,272},{1,273},{2,274},{3,275},{4,276},{5,277},{6,278},{7,279},{8... | collective-permute-start | bytes 491528 | tf_op jit(solution)/shard_map/ppermute | solution.py:49
  76.5 6.7 %collective-permute-done = bf16[128,640]{1,0:T(8,128)(2,1)} collective-permute-done((bf16[128,640]{1,0:T(8,128)(2,1)S(1)}, bf16[128,640]{1,0:T(8,128)(2,1)}, u32[]{:S(2)}, u32[]{:S(2)}) %collective-permute-start) | collective-permute-done | bytes 163872 | tf_op jit(solution)/shard_map/ppermute | solution.py:49
  83.2 9.4 %collective-permute-done.2 = bf16[128,640]{1,0:T(8,128)(2,1)} collective-permute-done((bf16[128,640]{1,0:T(8,128)(2,1)S(1)}, bf16[128,640]{1,0:T(8,128)(2,1)}, u32[]{:S(2)}, u32[]{:S(2)}) %collective-permute-start.2) | collective-permute-done | bytes 163872 | tf_op jit(solution)/shard_map/ppermute | solution.py:49
  92.6 1.2 pad_maximum_fusion.q_ref
  93.8 5.4 %attend.1 = bf16[4,128,640]{2,1,0:T(8,128)(2,1)S(1)} custom-call(s32[3]{0:T(128)S(1)} %pad_add_fusion.place_ref, s32[4]{0:T(128)S(1)} %copy-done.10, bf16[4,128,640]{2,1,0:T(8,128)(2,1)S(1)} %pad_maximum_fusion.q_ref, bf16[8,200,128]{2,1,0:T(8,128)(2,1)} %all_gather.16.mine_ref, bf16[8,200,128]{2,1,0:T(8,128)(2,1)} %collective-permute-done.4.theirs_ref), custom_call_target="tpu_custom_call" | custom-call | tf_op jit(solution)/shard_map/attend/pallas_call | solution.py:148
  99.2 15.2 %all_to_all.10.x_ref = bf16[4,128,640]{2,1,0:T(8,128)(2,1)S(1)} all-to-all(bf16[4,128,640]{2,1,0:T(8,128)(2,1)S(1)} %attend.1), channel_id=1, replica_groups=mesh['ylo'=2,'zh'=8,'zl'=2,'x'=4,'yhi'=2,'core'=2] {'ylo','zl'}, dimensions={0} | all-to-all | bytes 1310720 | tf_op jit(solution)/shard_map/all_to_all | solution.py:261
  114.7 14.1 %all-gather = bf16[512,512]{1,0:T(8,128)(2,1)S(1)} all-gather(bf16[128,512]{1,0:T(8,128)(2,1)S(1)} %combine.1), channel_id=2, replica_groups=mesh['ylo'=2,'zh'=8,'zl'=2,'x'=4,'yhi'=2,'core'=2] {'ylo','zl'}, dimensions={0}, use_global_device_ids=true | all-gather | bytes 655360 | tf_op jit(solution)/shard_map/all_gather | solution.py:262
  128.8 1.9 collective-permute-start.5
  131.5 1.1 collective-permute-done.5.other_ref
  133.4 1.6 copy-done.2
  134.9 1.0 copy-done.4
  136.0 1.0 copy-done.6
  137.0 3.1 %project.1 = bf16[2,4,2,2,128,128]{5,4,3,2,1,0:T(8,128)(2,1)S(1)} custom-call(bf16[4,128,512]{2,1,0:T(8,128)(2,1)S(1)} %bitcast.32, bf16[4,128,512]{2,1,0:T(8,128)(2,1)S(1)} %copy-done.6, bf16[8,1024,128]{2,1,0:T(8,128)(2,1)S(1)} %bitcast.30), custom_call_target="tpu_custom_call" | custom-call | tf_op jit(solution)/shard_map/project/pallas_call | solution.py:214
  140.2 1.0 copy-done.1
  141.1 7.7 %all-to-all-start.1 = ((bf16[8,2,2,128,128]{4,3,2,1,0:T(8,128)(2,1)}), bf16[8,2,2,128,128]{4,3,2,1,0:T(8,128)(2,1)}, u32[]{:S(2)}, u32[]{:S(2)}) async-start(bf16[8,2,2,128,128]{4,3,2,1,0:T(8,128)(2,1)} %bitcast.29), calls=%async_computation.1 | async-start | bytes 2097152 | tf_op jit(solution)/shard_map/all_to_all | solution.py:266
  148.9 14.9 %all-to-all-done.1 = bf16[8,2,2,128,128]{4,3,2,1,0:T(8,128)(2,1)} async-done(((bf16[8,2,2,128,128]{4,3,2,1,0:T(8,128)(2,1)}), bf16[8,2,2,128,128]{4,3,2,1,0:T(8,128)(2,1)}, u32[]{:S(2)}, u32[]{:S(2)}) %all-to-all-start.1) | async-done | bytes 1048608 | tf_op jit(solution)/shard_map/all_to_all | solution.py:266
  163.8 1.4 reduce_sum.22
  165.2 2.3 %collective-permute-start.10 = (bf16[128,128]{1,0:T(8,128)(2,1)S(1)}, bf16[128,128]{1,0:T(8,128)(2,1)S(1)}, u32[]{:S(2)}, u32[]{:S(2)}) collective-permute-start(bf16[128,128]{1,0:T(8,128)(2,1)S(1)} %get-tuple-element.11), channel_id=1, source_target_pairs={{0,17},{1,16},{2,19},{3,18},{4,21},{5,20},{6,23},{7,22},{8,273},{9... | collective-permute-start | bytes 98312 | tf_op jit(solution)/shard_map/ppermute | solution.py:63
  167.5 3.7 %collective-permute-start.7 = (bf16[128,128]{1,0:T(8,128)(2,1)S(1)}, bf16[128,128]{1,0:T(8,128)(2,1)S(1)}, u32[]{:S(2)}, u32[]{:S(2)}) collective-permute-start(bf16[128,128]{1,0:T(8,128)(2,1)S(1)} %get-tuple-element.14), channel_id=1, source_target_pairs={{0,0},{1,1},{2,2},{3,3},{4,4},{5,5},{6,6},{7,7},{8,256},{9,257},{1... | collective-permute-start | bytes 98312 | tf_op jit(solution)/shard_map/ppermute | solution.py:63
  171.2 5.4 %collective-permute-start.8 = (bf16[128,128]{1,0:T(8,128)(2,1)S(1)}, bf16[128,128]{1,0:T(8,128)(2,1)S(1)}, u32[]{:S(2)}, u32[]{:S(2)}) collective-permute-start(bf16[128,128]{1,0:T(8,128)(2,1)S(1)} %get-tuple-element.13), channel_id=1, source_target_pairs={{0,1},{1,0},{2,3},{3,2},{4,5},{5,4},{6,7},{7,6},{8,257},{9,256},{1... | collective-permute-start | bytes 98312 | tf_op jit(solution)/shard_map/ppermute | solution.py:63
  176.6 5.5 %collective-permute-start.9 = (bf16[128,128]{1,0:T(8,128)(2,1)S(1)}, bf16[128,128]{1,0:T(8,128)(2,1)S(1)}, u32[]{:S(2)}, u32[]{:S(2)}) collective-permute-start(bf16[128,128]{1,0:T(8,128)(2,1)S(1)} %get-tuple-element.12), channel_id=1, source_target_pairs={{0,16},{1,17},{2,18},{3,19},{4,20},{5,21},{6,22},{7,23},{8,272},{9... | collective-permute-start | bytes 98312 | tf_op jit(solution)/shard_map/ppermute | solution.py:63
  182.1 3.6 %collective-permute-done.9 = bf16[128,128]{1,0:T(8,128)(2,1)S(1)} collective-permute-done((bf16[128,128]{1,0:T(8,128)(2,1)S(1)}, bf16[128,128]{1,0:T(8,128)(2,1)S(1)}, u32[]{:S(2)}, u32[]{:S(2)}) %collective-permute-start.9) | collective-permute-done | bytes 32800 | tf_op jit(solution)/shard_map/ppermute | solution.py:63
  (41 shorter events, 6.2 us)
Async XLA Ops:
  6.5 1.9 copy-start
  6.5 126.8 %all-gather.4.cloned.1.call-start = ((), (), s32[]{:S(2)}) async-start(), calls=%async_computation.2 | async-start | bytes 2359296 | tf_op jit(solution)/shard_map/all_gather | solution.py:239
  8.5 8.8 %copy-start.11 = (f32[128]{0:T(128)S(1)}, f32[128]{0:T(128)}, u32[]{:S(2)}) copy-start(f32[128]{0:T(128)} %param.13) | copy-start | bytes 1540
  11.1 54.4 %copy-start.8 = (s32[128,2]{0,1:T(2,128)S(1)}, s32[128,2]{0,1:T(2,128)}, u32[]{:S(2)}) copy-start(s32[128,2]{0,1:T(2,128)} %param.15) | copy-start | bytes 3076
  11.1 54.4 %copy-start.9 = (f32[128]{0:T(128)S(1)}, f32[128]{0:T(128)}, u32[]{:S(2)}) copy-start(f32[128]{0:T(128)} %param.12) | copy-start | bytes 1540
  11.2 82.6 %copy-start.10 = (s32[4]{0:T(128)S(1)}, s32[4]{0:T(128)}, u32[]{:S(2)}) copy-start(s32[4]{0:T(128)} %count_ref.1) | copy-start | bytes 52
  11.3 8.9 %collective-permute-start.3 = (f32[200]{0:T(256)S(1)}, f32[200]{0:T(256)S(1)}, u32[]{:S(2)}, u32[]{:S(2)}) collective-permute-start(f32[200]{0:T(256)S(1)} %multiply_reduce_fusion), channel_id=1, source_target_pairs={{0,1},{1,0},{2,3},{3,2},{4,5},{5,4},{6,7},{7,6},{8,9},{9,8},{10,11... | collective-permute-start | bytes 2408 | tf_op jit(solution)/shard_map/ppermute | solution.py:42
  14.9 3.7 %collective-permute-start.6 = (bf16[512,128]{1,0:T(8,128)(2,1)}, bf16[512,128]{1,0:T(8,128)(2,1)}, u32[]{:S(2)}, u32[]{:S(2)}) collective-permute-start(bf16[512,128]{1,0:T(8,128)(2,1)} %get-tuple-element.6), channel_id=1, source_target_pairs={{0,1},{1,0},{2,3},{3,2},{4,5},{5,4},{6,7},{7,6},{8,9},{9,8},{10,11... | collective-permute-start | bytes 393224 | tf_op jit(solution)/shard_map/ppermute | solution.py:42
  63.6 30.2 %collective-permute-start.4 = (bf16[8,200,128]{2,1,0:T(8,128)(2,1)}, bf16[8,200,128]{2,1,0:T(8,128)(2,1)}, u32[]{:S(2)}, u32[]{:S(2)}) collective-permute-start(bf16[8,200,128]{2,1,0:T(8,128)(2,1)} %all_gather.16.mine_ref), channel_id=1, source_target_pairs={{0,1},{1,0},{2,3},{3,2},{4,5},{5,4},{6,7},{7,6},{8,9},{9,8},{10,11... | collective-permute-start | bytes 1228808 | tf_op jit(solution)/shard_map/ppermute | solution.py:42
  65.5 0.9 copy-start.7
  66.7 16.5 %collective-permute-start = (bf16[128,640]{1,0:T(8,128)(2,1)S(1)}, bf16[128,640]{1,0:T(8,128)(2,1)}, u32[]{:S(2)}, u32[]{:S(2)}) collective-permute-start(bf16[128,640]{1,0:T(8,128)(2,1)S(1)} %prepare.1), channel_id=1, source_target_pairs={{0,16},{1,17},{2,18},{3,19},{4,20},{5,21},{6,22},{7,23},{8,24},{9,... | collective-permute-start | bytes 491528 | tf_op jit(solution)/shard_map/ppermute | solution.py:49
  70.2 13.0 %collective-permute-start.1 = (bf16[128,640]{1,0:T(8,128)(2,1)S(1)}, bf16[128,640]{1,0:T(8,128)(2,1)}, u32[]{:S(2)}, u32[]{:S(2)}) collective-permute-start(bf16[128,640]{1,0:T(8,128)(2,1)S(1)} %prepare.1), channel_id=1, source_target_pairs={{0,256},{1,257},{2,258},{3,259},{4,260},{5,261},{6,262},{7,263},{8... | collective-permute-start | bytes 491528 | tf_op jit(solution)/shard_map/ppermute | solution.py:49
  73.2 19.3 %collective-permute-start.2 = (bf16[128,640]{1,0:T(8,128)(2,1)S(1)}, bf16[128,640]{1,0:T(8,128)(2,1)}, u32[]{:S(2)}, u32[]{:S(2)}) collective-permute-start(bf16[128,640]{1,0:T(8,128)(2,1)S(1)} %prepare.1), channel_id=1, source_target_pairs={{0,272},{1,273},{2,274},{3,275},{4,276},{5,277},{6,278},{7,279},{8... | collective-permute-start | bytes 491528 | tf_op jit(solution)/shard_map/ppermute | solution.py:49
  128.8 3.8 %collective-permute-start.5 = (bf16[4,128,512]{2,1,0:T(8,128)(2,1)S(1)}, bf16[4,128,512]{2,1,0:T(8,128)(2,1)S(1)}, u32[]{:S(2)}, u32[]{:S(2)}) collective-permute-start(bf16[4,128,512]{2,1,0:T(8,128)(2,1)S(1)} %bitcast.31), channel_id=1, source_target_pairs={{0,1},{1,0},{2,3},{3,2},{4,5},{5,4},{6,7},{7,6},{8,9},{9,8},{10,11... | collective-permute-start | bytes 1572872 | tf_op jit(solution)/shard_map/ppermute | solution.py:42
  130.7 0.8 copy-start.3
  132.5 0.8 copy-start.5
  133.4 1.6 copy-start.2
  134.9 1.0 copy-start.4
  136.0 1.0 copy-start.6
  140.2 1.0 copy-start.1
  141.1 22.7 %all-to-all-start.1 = ((bf16[8,2,2,128,128]{4,3,2,1,0:T(8,128)(2,1)}), bf16[8,2,2,128,128]{4,3,2,1,0:T(8,128)(2,1)}, u32[]{:S(2)}, u32[]{:S(2)}) async-start(bf16[8,2,2,128,128]{4,3,2,1,0:T(8,128)(2,1)} %bitcast.29), calls=%async_computation.1 | async-start | bytes 2097152 | tf_op jit(solution)/shard_map/all_to_all | solution.py:266
  165.2 16.9 %collective-permute-start.10 = (bf16[128,128]{1,0:T(8,128)(2,1)S(1)}, bf16[128,128]{1,0:T(8,128)(2,1)S(1)}, u32[]{:S(2)}, u32[]{:S(2)}) collective-permute-start(bf16[128,128]{1,0:T(8,128)(2,1)S(1)} %get-tuple-element.11), channel_id=1, source_target_pairs={{0,17},{1,16},{2,19},{3,18},{4,21},{5,20},{6,23},{7,22},{8,273},{9... | collective-permute-start | bytes 98312 | tf_op jit(solution)/shard_map/ppermute | solution.py:63
  167.5 14.6 %collective-permute-start.7 = (bf16[128,128]{1,0:T(8,128)(2,1)S(1)}, bf16[128,128]{1,0:T(8,128)(2,1)S(1)}, u32[]{:S(2)}, u32[]{:S(2)}) collective-permute-start(bf16[128,128]{1,0:T(8,128)(2,1)S(1)} %get-tuple-element.14), channel_id=1, source_target_pairs={{0,0},{1,1},{2,2},{3,3},{4,4},{5,5},{6,6},{7,7},{8,256},{9,257},{1... | collective-permute-start | bytes 98312 | tf_op jit(solution)/shard_map/ppermute | solution.py:63
  171.2 10.9 %collective-permute-start.8 = (bf16[128,128]{1,0:T(8,128)(2,1)S(1)}, bf16[128,128]{1,0:T(8,128)(2,1)S(1)}, u32[]{:S(2)}, u32[]{:S(2)}) collective-permute-start(bf16[128,128]{1,0:T(8,128)(2,1)S(1)} %get-tuple-element.13), channel_id=1, source_target_pairs={{0,1},{1,0},{2,3},{3,2},{4,5},{5,4},{6,7},{7,6},{8,257},{9,256},{1... | collective-permute-start | bytes 98312 | tf_op jit(solution)/shard_map/ppermute | solution.py:63
  176.6 9.1 %collective-permute-start.9 = (bf16[128,128]{1,0:T(8,128)(2,1)S(1)}, bf16[128,128]{1,0:T(8,128)(2,1)S(1)}, u32[]{:S(2)}, u32[]{:S(2)}) collective-permute-start(bf16[128,128]{1,0:T(8,128)(2,1)S(1)} %get-tuple-element.12), channel_id=1, source_target_pairs={{0,16},{1,17},{2,18},{3,19},{4,20},{5,21},{6,22},{7,23},{8,272},{9... | collective-permute-start | bytes 98312 | tf_op jit(solution)/shard_map/ppermute | solution.py:63
Sparse Core Ops, SparseCore 0:
  20.3 78.8 all-gather.3

commit v3 on v2

v3 whole, which is shorter than its diff:
```python
import math

import jax
import jax.numpy as jnp
from jax import lax
from jax.experimental import pallas as pl
from jax.experimental.pallas import tpu as pltpu
from jax.sharding import Mesh, PartitionSpec as P

HD = 128
TILES = 4
EPSILON = 1e-05
NEG = -1e30
AXES = ("ylo", "z", "x", "yhi", "core")
SIZES = (2, 16, 4, 2, 2)
ROWS = 128
HEADS = 4
WIDTH = HEADS * HD
LOCAL = 200
BLOCKS = 16
SLOTS = BLOCKS * LOCAL
BF = jnp.bfloat16
F32 = jnp.float32


def flat(ylo, z, x, yhi, core):
    return (((ylo * 16 + z) * 4 + x) * 2 + yhi) * 2 + core


def swapped(value, axis):
    return lax.ppermute(value, axis, [(0, 1), (1, 0)])


def placed(value, flip):
    pairs = []
    for source in range(512):
        core, yhi, x, z = source % 2, source // 2 % 2, source // 4 % 4, source // 16 % 16
        target = flat(x // 2, z, 2 * (source // 256) + x % 2, yhi, core ^ flip)
        pairs.append((source, target))
    return lax.ppermute(value, AXES, pairs)


def vmem():
    return pl.BlockSpec(memory_space=pltpu.VMEM)


def smem():
    return pl.BlockSpec(memory_space=pltpu.SMEM)


def params(mib):
    return pltpu.CompilerParams(vmem_limit_bytes=mib << 20)


def prepare_kernel(q_ref, gain_ref, span_ref, o_ref):
    gain = gain_ref[...]
    for head in range(HEADS):
        columns = slice(head * HD, (head + 1) * HD)
        field = q_ref[:, columns].astype(F32)
        mean_sq = jnp.mean(field * field, axis=1, keepdims=True)
        o_ref[:, columns] = (field / jnp.sqrt(mean_sq + EPSILON) * gain).astype(BF)
    row = lax.broadcasted_iota(jnp.int32, (ROWS, HD), 0)
    lane = lax.broadcasted_iota(jnp.int32, (ROWS, HD), 1)
    begin = jnp.sum(jnp.where(row == lane, span_ref[0:1, :], 0), axis=1, keepdims=True)
    end = jnp.sum(jnp.where(row == lane, span_ref[1:2, :], 0), axis=1, keepdims=True)
    inside = (begin <= lane) & (lane < end)
    o_ref[:, WIDTH:] = jnp.where((lane <= TILES) & ~inside, NEG, 0.0).astype(BF)


def prepare(queries, q_gain, spans):
    return pl.pallas_call(
        prepare_kernel,
        in_specs=[vmem(), vmem(), vmem()],
        out_specs=vmem(),
        out_shape=jax.ShapeDtypeStruct((ROWS, WIDTH + HD), BF),
        compiler_params=params(4),
        name="prepare",
    )(queries, q_gain.reshape(1, HD), spans.T)


def attend_kernel(place_ref, count_ref, q_ref, far_ref, mine_ref, theirs_ref, o_ref, key_s, value_s):
    core, ylo = place_ref[0], place_ref[1]
    half = HD // 2
    lane = lax.broadcasted_iota(jnp.int32, (LOCAL, HD), 1)
    item = lax.broadcasted_iota(jnp.int32, (LOCAL, HD), 0)
    for block in range(BLOCKS):
        rows = slice(block * LOCAL, (block + 1) * LOCAL)
        mine, theirs = mine_ref[block], theirs_ref[block]
        left = jnp.where(core == 0, mine, theirs)
        right = jnp.where(core == 0, theirs, mine)
        key_s[rows, :HD] = jnp.concatenate([left[:, :half], right[:, :half]], axis=1)
        value_s[rows, :HD] = jnp.concatenate([left[:, half:], right[:, half:]], axis=1)
        tile = 2 * ylo + block // 8
        absent = item + (block % 8) * LOCAL >= count_ref[tile]
        key_s[rows, HD:] = jnp.where(
            (lane == tile) | ((lane == TILES) & absent), 1.0, 0.0
        ).astype(BF)
    value_s[:, HD:] = jnp.ones((SLOTS, HD), BF)
    query_ext = jnp.concatenate([q_ref[:, WIDTH:], far_ref[:, WIDTH:]], axis=0)
    wide = lax.broadcasted_iota(jnp.int32, (2 * ROWS, HD), 1)
    totals = jnp.zeros((2 * ROWS, HD), F32)
    for head in range(HEADS):
        columns = slice(head * HD, (head + 1) * HD)
        query = jnp.concatenate([q_ref[:, columns], far_ref[:, columns]], axis=0)
        scores = lax.dot_general(
            jnp.concatenate([query, query_ext], axis=1),
            key_s[...],
            (((1,), (1,)), ((), ())),
            preferred_element_type=F32,
        )
        weights = jnp.exp2(scores * (math.log2(math.e) / math.sqrt(HD))).astype(BF)
        result = jnp.dot(weights, value_s[...], preferred_element_type=F32)
        numer = result[:, :HD].astype(BF)
        o_ref[ylo, :, columns] = numer[:ROWS]
        o_ref[1 - ylo, :, columns] = numer[ROWS:]
        totals = jnp.where(wide % HEADS == head, result[:, HD:], totals)
    high = totals.astype(BF)
    low = (totals - high.astype(F32)).astype(BF)
    packed = jnp.where(wide < HEADS, high.astype(F32), low.astype(F32)).astype(BF)
    o_ref[ylo, :, WIDTH:] = packed[:ROWS]
    o_ref[1 - ylo, :, WIDTH:] = packed[ROWS:]


def attend(place, counts, query, far, mine, theirs):
    return pl.pallas_call(
        attend_kernel,
        in_specs=[smem(), smem(), vmem(), vmem(), vmem(), vmem()],
        out_specs=vmem(),
        out_shape=jax.ShapeDtypeStruct((2, ROWS, WIDTH + HD), BF),
        scratch_shapes=[pltpu.VMEM((SLOTS, 2 * HD), BF), pltpu.VMEM((SLOTS, 2 * HD), BF)],
        compiler_params=params(32),
        name="attend",
    )(place, counts, query, far, mine, theirs)


def combine_kernel(near_ref, far_ref, o_ref):
    for block in range(2):
        summed = near_ref[block].astype(F32) + far_ref[block].astype(F32)
        for head in range(HEADS):
            columns = slice(head * HD, (head + 1) * HD)
            high = summed[:, WIDTH + head : WIDTH + head + 1]
            low = summed[:, WIDTH + HEADS + head : WIDTH + HEADS + head + 1]
            rows = slice(block * ROWS, (block + 1) * ROWS)
            o_ref[rows, columns] = (summed[:, columns] / (high + low)).astype(BF)


def combine(near, far):
    return pl.pallas_call(
        combine_kernel,
        in_specs=[vmem(), vmem()],
        out_specs=vmem(),
        out_shape=jax.ShapeDtypeStruct((2 * ROWS, WIDTH), BF),
        compiler_params=params(4),
        name="combine",
    )(near, far)


def project_kernel(own_ref, other_ref, w_hbm, o_hbm, w_s, o_s, in_sem, out_sem):
    steps = BLOCKS // 2
    fetch = [
        pltpu.make_async_copy(
            w_hbm.at[pl.ds(2 * step, 2)], w_s.at[pl.ds(2 * step, 2)], in_sem.at[step]
        )
        for step in range(steps)
    ]
    for copy in fetch:
        copy.start()
    drain = []
    for step in range(steps):
        fetch[step].wait()
        weight = jnp.concatenate([w_s[2 * step], w_s[2 * step + 1]], axis=1)
        result = jnp.dot(own_ref[...], weight[:WIDTH], preferred_element_type=F32)
        result = result + jnp.dot(other_ref[...], weight[WIDTH:], preferred_element_type=F32)
        result = result.astype(BF)
        o_s[step, 0] = result[:ROWS]
        o_s[step, 1] = result[ROWS:]
        copy = pltpu.make_async_copy(
            o_s.at[step], o_hbm.at[:, step // 2, step % 2], out_sem.at[step]
        )
        copy.start()
        drain.append(copy)
    for copy in drain:
        copy.wait()


def project(own, other, weight):
    hbm = pl.BlockSpec(memory_space=pltpu.HBM)
    return pl.pallas_call(
        project_kernel,
        in_specs=[vmem(), vmem(), hbm],
        out_specs=hbm,
        out_shape=jax.ShapeDtypeStruct((2, 4, 2, ROWS, 2 * HD), BF),
        scratch_shapes=[
            pltpu.VMEM((BLOCKS, 2 * WIDTH, HD), BF),
            pltpu.VMEM((8, 2, ROWS, 2 * HD), BF),
            pltpu.SemaphoreType.DMA((8,)),
            pltpu.SemaphoreType.DMA((8,)),
        ],
        compiler_params=params(12),
        name="project",
    )(own, other, weight)


def local(queries, vision, kv_weight, out_weight, q_gain, k_gain, tile_counts, spans):
    core = lax.axis_index("core")
    ylo = lax.axis_index("ylo")
    half = HD // 2

    query = prepare(queries, q_gain, spans)
    vision, query = lax.optimization_barrier((vision, query))
    far = swapped(query, "ylo")

    kept = lax.dynamic_slice_in_dim(out_weight, core * HD, HD, axis=1)
    sent = lax.dynamic_slice_in_dim(out_weight, (1 - core) * HD, HD, axis=1)
    pair = jnp.concatenate([kept, swapped(sent, "core")], axis=0)
    weight = lax.all_gather(pair, "z", axis=0, tiled=False)

    both = jnp.transpose(kv_weight, (0, 2, 1)).reshape(HD, vision.shape[1])
    projected = lax.dot_general(
        vision, both, (((1,), (1,)), ((), ())), preferred_element_type=F32
    )
    key_raw = projected[:, :half]
    own_squares = jnp.sum(key_raw * key_raw, axis=1)
    inverse = 1.0 / jnp.sqrt((own_squares + swapped(own_squares, "core")) / HD + EPSILON)
    gain_half = lax.dynamic_slice_in_dim(k_gain, core * half, half)
    key_half = key_raw * inverse[:, None] * gain_half[None, :]
    local_pair = jnp.concatenate([key_half, projected[:, half:]], axis=1).astype(BF)
    local_pair, far = lax.optimization_barrier((local_pair, far))
    mine = lax.all_gather(local_pair, "z", axis=0, tiled=False)
    theirs = swapped(mine, "core")

    place = jnp.stack([core, ylo]).astype(jnp.int32)
    partial = attend(place, tile_counts, query, far, mine, theirs)
    own = combine(partial, swapped(partial, "ylo"))
    other = swapped(own, "core")

    product = project(own, other, weight).reshape(8, 2, ROWS, 2 * HD)
    parts = lax.all_to_all(product, ("x", "yhi"), 0, 0, tiled=True)
    summed = jnp.sum(parts.astype(F32), axis=0).astype(BF)
    same = placed(lax.dynamic_index_in_dim(summed, core, 0, keepdims=False), 0)
    cross = placed(lax.dynamic_index_in_dim(summed, 1 - core, 0, keepdims=False), 1)
    even = jnp.where(core == 0, same, cross)
    odd = jnp.where(core == 0, cross, same)
    return jnp.concatenate([even[:, :HD], odd[:, :HD], even[:, HD:], odd[:, HD:]], axis=1)


def solution(mesh):
    split = Mesh(mesh.devices.reshape(SIZES), AXES)
    seq, head = ("ylo", "z"), ("x", "yhi", "core")
    return jax.shard_map(
        local,
        mesh=split,
        in_specs=(
            P(seq, head),
            P(seq, None),
            P(None, None, head),
            P(head, seq),
            P(),
            P(),
            P(),
            P(seq, None),
        ),
        out_specs=P(seq, head),
        check_vma=False,
    )
```

time: 196 us -> 158 us (0.81)
  blocking collectives: 71.6 us -> 48 us
  starting transfers between devices: 42.4 us -> 29.1 us
  other arithmetic: 6.04 us -> 3.95 us
    ppermute x3 -> x0, waiting for transfers between devices: 16.1 us -> none  [crossed(): return lax.ppermute(value, AXES, pairs)]
    all_to_all x1 -> x0, blocking collectives: 15.2 us -> none  [local(): attended = combine(lax.all_to_all(partial, QUAD, 0, 0, tiled=True))]
    ppermute x4 -> x6, waiting for transfers between devices: 1.58 us -> 16.5 us  [swapped(): return lax.ppermute(value, axis, [(0, 1), (1, 0)])]
    ppermute x4 -> x2, starting transfers between devices: 16.8 us -> 5.71 us  [placed(): return lax.ppermute(value, AXES, pairs)]
    ppermute x3 -> x0, starting transfers between devices: 9.72 us -> none  [crossed(): return lax.ppermute(value, AXES, pairs)]
    all_gather x2 -> x1, blocking collectives: 56.4 us -> 48 us  [local(): mine = lax.all_gather(local_pair, 'z', axis=0, tiled=False)]
    ppermute x4 -> x6, starting transfers between devices: 8.14 us -> 14.3 us  [swapped(): return lax.ppermute(value, axis, [(0, 1), (1, 0)])]
    ppermute x4 -> x2, waiting for transfers between devices: 3.57 us -> 6.05 us  [placed(): return lax.ppermute(value, AXES, pairs)]
  transfers between devices with their start and end apart: 13 -> 10, of which waited for: 6 -> 8; matrix products, arithmetic and copies ran while one was open for 3% -> 3% of each run, Pallas kernels for 3% -> 4%
where the time goes in v3:
time: 158 us; the launch traced here: 155 us
  blocking collectives  48 us (30%)
  waiting for transfers between devices  37.5 us (24%)
  starting transfers between devices  29.1 us (18%)
  between operations  13.6 us (9%)
  Pallas kernels  10.7 us (7%)
  local copies, waits for them, and re-layouts  9.7 us (6%)
  other arithmetic  3.95 us (2%)
  matrix products  2.66 us (2%)
    all_gather x1, blocking collectives, local(): mine = lax.all_gather(local_pair, 'z', axis=0, tiled=False)  48 us
    ppermute x6, waiting for transfers between devices, swapped(): return lax.ppermute(value, axis, [(0, 1), (1, 0)])  16.5 us
    all_to_all x1, waiting for transfers between devices, local(): parts = lax.all_to_all(product, ('x', 'yhi'), 0, 0, tiled=True)  14.9 us
    ppermute x6, starting transfers between devices, swapped(): return lax.ppermute(value, axis, [(0, 1), (1, 0)])  14.3 us
    all_to_all x1, starting transfers between devices, local(): parts = lax.all_to_all(product, ('x', 'yhi'), 0, 0, tiled=True)  9.07 us
    unnamed x18, local copies, waits for them, and re-layouts  7.08 us
    ppermute x2, waiting for transfers between devices, placed(): return lax.ppermute(value, AXES, pairs)  6.05 us
    ppermute x2, starting transfers between devices, placed(): return lax.ppermute(value, AXES, pairs)  5.71 us
  transfers between devices with their start and end apart: 10, of which 8 were waited for; matrix products, arithmetic and copies ran while one was open for 3% of the time, Pallas kernels for 4%

profile of v3, /device:TPU:6, one launch (start us, length us, event | category | flops | bytes accessed | tf_op | source)
XLA Modules:
  0.0 155.2 jit_solution(15725668154301222026)
XLA Ops:
  6.5 1.1 constant_dynamic-slice_fusion.1
  7.7 1.9 %collective-permute-start.5 = (bf16[512,128]{1,0:T(8,128)(2,1)S(1)}, bf16[512,128]{1,0:T(8,128)(2,1)S(1)}, u32[]{:S(2)}, u32[]{:S(2)}) collective-permute-start(bf16[512,128]{1,0:T(8,128)(2,1)S(1)} %get-tuple-element.14), channel_id=1, source_target_pairs={{0,1},{1,0},{2,3},{3,2},{4,5},{5,4},{6,7},{7,6},{8,9},{9,8},{10,11... | collective-permute-start | bytes 393224 | tf_op jit(solution)/shard_map/ppermute | solution.py:31
  9.6 1.3 collective-permute-done.5
  10.9 0.7 pad_maximum_fusion
  11.7 0.9 copy-done.5
  14.2 2.7 %fusion.2 = f32[200,128]{1,0:T(8,128)S(1)} fusion(bf16[200,8192]{1,0:T(8,128)(2,1)S(1)} %copy-done, bf16[128,8192]{1,0:T(8,128)(2,1)} %bitcast.20), kind=kOutput, calls=%fused_computation.16 | convolution fusion | flops 419430400 | bytes 5476352 | tf_op jit(solution)/shard_map/dot_general | solution.py:219
  17.0 2.1 %collective-permute-start = (f32[200]{0:T(256)S(1)}, f32[200]{0:T(256)S(1)}, u32[]{:S(2)}, u32[]{:S(2)}) collective-permute-start(f32[200]{0:T(256)S(1)} %multiply_reduce_fusion), channel_id=1, source_target_pairs={{0,1},{1,0},{2,3},{3,2},{4,5},{5,4},{6,7},{7,6},{8,9},{9,8},{10,11... | collective-permute-start | bytes 2408 | tf_op jit(solution)/shard_map/ppermute | solution.py:31
  19.0 3.5 %collective-permute-start.1 = (bf16[128,640]{1,0:T(8,128)(2,1)S(1)}, bf16[128,640]{1,0:T(8,128)(2,1)}, u32[]{:S(2)}, u32[]{:S(2)}) collective-permute-start(bf16[128,640]{1,0:T(8,128)(2,1)S(1)} %prepare.1.q_ref), channel_id=1, source_target_pairs={{0,256},{256,0},{1,257},{257,1},{2,258},{258,2},{3,259},{259,3},{4... | collective-permute-start | bytes 491528 | tf_op jit(solution)/shard_map/ppermute | solution.py:31
  22.5 0.7 slice.34
  23.2 0.7 dynamic_slice.16
  24.1 0.9 pad_maximum_fusion.2
  25.0 2.5 %collective-permute-done.1.far_ref = bf16[128,640]{1,0:T(8,128)(2,1)} collective-permute-done((bf16[128,640]{1,0:T(8,128)(2,1)S(1)}, bf16[128,640]{1,0:T(8,128)(2,1)}, u32[]{:S(2)}, u32[]{:S(2)}) %collective-permute-start.1) | collective-permute-done | bytes 163872 | tf_op jit(solution)/shard_map/ppermute | solution.py:31
  27.5 48.0 %all-gather = bf16[3200,128]{1,0:T(8,128)(2,1)} all-gather(bf16[200,128]{1,0:T(8,128)(2,1)S(1)} %pad_maximum_fusion.2), channel_id=2, replica_groups=mesh['ylo'=2,'z'=16,'x'=4,'yhi'=2,'core'=2] {'z'}, dimensions={0}, use_global_device_ids=true | all-gather | bytes 870400 | tf_op jit(solution)/shard_map/all_gather | solution.py:229
  75.5 1.9 %collective-permute-start.2 = (bf16[16,200,128]{2,1,0:T(8,128)(2,1)}, bf16[16,200,128]{2,1,0:T(8,128)(2,1)}, u32[]{:S(2)}, u32[]{:S(2)}) collective-permute-start(bf16[16,200,128]{2,1,0:T(8,128)(2,1)} %bitcast.6.mine_ref), channel_id=1, source_target_pairs={{0,1},{1,0},{2,3},{3,2},{4,5},{5,4},{6,7},{7,6},{8,9},{9,8},{10,11... | collective-permute-start | bytes 2457608 | tf_op jit(solution)/shard_map/ppermute | solution.py:31
  77.5 2.6 %collective-permute-done.2.theirs_ref = bf16[16,200,128]{2,1,0:T(8,128)(2,1)} collective-permute-done((bf16[16,200,128]{2,1,0:T(8,128)(2,1)}, bf16[16,200,128]{2,1,0:T(8,128)(2,1)}, u32[]{:S(2)}, u32[]{:S(2)}) %collective-permute-start.2) | collective-permute-done | bytes 819232 | tf_op jit(solution)/shard_map/ppermute | solution.py:31
  80.1 5.7 %attend.1.near_ref = bf16[2,128,640]{2,1,0:T(8,128)(2,1)S(1)} custom-call(s32[2]{0:T(128)S(1)} %pad_add_fusion.place_ref, s32[4]{0:T(128)S(1)} %copy-done.8, bf16[128,640]{1,0:T(8,128)(2,1)S(1)} %prepare.1.q_ref, bf16[128,640]{1,0:T(8,128)(2,1)} %collective-permute-done.1.far_ref, bf16[16,200,128]{2,1,0:T(8,128)(2,1)} %bitcast.6.mine_ref, ...), custom_call_target="tpu_custom_call" | custom-call | tf_op jit(solution)/shard_map/attend/pallas_call | solution.py:125
  85.7 3.0 %collective-permute-start.3 = (bf16[2,128,640]{2,1,0:T(8,128)(2,1)S(1)}, bf16[2,128,640]{2,1,0:T(8,128)(2,1)S(1)}, u32[]{:S(2)}, u32[]{:S(2)}) collective-permute-start(bf16[2,128,640]{2,1,0:T(8,128)(2,1)S(1)} %attend.1.near_ref), channel_id=1, source_target_pairs={{0,256},{256,0},{1,257},{257,1},{2,258},{258,2},{3,259},{259,3},{4... | collective-permute-start | bytes 983048 | tf_op jit(solution)/shard_map/ppermute | solution.py:31
  88.7 8.6 %collective-permute-done.3.far_ref = bf16[2,128,640]{2,1,0:T(8,128)(2,1)S(1)} collective-permute-done((bf16[2,128,640]{2,1,0:T(8,128)(2,1)S(1)}, bf16[2,128,640]{2,1,0:T(8,128)(2,1)S(1)}, u32[]{:S(2)}, u32[]{:S(2)}) %collective-permute-start.3) | collective-permute-done | bytes 327712 | tf_op jit(solution)/shard_map/ppermute | solution.py:31
  97.8 1.9 %collective-permute-start.4 = (bf16[256,512]{1,0:T(8,128)(2,1)S(1)}, bf16[256,512]{1,0:T(8,128)(2,1)S(1)}, u32[]{:S(2)}, u32[]{:S(2)}) collective-permute-start(bf16[256,512]{1,0:T(8,128)(2,1)S(1)} %combine.1.own_ref), channel_id=1, source_target_pairs={{0,1},{1,0},{2,3},{3,2},{4,5},{5,4},{6,7},{7,6},{8,9},{9,8},{10,11... | collective-permute-start | bytes 786440 | tf_op jit(solution)/shard_map/ppermute | solution.py:31
  99.7 1.5 collective-permute-done.4.other_ref
  101.2 0.7 copy-done.3
  101.9 2.2 %copy-done.1 = bf16[16384,128]{1,0:T(8,128)(2,1)S(1)} copy-done((bf16[16384,128]{1,0:T(8,128)(2,1)S(1)}, bf16[16384,128]{1,0:T(8,128)(2,1)}, u32[]{:S(2)}) %copy-start.1) | copy-done | bytes 4194328
  104.1 0.9 copy-done.4
  105.1 4.4 %project.1 = bf16[2,4,2,128,256]{4,3,2,1,0:T(8,128)(2,1)S(1)} custom-call(bf16[256,512]{1,0:T(8,128)(2,1)S(1)} %combine.1.own_ref, bf16[256,512]{1,0:T(8,128)(2,1)S(1)} %copy-done.4, bf16[16,1024,128]{2,1,0:T(8,128)(2,1)S(1)} %bitcast.16), custom_call_target="tpu_custom_call" | custom-call | tf_op jit(solution)/shard_map/project/pallas_call | solution.py:188
  109.5 1.0 copy-done.2
  110.5 9.1 %all-to-all-start = ((bf16[8,2,128,256]{3,2,1,0:T(8,128)(2,1)}), bf16[8,2,128,256]{3,2,1,0:T(8,128)(2,1)}, u32[]{:S(2)}, u32[]{:S(2)}) async-start(bf16[8,2,128,256]{3,2,1,0:T(8,128)(2,1)} %bitcast.17), calls=%async_computation | async-start | bytes 2097152 | tf_op jit(solution)/shard_map/all_to_all | solution.py:238
  119.6 14.9 %all-to-all-done = bf16[8,2,128,256]{3,2,1,0:T(8,128)(2,1)} async-done(((bf16[8,2,128,256]{3,2,1,0:T(8,128)(2,1)}), bf16[8,2,128,256]{3,2,1,0:T(8,128)(2,1)}, u32[]{:S(2)}, u32[]{:S(2)}) %all-to-all-start) | async-done | bytes 1048608 | tf_op jit(solution)/shard_map/all_to_all | solution.py:238
  134.5 1.4 reduce_sum.22
  135.9 3.8 %collective-permute-start.6 = (bf16[128,256]{1,0:T(8,128)(2,1)S(1)}, bf16[128,256]{1,0:T(8,128)(2,1)S(1)}, u32[]{:S(2)}, u32[]{:S(2)}) collective-permute-start(bf16[128,256]{1,0:T(8,128)(2,1)S(1)} %get-tuple-element.17), channel_id=1, source_target_pairs={{0,0},{1,1},{2,2},{3,3},{4,4},{5,5},{6,6},{7,7},{8,256},{9,257},{1... | collective-permute-start | bytes 196616 | tf_op jit(solution)/shard_map/ppermute | solution.py:40
  139.7 1.9 %collective-permute-start.7 = (bf16[128,256]{1,0:T(8,128)(2,1)S(1)}, bf16[128,256]{1,0:T(8,128)(2,1)S(1)}, u32[]{:S(2)}, u32[]{:S(2)}) collective-permute-start(bf16[128,256]{1,0:T(8,128)(2,1)S(1)} %get-tuple-element.18), channel_id=1, source_target_pairs={{0,1},{1,0},{2,3},{3,2},{4,5},{5,4},{6,7},{7,6},{8,257},{9,256},{1... | collective-permute-start | bytes 196616 | tf_op jit(solution)/shard_map/ppermute | solution.py:40
  141.6 2.8 %collective-permute-done.6 = bf16[128,256]{1,0:T(8,128)(2,1)S(1)} collective-permute-done((bf16[128,256]{1,0:T(8,128)(2,1)S(1)}, bf16[128,256]{1,0:T(8,128)(2,1)S(1)}, u32[]{:S(2)}, u32[]{:S(2)}) %collective-permute-start.6) | collective-permute-done | bytes 65568 | tf_op jit(solution)/shard_map/ppermute | solution.py:40
  144.5 3.2 %collective-permute-done.7 = bf16[128,256]{1,0:T(8,128)(2,1)S(1)} collective-permute-done((bf16[128,256]{1,0:T(8,128)(2,1)S(1)}, bf16[128,256]{1,0:T(8,128)(2,1)S(1)}, u32[]{:S(2)}, u32[]{:S(2)}) %collective-permute-start.7) | collective-permute-done | bytes 65568 | tf_op jit(solution)/shard_map/ppermute | solution.py:40
  (27 shorter events, 3.0 us)
Async XLA Ops:
  6.5 7.6 %copy-start = (bf16[200,8192]{1,0:T(8,128)(2,1)S(1)}, bf16[200,8192]{1,0:T(8,128)(2,1)}, u32[]{:S(2)}) copy-start(bf16[200,8192]{1,0:T(8,128)(2,1)} %param.9) | copy-start | bytes 9830404
  6.5 95.4 %all-gather.4.cloned.1.call-start = ((), (), s32[]{:S(2)}) async-start(), calls=%async_computation.1 | async-start | bytes 4456448 | tf_op jit(solution)/shard_map/all_gather | solution.py:216
  7.7 3.2 %collective-permute-start.5 = (bf16[512,128]{1,0:T(8,128)(2,1)S(1)}, bf16[512,128]{1,0:T(8,128)(2,1)S(1)}, u32[]{:S(2)}, u32[]{:S(2)}) collective-permute-start(bf16[512,128]{1,0:T(8,128)(2,1)S(1)} %get-tuple-element.14), channel_id=1, source_target_pairs={{0,1},{1,0},{2,3},{3,2},{4,5},{5,4},{6,7},{7,6},{8,9},{9,8},{10,11... | collective-permute-start | bytes 393224 | tf_op jit(solution)/shard_map/ppermute | solution.py:31
  11.7 0.9 copy-start.5
  12.6 0.7 copy-start.6
  13.2 0.7 copy-start.7
  14.2 65.9 %copy-start.8 = (s32[4]{0:T(128)S(1)}, s32[4]{0:T(128)}, u32[]{:S(2)}) copy-start(s32[4]{0:T(128)} %count_ref.1) | copy-start | bytes 52
  17.0 7.0 %collective-permute-start = (f32[200]{0:T(256)S(1)}, f32[200]{0:T(256)S(1)}, u32[]{:S(2)}, u32[]{:S(2)}) collective-permute-start(f32[200]{0:T(256)S(1)} %multiply_reduce_fusion), channel_id=1, source_target_pairs={{0,1},{1,0},{2,3},{3,2},{4,5},{5,4},{6,7},{7,6},{8,9},{9,8},{10,11... | collective-permute-start | bytes 2408 | tf_op jit(solution)/shard_map/ppermute | solution.py:31
  19.0 8.5 %collective-permute-start.1 = (bf16[128,640]{1,0:T(8,128)(2,1)S(1)}, bf16[128,640]{1,0:T(8,128)(2,1)}, u32[]{:S(2)}, u32[]{:S(2)}) collective-permute-start(bf16[128,640]{1,0:T(8,128)(2,1)S(1)} %prepare.1.q_ref), channel_id=1, source_target_pairs={{0,256},{256,0},{1,257},{257,1},{2,258},{258,2},{3,259},{259,3},{4... | collective-permute-start | bytes 491528 | tf_op jit(solution)/shard_map/ppermute | solution.py:31
  75.5 4.6 %collective-permute-start.2 = (bf16[16,200,128]{2,1,0:T(8,128)(2,1)}, bf16[16,200,128]{2,1,0:T(8,128)(2,1)}, u32[]{:S(2)}, u32[]{:S(2)}) collective-permute-start(bf16[16,200,128]{2,1,0:T(8,128)(2,1)} %bitcast.6.mine_ref), channel_id=1, source_target_pairs={{0,1},{1,0},{2,3},{3,2},{4,5},{5,4},{6,7},{7,6},{8,9},{9,8},{10,11... | collective-permute-start | bytes 2457608 | tf_op jit(solution)/shard_map/ppermute | solution.py:31
  85.7 11.6 %collective-permute-start.3 = (bf16[2,128,640]{2,1,0:T(8,128)(2,1)S(1)}, bf16[2,128,640]{2,1,0:T(8,128)(2,1)S(1)}, u32[]{:S(2)}, u32[]{:S(2)}) collective-permute-start(bf16[2,128,640]{2,1,0:T(8,128)(2,1)S(1)} %attend.1.near_ref), channel_id=1, source_target_pairs={{0,256},{256,0},{1,257},{257,1},{2,258},{258,2},{3,259},{259,3},{4... | collective-permute-start | bytes 983048 | tf_op jit(solution)/shard_map/ppermute | solution.py:31
  97.8 3.4 %collective-permute-start.4 = (bf16[256,512]{1,0:T(8,128)(2,1)S(1)}, bf16[256,512]{1,0:T(8,128)(2,1)S(1)}, u32[]{:S(2)}, u32[]{:S(2)}) collective-permute-start(bf16[256,512]{1,0:T(8,128)(2,1)S(1)} %combine.1.own_ref), channel_id=1, source_target_pairs={{0,1},{1,0},{2,3},{3,2},{4,5},{5,4},{6,7},{7,6},{8,9},{9,8},{10,11... | collective-permute-start | bytes 786440 | tf_op jit(solution)/shard_map/ppermute | solution.py:31
  101.2 0.7 copy-start.3
  101.9 2.2 %copy-start.1 = (bf16[16384,128]{1,0:T(8,128)(2,1)S(1)}, bf16[16384,128]{1,0:T(8,128)(2,1)}, u32[]{:S(2)}) copy-start(bf16[16384,128]{1,0:T(8,128)(2,1)} %all-gather.4.cloned.1.call-done) | copy-start | bytes 12582916
  104.1 0.9 copy-start.4
  109.5 1.0 copy-start.2
  110.5 24.0 %all-to-all-start = ((bf16[8,2,128,256]{3,2,1,0:T(8,128)(2,1)}), bf16[8,2,128,256]{3,2,1,0:T(8,128)(2,1)}, u32[]{:S(2)}, u32[]{:S(2)}) async-start(bf16[8,2,128,256]{3,2,1,0:T(8,128)(2,1)} %bitcast.17), calls=%async_computation | async-start | bytes 2097152 | tf_op jit(solution)/shard_map/all_to_all | solution.py:238
  135.9 8.6 %collective-permute-start.6 = (bf16[128,256]{1,0:T(8,128)(2,1)S(1)}, bf16[128,256]{1,0:T(8,128)(2,1)S(1)}, u32[]{:S(2)}, u32[]{:S(2)}) collective-permute-start(bf16[128,256]{1,0:T(8,128)(2,1)S(1)} %get-tuple-element.17), channel_id=1, source_target_pairs={{0,0},{1,1},{2,2},{3,3},{4,4},{5,5},{6,6},{7,7},{8,256},{9,257},{1... | collective-permute-start | bytes 196616 | tf_op jit(solution)/shard_map/ppermute | solution.py:40
  139.7 8.0 %collective-permute-start.7 = (bf16[128,256]{1,0:T(8,128)(2,1)S(1)}, bf16[128,256]{1,0:T(8,128)(2,1)S(1)}, u32[]{:S(2)}, u32[]{:S(2)}) collective-permute-start(bf16[128,256]{1,0:T(8,128)(2,1)S(1)} %get-tuple-element.18), channel_id=1, source_target_pairs={{0,1},{1,0},{2,3},{3,2},{4,5},{5,4},{6,7},{7,6},{8,257},{9,256},{1... | collective-permute-start | bytes 196616 | tf_op jit(solution)/shard_map/ppermute | solution.py:40
Sparse Core Ops, SparseCore 0:
  11.8 87.1 all-gather.3

commit v4 on v3

--- a/solution.py
+++ b/solution.py
@@ -70,12 +70,44 @@
 def prepare(queries, q_gain, spans):
     return pl.pallas_call(
         prepare_kernel,
-        in_specs=[vmem(), vmem(), vmem()],
-        out_specs=vmem(),
         out_shape=jax.ShapeDtypeStruct((ROWS, WIDTH + HD), BF),
         compiler_params=params(4),
         name="prepare",
     )(queries, q_gain.reshape(1, HD), spans.T)
+
+
+def column(row, count):
+    width = row.shape[1]
+    across = lax.broadcasted_iota(jnp.int32, (count, width), 1)
+    down = lax.broadcasted_iota(jnp.int32, (count, width), 0)
+    return jnp.sum(jnp.where(across == down, row, 0.0), axis=1, keepdims=True)
+
+
+def pack_kernel(place_ref, x_ref, own_ref, other_ref, gain_ref, o_ref):
+    mean_sq = (column(own_ref[...], LOCAL) + column(other_ref[...], LOCAL)) / HD
+    gain = gain_ref[...]
+    gain = jnp.where(place_ref[0] == 0, gain, jnp.concatenate([gain[:, HD // 2 :]] * 2, axis=1))
+    lane = lax.broadcasted_iota(jnp.int32, (LOCAL, HD), 1)
+    field = x_ref[...]
+    key = field / jnp.sqrt(mean_sq + EPSILON) * gain
+    o_ref[...] = jnp.where(lane < HD // 2, key, field).astype(BF)
+
+
+def pack(place, projected, own_squares, other_squares, k_gain):
+    return pl.pallas_call(
+        pack_kernel,
+        in_specs=[smem(), vmem(), vmem(), vmem(), vmem()],
+        out_specs=vmem(),
+        out_shape=jax.ShapeDtypeStruct((LOCAL, HD), BF),
+        compiler_params=params(4),
+        name="pack",
+    )(
+        place,
+        projected,
+        own_squares.reshape(1, LOCAL),
+        other_squares.reshape(1, LOCAL),
+        k_gain.reshape(1, HD),
+    )
 
 
 def attend_kernel(place_ref, count_ref, q_ref, far_ref, mine_ref, theirs_ref, o_ref, key_s, value_s):
@@ -198,13 +230,59 @@
         ],
         compiler_params=params(12),
         name="project",
-    )(own, other, weight)
+    )(own, other, pltpu.with_memory_space_constraint(weight, pltpu.HBM))
+
+
+def reduce_kernel(place_ref, x_ref, same_ref, cross_ref):
+    sums = []
+    for core in range(2):
+        total = x_ref[0, core].astype(F32)
+        for source in range(1, 8):
+            total = total + x_ref[source, core].astype(F32)
+        sums.append(total)
+    first = place_ref[0] == 0
+    same_ref[...] = jnp.where(first, sums[0], sums[1]).astype(BF)
+    cross_ref[...] = jnp.where(first, sums[1], sums[0]).astype(BF)
+
+
+def reduce(place, parts):
+    return pl.pallas_call(
+        reduce_kernel,
+        in_specs=[smem(), vmem()],
+        out_specs=[vmem(), vmem()],
+        out_shape=[jax.ShapeDtypeStruct((ROWS, 2 * HD), BF)] * 2,
+        compiler_params=params(4),
+        name="reduce",
+    )(place, parts)
+
+
+def assemble_kernel(place_ref, same_ref, cross_ref, o_ref):
+    first = place_ref[0] == 0
+    same, cross = same_ref[...].astype(F32), cross_ref[...].astype(F32)
+    even = jnp.where(first, same, cross).astype(BF)
+    odd = jnp.where(first, cross, same).astype(BF)
+    o_ref[:, 0:HD] = even[:, :HD]
+    o_ref[:, HD : 2 * HD] = odd[:, :HD]
+    o_ref[:, 2 * HD : 3 * HD] = even[:, HD:]
+    o_ref[:, 3 * HD :] = odd[:, HD:]
+
+
+def assemble(place, same, cross):
+    return pl.pallas_call(
+        assemble_kernel,
+        in_specs=[smem(), vmem(), vmem()],
+        out_shape=jax.ShapeDtypeStruct((ROWS, WIDTH), BF),
+        compiler_params=params(4),
+        name="assemble",
+    )(place, same, cross)
 
 
 def local(queries, vision, kv_weight, out_weight, q_gain, k_gain, tile_counts, spans):
     core = lax.axis_index("core")
     ylo = lax.axis_index("ylo")
     half = HD // 2
+
+    place = jnp.stack([core, ylo]).astype(jnp.int32)
 
     query = prepare(queries, q_gain, spans)
     vision, query = lax.optimization_barrier((vision, query))
@@ -221,27 +299,18 @@
     )
     key_raw = projected[:, :half]
     own_squares = jnp.sum(key_raw * key_raw, axis=1)
-    inverse = 1.0 / jnp.sqrt((own_squares + swapped(own_squares, "core")) / HD + EPSILON)
-    gain_half = lax.dynamic_slice_in_dim(k_gain, core * half, half)
-    key_half = key_raw * inverse[:, None] * gain_half[None, :]
-    local_pair = jnp.concatenate([key_half, projected[:, half:]], axis=1).astype(BF)
-    local_pair, far = lax.optimization_barrier((local_pair, far))
+    local_pair = pack(place, projected, own_squares, swapped(own_squares, "core"), k_gain)
     mine = lax.all_gather(local_pair, "z", axis=0, tiled=False)
     theirs = swapped(mine, "core")
 
-    place = jnp.stack([core, ylo]).astype(jnp.int32)
     partial = attend(place, tile_counts, query, far, mine, theirs)
     own = combine(partial, swapped(partial, "ylo"))
     other = swapped(own, "core")
 
     product = project(own, other, weight).reshape(8, 2, ROWS, 2 * HD)
     parts = lax.all_to_all(product, ("x", "yhi"), 0, 0, tiled=True)
-    summed = jnp.sum(parts.astype(F32), axis=0).astype(BF)
-    same = placed(lax.dynamic_index_in_dim(summed, core, 0, keepdims=False), 0)
-    cross = placed(lax.dynamic_index_in_dim(summed, 1 - core, 0, keepdims=False), 1)
-    even = jnp.where(core == 0, same, cross)
-    odd = jnp.where(core == 0, cross, same)
-    return jnp.concatenate([even[:, :HD], odd[:, :HD], even[:, HD:], odd[:, HD:]], axis=1)
+    same, cross = reduce(place, parts)
+    return assemble(place, placed(same, 0), placed(cross, 1))
 
 
 def solution(mesh):

time: 158 us -> 151 us (0.956); the launches traced: 155 us -> 150 us
  blocking collectives: 48 us -> 70 us
  waiting for transfers between devices: 37.5 us -> 22.6 us
  starting transfers between devices: 29.1 us -> 21 us
  local copies, waits for them, and re-layouts: 9.7 us -> 6.33 us
  other arithmetic: 3.95 us -> 0.9 us
  Pallas kernels: 10.7 us -> 13.2 us
    all_to_all x0 -> x1, blocking collectives: none -> 21.9 us  [local(): parts = lax.all_to_all(product, ('x', 'yhi'), 0, 0, tiled=True)]
    all_to_all x1 -> x0, waiting for transfers between devices: 14.9 us -> none  [local(): parts = lax.all_to_all(product, ('x', 'yhi'), 0, 0, tiled=True)]
    all_to_all x1 -> x0, starting transfers between devices: 9.07 us -> none  [local(): parts = lax.all_to_all(product, ('x', 'yhi'), 0, 0, tiled=True)]
    pallas_call x1 -> x4, Pallas kernels: 0.25 us -> 2.86 us  [the longest x1 1.23 us: assemble(): pl.pallas_call(assemble_kernel, in_specs=[smem(), vmem(), vmem()], out_sh...]
    unnamed x18 -> x16, local copies, waits for them, and re-layouts: 7.08 us -> 5.19 us
  transfers between devices with their start and end apart: 10 -> 9, of which waited for: 8 -> 7; matrix products, arithmetic and copies ran while one was open for 3% -> 2% of each run, Pallas kernels for 4% -> 4%
where the time goes in v4:
time: 151 us; the launch traced here: 150 us
  blocking collectives  70 us (46%)
  waiting for transfers between devices  22.6 us (15%)
  starting transfers between devices  21 us (14%)
  between operations  13.5 us (9%)
  Pallas kernels  13.2 us (9%)
  local copies, waits for them, and re-layouts  6.33 us (4%)
  matrix products  2.65 us (2%)
    all_gather x1, blocking collectives, local(): mine = lax.all_gather(local_pair, 'z', axis=0, tiled=False)  48.2 us
    all_to_all x1, blocking collectives, local(): parts = lax.all_to_all(product, ('x', 'yhi'), 0, 0, tiled=True)  21.9 us
    ppermute x6, waiting for transfers between devices, swapped(): return lax.ppermute(value, axis, [(0, 1), (1, 0)])  16.5 us
    ppermute x6, starting transfers between devices, swapped(): return lax.ppermute(value, axis, [(0, 1), (1, 0)])  14.8 us
    ppermute x2, starting transfers between devices, placed(): return lax.ppermute(value, AXES, pairs)  6.2 us
    ppermute x2, waiting for transfers between devices, placed(): return lax.ppermute(value, AXES, pairs)  6.06 us
    unnamed x16, local copies, waits for them, and re-layouts  5.19 us
    pallas_call x1, Pallas kernels, project(): pl.pallas_call(project_kernel, in_specs=[vmem(), vmem(), hbm], out_specs=...  5.17 us
  transfers between devices with their start and end apart: 9, of which 7 were waited for; matrix products, arithmetic and copies ran while one was open for 2% of the time, Pallas kernels for 4%

profile of v4, /device:TPU:6, one launch (start us, length us, event | category | flops | bytes accessed | tf_op | source)
XLA Modules:
  0.0 150.3 jit_solution(14435389567842170684)
XLA Ops:
  6.5 1.1 constant_dynamic-slice_fusion.1
  7.7 1.9 %collective-permute-start.5 = (bf16[512,128]{1,0:T(8,128)(2,1)S(1)}, bf16[512,128]{1,0:T(8,128)(2,1)S(1)}, u32[]{:S(2)}, u32[]{:S(2)}) collective-permute-start(bf16[512,128]{1,0:T(8,128)(2,1)S(1)} %get-tuple-element.14), channel_id=1, source_target_pairs={{0,1},{1,0},{2,3},{3,2},{4,5},{5,4},{6,7},{7,6},{8,9},{9,8},{10,11... | collective-permute-start | bytes 393224 | tf_op jit(solution)/shard_map/ppermute | solution.py:31
  9.6 1.3 collective-permute-done.5
  10.9 0.7 pad_maximum_fusion
  11.7 0.9 copy-done.3
  12.6 0.7 copy-done.4
  13.3 0.7 copy-done.5
  14.2 2.7 %fusion.1.x_ref = f32[200,128]{1,0:T(8,128)S(1)} fusion(bf16[200,8192]{1,0:T(8,128)(2,1)S(1)} %copy-done, bf16[128,8192]{1,0:T(8,128)(2,1)} %bitcast.24), kind=kOutput, calls=%fused_computation.6 | convolution fusion | flops 419430400 | bytes 5476352 | tf_op jit(solution)/shard_map/dot_general | solution.py:297
  17.0 2.1 %collective-permute-start.1 = (f32[200]{0:T(256)S(1)}, f32[200]{0:T(256)S(1)}, u32[]{:S(2)}, u32[]{:S(2)}) collective-permute-start(f32[200]{0:T(256)S(1)} %fusion), channel_id=1, source_target_pairs={{0,1},{1,0},{2,3},{3,2},{4,5},{5,4},{6,7},{7,6},{8,9},{9,8},{10,11... | collective-permute-start | bytes 2408 | tf_op jit(solution)/shard_map/ppermute | solution.py:31
  19.1 0.9 collective-permute-done.1
  20.0 0.7 copy-done.6
  20.6 0.7 pack.1
  21.3 48.2 %all-gather = bf16[3200,128]{1,0:T(8,128)(2,1)S(1)} all-gather(bf16[200,128]{1,0:T(8,128)(2,1)S(1)} %pack.1), channel_id=2, replica_groups=mesh['ylo'=2,'z'=16,'x'=4,'yhi'=2,'core'=2] {'z'}, dimensions={0}, use_global_device_ids=true | all-gather | bytes 870400 | tf_op jit(solution)/shard_map/all_gather | solution.py:303
  69.5 1.9 %collective-permute-start.2 = (bf16[16,200,128]{2,1,0:T(8,128)(2,1)S(1)}, bf16[16,200,128]{2,1,0:T(8,128)(2,1)S(1)}, u32[]{:S(2)}, u32[]{:S(2)}) collective-permute-start(bf16[16,200,128]{2,1,0:T(8,128)(2,1)S(1)} %bitcast.16), channel_id=1, source_target_pairs={{0,1},{1,0},{2,3},{3,2},{4,5},{5,4},{6,7},{7,6},{8,9},{9,8},{10,11... | collective-permute-start | bytes 2457608 | tf_op jit(solution)/shard_map/ppermute | solution.py:31
  71.4 3.5 %collective-permute-start = (bf16[128,640]{1,0:T(8,128)(2,1)S(1)}, bf16[128,640]{1,0:T(8,128)(2,1)S(1)}, u32[]{:S(2)}, u32[]{:S(2)}) collective-permute-start(bf16[128,640]{1,0:T(8,128)(2,1)S(1)} %prepare.1.q_ref), channel_id=1, source_target_pairs={{0,256},{256,0},{1,257},{257,1},{2,258},{258,2},{3,259},{259,3},{4... | collective-permute-start | bytes 491528 | tf_op jit(solution)/shard_map/ppermute | solution.py:31
  75.0 5.0 %collective-permute-done.far_ref = bf16[128,640]{1,0:T(8,128)(2,1)S(1)} collective-permute-done((bf16[128,640]{1,0:T(8,128)(2,1)S(1)}, bf16[128,640]{1,0:T(8,128)(2,1)S(1)}, u32[]{:S(2)}, u32[]{:S(2)}) %collective-permute-start) | collective-permute-done | bytes 163872 | tf_op jit(solution)/shard_map/ppermute | solution.py:31
  79.9 0.7 copy-done.7
  80.6 4.8 %attend.1.near_ref = bf16[2,128,640]{2,1,0:T(8,128)(2,1)S(1)} custom-call(s32[2]{0:T(128)S(1)} %pad_add_fusion.place_ref, s32[4]{0:T(128)S(1)} %copy-done.7, bf16[128,640]{1,0:T(8,128)(2,1)S(1)} %prepare.1.q_ref, bf16[128,640]{1,0:T(8,128)(2,1)S(1)} %collective-permute-done.far_ref, bf16[16,200,128]{2,1,0:T(8,128)(2,1)S(1)} %bitcast.17, ...), custom_call_target="tpu_custom_call" | custom-call | tf_op jit(solution)/shard_map/attend/pallas_call | solution.py:157
  85.4 3.5 %collective-permute-start.3 = (bf16[2,128,640]{2,1,0:T(8,128)(2,1)S(1)}, bf16[2,128,640]{2,1,0:T(8,128)(2,1)S(1)}, u32[]{:S(2)}, u32[]{:S(2)}) collective-permute-start(bf16[2,128,640]{2,1,0:T(8,128)(2,1)S(1)} %attend.1.near_ref), channel_id=1, source_target_pairs={{0,256},{256,0},{1,257},{257,1},{2,258},{258,2},{3,259},{259,3},{4... | collective-permute-start | bytes 983048 | tf_op jit(solution)/shard_map/ppermute | solution.py:31
  88.9 7.8 %collective-permute-done.3.far_ref = bf16[2,128,640]{2,1,0:T(8,128)(2,1)S(1)} collective-permute-done((bf16[2,128,640]{2,1,0:T(8,128)(2,1)S(1)}, bf16[2,128,640]{2,1,0:T(8,128)(2,1)S(1)}, u32[]{:S(2)}, u32[]{:S(2)}) %collective-permute-start.3) | collective-permute-done | bytes 327712 | tf_op jit(solution)/shard_map/ppermute | solution.py:31
  97.1 1.9 %collective-permute-start.4 = (bf16[256,512]{1,0:T(8,128)(2,1)S(1)}, bf16[256,512]{1,0:T(8,128)(2,1)S(1)}, u32[]{:S(2)}, u32[]{:S(2)}) collective-permute-start(bf16[256,512]{1,0:T(8,128)(2,1)S(1)} %combine.1.own_ref), channel_id=1, source_target_pairs={{0,1},{1,0},{2,3},{3,2},{4,5},{5,4},{6,7},{7,6},{8,9},{9,8},{10,11... | collective-permute-start | bytes 786440 | tf_op jit(solution)/shard_map/ppermute | solution.py:31
  99.0 1.5 collective-permute-done.4.other_ref
  100.6 0.7 copy-done.1
  101.2 0.9 copy-done.2
  102.2 5.2 %project.1 = bf16[2,4,2,128,256]{4,3,2,1,0:T(8,128)(2,1)S(1)} custom-call(bf16[256,512]{1,0:T(8,128)(2,1)S(1)} %combine.1.own_ref, bf16[256,512]{1,0:T(8,128)(2,1)S(1)} %copy-done.2, bf16[16,1024,128]{2,1,0:T(8,128)(2,1)} %bitcast.23), custom_call_target="tpu_custom_call" | custom-call | tf_op jit(solution)/shard_map/project/pallas_call | solution.py:220
  107.4 21.9 %all_to_all.5.x_ref = bf16[8,2,128,256]{3,2,1,0:T(8,128)(2,1)S(1)} all-to-all(bf16[8,2,128,256]{3,2,1,0:T(8,128)(2,1)S(1)} %bitcast.15), channel_id=1, replica_groups=mesh['ylo'=2,'z'=16,'x'=4,'yhi'=2,'core'=2] {'x','yhi'}, dimensions={0} | all-to-all | bytes 2097152 | tf_op jit(solution)/shard_map/all_to_all | solution.py:311
  129.2 0.7 reduce.1
  129.9 4.3 %collective-permute-start.6 = (bf16[128,256]{1,0:T(8,128)(2,1)S(1)}, bf16[128,256]{1,0:T(8,128)(2,1)S(1)}, u32[]{:S(2)}, u32[]{:S(2)}) collective-permute-start(bf16[128,256]{1,0:T(8,128)(2,1)S(1)} %get-tuple-element.11), channel_id=1, source_target_pairs={{0,0},{1,1},{2,2},{3,3},{4,4},{5,5},{6,6},{7,7},{8,256},{9,257},{1... | collective-permute-start | bytes 196616 | tf_op jit(solution)/shard_map/ppermute | solution.py:40
  134.2 1.9 %collective-permute-start.7 = (bf16[128,256]{1,0:T(8,128)(2,1)S(1)}, bf16[128,256]{1,0:T(8,128)(2,1)S(1)}, u32[]{:S(2)}, u32[]{:S(2)}) collective-permute-start(bf16[128,256]{1,0:T(8,128)(2,1)S(1)} %get-tuple-element.12), channel_id=1, source_target_pairs={{0,1},{1,0},{2,3},{3,2},{4,5},{5,4},{6,7},{7,6},{8,257},{9,256},{1... | collective-permute-start | bytes 196616 | tf_op jit(solution)/shard_map/ppermute | solution.py:40
  136.1 2.3 %collective-permute-done.6.same_ref = bf16[128,256]{1,0:T(8,128)(2,1)S(1)} collective-permute-done((bf16[128,256]{1,0:T(8,128)(2,1)S(1)}, bf16[128,256]{1,0:T(8,128)(2,1)S(1)}, u32[]{:S(2)}, u32[]{:S(2)}) %collective-permute-start.6) | collective-permute-done | bytes 65568 | tf_op jit(solution)/shard_map/ppermute | solution.py:40
  138.5 3.7 %collective-permute-done.7.cross_ref = bf16[128,256]{1,0:T(8,128)(2,1)S(1)} collective-permute-done((bf16[128,256]{1,0:T(8,128)(2,1)S(1)}, bf16[128,256]{1,0:T(8,128)(2,1)S(1)}, u32[]{:S(2)}, u32[]{:S(2)}) %collective-permute-start.7) | collective-permute-done | bytes 65568 | tf_op jit(solution)/shard_map/ppermute | solution.py:40
  142.2 1.2 assemble.1
  (17 shorter events, 0.9 us)
Async XLA Ops:
  6.5 7.6 %copy-start = (bf16[200,8192]{1,0:T(8,128)(2,1)S(1)}, bf16[200,8192]{1,0:T(8,128)(2,1)}, u32[]{:S(2)}) copy-start(bf16[200,8192]{1,0:T(8,128)(2,1)} %param.9) | copy-start | bytes 9830404
  6.5 94.7 %all-gather.4.cloned.1.call-start = ((), (), s32[]{:S(2)}) async-start(), calls=%async_computation.1 | async-start | bytes 4456448 | tf_op jit(solution)/shard_map/all_gather | solution.py:294
  7.7 3.2 %collective-permute-start.5 = (bf16[512,128]{1,0:T(8,128)(2,1)S(1)}, bf16[512,128]{1,0:T(8,128)(2,1)S(1)}, u32[]{:S(2)}, u32[]{:S(2)}) collective-permute-start(bf16[512,128]{1,0:T(8,128)(2,1)S(1)} %get-tuple-element.14), channel_id=1, source_target_pairs={{0,1},{1,0},{2,3},{3,2},{4,5},{5,4},{6,7},{7,6},{8,9},{9,8},{10,11... | collective-permute-start | bytes 393224 | tf_op jit(solution)/shard_map/ppermute | solution.py:31
  11.7 0.9 copy-start.3
  12.6 0.7 copy-start.4
  13.3 0.7 copy-start.5
  17.0 3.0 %collective-permute-start.1 = (f32[200]{0:T(256)S(1)}, f32[200]{0:T(256)S(1)}, u32[]{:S(2)}, u32[]{:S(2)}) collective-permute-start(f32[200]{0:T(256)S(1)} %fusion), channel_id=1, source_target_pairs={{0,1},{1,0},{2,3},{3,2},{4,5},{5,4},{6,7},{7,6},{8,9},{9,8},{10,11... | collective-permute-start | bytes 2408 | tf_op jit(solution)/shard_map/ppermute | solution.py:31
  20.0 0.7 copy-start.6
  69.5 10.4 %collective-permute-start.2 = (bf16[16,200,128]{2,1,0:T(8,128)(2,1)S(1)}, bf16[16,200,128]{2,1,0:T(8,128)(2,1)S(1)}, u32[]{:S(2)}, u32[]{:S(2)}) collective-permute-start(bf16[16,200,128]{2,1,0:T(8,128)(2,1)S(1)} %bitcast.16), channel_id=1, source_target_pairs={{0,1},{1,0},{2,3},{3,2},{4,5},{5,4},{6,7},{7,6},{8,9},{9,8},{10,11... | collective-permute-start | bytes 2457608 | tf_op jit(solution)/shard_map/ppermute | solution.py:31
  71.4 8.5 %collective-permute-start = (bf16[128,640]{1,0:T(8,128)(2,1)S(1)}, bf16[128,640]{1,0:T(8,128)(2,1)S(1)}, u32[]{:S(2)}, u32[]{:S(2)}) collective-permute-start(bf16[128,640]{1,0:T(8,128)(2,1)S(1)} %prepare.1.q_ref), channel_id=1, source_target_pairs={{0,256},{256,0},{1,257},{257,1},{2,258},{258,2},{3,259},{259,3},{4... | collective-permute-start | bytes 491528 | tf_op jit(solution)/shard_map/ppermute | solution.py:31
  79.9 0.7 copy-start.7
  85.4 11.3 %collective-permute-start.3 = (bf16[2,128,640]{2,1,0:T(8,128)(2,1)S(1)}, bf16[2,128,640]{2,1,0:T(8,128)(2,1)S(1)}, u32[]{:S(2)}, u32[]{:S(2)}) collective-permute-start(bf16[2,128,640]{2,1,0:T(8,128)(2,1)S(1)} %attend.1.near_ref), channel_id=1, source_target_pairs={{0,256},{256,0},{1,257},{257,1},{2,258},{258,2},{3,259},{259,3},{4... | collective-permute-start | bytes 983048 | tf_op jit(solution)/shard_map/ppermute | solution.py:31
  97.1 3.4 %collective-permute-start.4 = (bf16[256,512]{1,0:T(8,128)(2,1)S(1)}, bf16[256,512]{1,0:T(8,128)(2,1)S(1)}, u32[]{:S(2)}, u32[]{:S(2)}) collective-permute-start(bf16[256,512]{1,0:T(8,128)(2,1)S(1)} %combine.1.own_ref), channel_id=1, source_target_pairs={{0,1},{1,0},{2,3},{3,2},{4,5},{5,4},{6,7},{7,6},{8,9},{9,8},{10,11... | collective-permute-start | bytes 786440 | tf_op jit(solution)/shard_map/ppermute | solution.py:31
  100.6 0.7 copy-start.1
  101.2 1.0 copy-start.2
  129.9 8.6 %collective-permute-start.6 = (bf16[128,256]{1,0:T(8,128)(2,1)S(1)}, bf16[128,256]{1,0:T(8,128)(2,1)S(1)}, u32[]{:S(2)}, u32[]{:S(2)}) collective-permute-start(bf16[128,256]{1,0:T(8,128)(2,1)S(1)} %get-tuple-element.11), channel_id=1, source_target_pairs={{0,0},{1,1},{2,2},{3,3},{4,4},{5,5},{6,6},{7,7},{8,256},{9,257},{1... | collective-permute-start | bytes 196616 | tf_op jit(solution)/shard_map/ppermute | solution.py:40
  134.2 8.0 %collective-permute-start.7 = (bf16[128,256]{1,0:T(8,128)(2,1)S(1)}, bf16[128,256]{1,0:T(8,128)(2,1)S(1)}, u32[]{:S(2)}, u32[]{:S(2)}) collective-permute-start(bf16[128,256]{1,0:T(8,128)(2,1)S(1)} %get-tuple-element.12), channel_id=1, source_target_pairs={{0,1},{1,0},{2,3},{3,2},{4,5},{5,4},{6,7},{7,6},{8,257},{9,256},{1... | collective-permute-start | bytes 196616 | tf_op jit(solution)/shard_map/ppermute | solution.py:40
Sparse Core Ops, SparseCore 0:
  11.8 86.6 all-gather.3

commit v5 on v4

--- a/solution.py
+++ b/solution.py
@@ -68,12 +68,16 @@
 
 
 def prepare(queries, q_gain, spans):
+    inputs = (queries, q_gain.reshape(1, HD), spans.T)
     return pl.pallas_call(
         prepare_kernel,
+        grid=(1,),
+        in_specs=[pl.BlockSpec(value.shape, lambda i: (0, 0)) for value in inputs],
+        out_specs=pl.BlockSpec((ROWS, WIDTH + HD), lambda i: (0, 0)),
         out_shape=jax.ShapeDtypeStruct((ROWS, WIDTH + HD), BF),
         compiler_params=params(4),
         name="prepare",
-    )(queries, q_gain.reshape(1, HD), spans.T)
+    )(*(pltpu.with_memory_space_constraint(value, pltpu.HBM) for value in inputs))
 
 
 def column(row, count):
@@ -110,7 +114,7 @@
     )
 
 
-def attend_kernel(place_ref, count_ref, q_ref, far_ref, mine_ref, theirs_ref, o_ref, key_s, value_s):
+def attend_kernel(place_ref, q_ref, far_ref, mine_ref, theirs_ref, o_ref, key_s, value_s):
     core, ylo = place_ref[0], place_ref[1]
     half = HD // 2
     lane = lax.broadcasted_iota(jnp.int32, (LOCAL, HD), 1)
@@ -123,7 +127,7 @@
         key_s[rows, :HD] = jnp.concatenate([left[:, :half], right[:, :half]], axis=1)
         value_s[rows, :HD] = jnp.concatenate([left[:, half:], right[:, half:]], axis=1)
         tile = 2 * ylo + block // 8
-        absent = item + (block % 8) * LOCAL >= count_ref[tile]
+        absent = item + (block % 8) * LOCAL >= place_ref[2 + tile]
         key_s[rows, HD:] = jnp.where(
             (lane == tile) | ((lane == TILES) & absent), 1.0, 0.0
         ).astype(BF)
@@ -153,16 +157,16 @@
     o_ref[1 - ylo, :, WIDTH:] = packed[ROWS:]
 
 
-def attend(place, counts, query, far, mine, theirs):
+def attend(place, query, far, mine, theirs):
     return pl.pallas_call(
         attend_kernel,
-        in_specs=[smem(), smem(), vmem(), vmem(), vmem(), vmem()],
+        in_specs=[smem(), vmem(), vmem(), vmem(), vmem()],
         out_specs=vmem(),
         out_shape=jax.ShapeDtypeStruct((2, ROWS, WIDTH + HD), BF),
         scratch_shapes=[pltpu.VMEM((SLOTS, 2 * HD), BF), pltpu.VMEM((SLOTS, 2 * HD), BF)],
         compiler_params=params(32),
         name="attend",
-    )(place, counts, query, far, mine, theirs)
+    )(place, query, far, mine, theirs)
 
 
 def combine_kernel(near_ref, far_ref, o_ref):
@@ -187,8 +191,10 @@
     )(near, far)
 
 
-def project_kernel(own_ref, other_ref, w_hbm, o_hbm, w_s, o_s, in_sem, out_sem):
+def project_kernel(own_ref, other_hbm, w_hbm, o_hbm, a_s, w_s, o_s, in_sem, out_sem):
     steps = BLOCKS // 2
+    other = pltpu.make_async_copy(other_hbm, a_s, in_sem.at[steps])
+    other.start()
     fetch = [
         pltpu.make_async_copy(
             w_hbm.at[pl.ds(2 * step, 2)], w_s.at[pl.ds(2 * step, 2)], in_sem.at[step]
@@ -197,13 +203,13 @@
     ]
     for copy in fetch:
         copy.start()
+    other.wait()
+    attended = jnp.concatenate([own_ref[...], a_s[...]], axis=1)
     drain = []
     for step in range(steps):
         fetch[step].wait()
         weight = jnp.concatenate([w_s[2 * step], w_s[2 * step + 1]], axis=1)
-        result = jnp.dot(own_ref[...], weight[:WIDTH], preferred_element_type=F32)
-        result = result + jnp.dot(other_ref[...], weight[WIDTH:], preferred_element_type=F32)
-        result = result.astype(BF)
+        result = jnp.dot(attended, weight, preferred_element_type=F32).astype(BF)
         o_s[step, 0] = result[:ROWS]
         o_s[step, 1] = result[ROWS:]
         copy = pltpu.make_async_copy(
@@ -219,18 +225,23 @@
     hbm = pl.BlockSpec(memory_space=pltpu.HBM)
     return pl.pallas_call(
         project_kernel,
-        in_specs=[vmem(), vmem(), hbm],
+        in_specs=[vmem(), hbm, hbm],
         out_specs=hbm,
         out_shape=jax.ShapeDtypeStruct((2, 4, 2, ROWS, 2 * HD), BF),
         scratch_shapes=[
+            pltpu.VMEM((2 * ROWS, WIDTH), BF),
             pltpu.VMEM((BLOCKS, 2 * WIDTH, HD), BF),
             pltpu.VMEM((8, 2, ROWS, 2 * HD), BF),
-            pltpu.SemaphoreType.DMA((8,)),
+            pltpu.SemaphoreType.DMA((9,)),
             pltpu.SemaphoreType.DMA((8,)),
         ],
         compiler_params=params(12),
         name="project",
-    )(own, other, pltpu.with_memory_space_constraint(weight, pltpu.HBM))
+    )(
+        own,
+        pltpu.with_memory_space_constraint(other, pltpu.HBM),
+        pltpu.with_memory_space_constraint(weight, pltpu.HBM),
+    )
 
 
 def reduce_kernel(place_ref, x_ref, same_ref, cross_ref):
@@ -282,28 +293,29 @@
     ylo = lax.axis_index("ylo")
     half = HD // 2
 
-    place = jnp.stack([core, ylo]).astype(jnp.int32)
+    place = jnp.concatenate([jnp.stack([core, ylo]).astype(jnp.int32), tile_counts])
 
     query = prepare(queries, q_gain, spans)
-    vision, query = lax.optimization_barrier((vision, query))
-    far = swapped(query, "ylo")
 
     kept = lax.dynamic_slice_in_dim(out_weight, core * HD, HD, axis=1)
     sent = lax.dynamic_slice_in_dim(out_weight, (1 - core) * HD, HD, axis=1)
-    pair = jnp.concatenate([kept, swapped(sent, "core")], axis=0)
+    got, query = lax.optimization_barrier((swapped(sent, "core"), query))
+    pair = jnp.concatenate([kept, got], axis=0)
+    far = swapped(query, "ylo")
     weight = lax.all_gather(pair, "z", axis=0, tiled=False)
 
     both = jnp.transpose(kv_weight, (0, 2, 1)).reshape(HD, vision.shape[1])
     projected = lax.dot_general(
         vision, both, (((1,), (1,)), ((), ())), preferred_element_type=F32
     )
+    projected, far = lax.optimization_barrier((projected, far))
     key_raw = projected[:, :half]
     own_squares = jnp.sum(key_raw * key_raw, axis=1)
     local_pair = pack(place, projected, own_squares, swapped(own_squares, "core"), k_gain)
     mine = lax.all_gather(local_pair, "z", axis=0, tiled=False)
     theirs = swapped(mine, "core")
 
-    partial = attend(place, tile_counts, query, far, mine, theirs)
+    partial = attend(place, query, far, mine, theirs)
     own = combine(partial, swapped(partial, "ylo"))
     other = swapped(own, "core")
 

time: 151 us -> 146 us (0.967)
  local copies, waits for them, and re-layouts: 6.33 us -> 1.15 us
  blocking collectives: 70 us -> 67.2 us
    unnamed x16 -> x6, local copies, waits for them, and re-layouts: 5.19 us -> 0.02 us
    all_gather x1, waiting for transfers between devices: 0.01 us -> 2.47 us  [local(): weight = lax.all_gather(pair, 'z', axis=0, tiled=False)]
    all_to_all x1, blocking collectives: 21.9 us -> 20 us  [local(): parts = lax.all_to_all(product, ('x', 'yhi'), 0, 0, tiled=True)]
  transfers between devices with their start and end apart: 9 -> 9, of which waited for: 7 -> 9; matrix products, arithmetic and copies ran while one was open for 2% -> 2% of each run, Pallas kernels for 4% -> 5%
where the time goes in v5:
time: 146 us; the launch traced here: 145 us
  blocking collectives  67.2 us (46%)
  waiting for transfers between devices  24.1 us (17%)
  starting transfers between devices  20.8 us (14%)
  Pallas kernels  14.7 us (10%)
  between operations  13.6 us (9%)
  matrix products  2.65 us (2%)
    all_gather x1, blocking collectives, local(): mine = lax.all_gather(local_pair, 'z', axis=0, tiled=False)  47.2 us
    all_to_all x1, blocking collectives, local(): parts = lax.all_to_all(product, ('x', 'yhi'), 0, 0, tiled=True)  20 us
    ppermute x6, waiting for transfers between devices, swapped(): return lax.ppermute(value, axis, [(0, 1), (1, 0)])  15.5 us
    ppermute x6, starting transfers between devices, swapped(): return lax.ppermute(value, axis, [(0, 1), (1, 0)])  14.6 us
    ppermute x2, starting transfers between devices, placed(): return lax.ppermute(value, AXES, pairs)  6.17 us
    ppermute x2, waiting for transfers between devices, placed(): return lax.ppermute(value, AXES, pairs)  6.06 us
    pallas_call x1, Pallas kernels, project(): pl.pallas_call(project_kernel, in_specs=[vmem(), hbm, hbm], out_specs=hbm...  5.27 us
    pallas_call x1, Pallas kernels, attend(): pl.pallas_call(attend_kernel, in_specs=[smem(), vmem(), vmem(), vmem(), v...  5.21 us
  transfers between devices with their start and end apart: 9, of which 9 were waited for; matrix products, arithmetic and copies ran while one was open for 2% of the time, Pallas kernels for 5%

profile of v5, /device:TPU:6, one launch (start us, length us, event | category | flops | bytes accessed | tf_op | source)
XLA Modules:
  0.0 145.0 jit_solution(8645984590082084839)
XLA Ops:
  6.5 1.1 constant_dynamic-slice_fusion
  7.7 1.9 %collective-permute-start = (bf16[512,128]{1,0:T(8,128)(2,1)S(1)}, bf16[512,128]{1,0:T(8,128)(2,1)S(1)}, u32[]{:S(2)}, u32[]{:S(2)}) collective-permute-start(bf16[512,128]{1,0:T(8,128)(2,1)S(1)} %get-tuple-element.18), channel_id=1, source_target_pairs={{0,1},{1,0},{2,3},{3,2},{4,5},{5,4},{6,7},{7,6},{8,9},{9,8},{10,11... | collective-permute-start | bytes 393224 | tf_op jit(solution)/shard_map/ppermute | solution.py:31
  9.6 1.2 prepare.1.q_ref
  10.8 0.1 collective-permute-done
  10.9 0.7 pad_maximum_fusion
  11.6 0.0 all-gather.4.cloned.1.call-update
  11.7 3.5 %collective-permute-start.1 = (bf16[128,640]{1,0:T(8,128)(2,1)S(1)}, bf16[128,640]{1,0:T(8,128)(2,1)}, u32[]{:S(2)}, u32[]{:S(2)}) collective-permute-start(bf16[128,640]{1,0:T(8,128)(2,1)S(1)} %prepare.1.q_ref), channel_id=1, source_target_pairs={{0,256},{256,0},{1,257},{257,1},{2,258},{258,2},{3,259},{259,3},{4... | collective-permute-start | bytes 491528 | tf_op jit(solution)/shard_map/ppermute | solution.py:31
  15.2 2.7 %fusion.x_ref = f32[200,128]{1,0:T(8,128)S(1)} fusion(bf16[200,8192]{1,0:T(8,128)(2,1)S(1)} %copy-done, bf16[128,8192]{1,0:T(8,128)(2,1)} %bitcast.22), kind=kOutput, calls=%fused_computation.5 | convolution fusion | flops 419430400 | bytes 5476352 | tf_op jit(solution)/shard_map/dot_general | solution.py:308
  17.9 2.3 %collective-permute-done.1.far_ref = bf16[128,640]{1,0:T(8,128)(2,1)} collective-permute-done((bf16[128,640]{1,0:T(8,128)(2,1)S(1)}, bf16[128,640]{1,0:T(8,128)(2,1)}, u32[]{:S(2)}, u32[]{:S(2)}) %collective-permute-start.1) | collective-permute-done | bytes 163872 | tf_op jit(solution)/shard_map/ppermute | solution.py:31
  20.2 0.1 multiply_reduce_fusion
  20.3 1.9 %collective-permute-start.2 = (f32[200]{0:T(256)S(1)}, f32[200]{0:T(256)S(1)}, u32[]{:S(2)}, u32[]{:S(2)}) collective-permute-start(f32[200]{0:T(256)S(1)} %multiply_reduce_fusion), channel_id=1, source_target_pairs={{0,1},{1,0},{2,3},{3,2},{4,5},{5,4},{6,7},{7,6},{8,9},{9,8},{10,11... | collective-permute-start | bytes 2408 | tf_op jit(solution)/shard_map/ppermute | solution.py:31
  22.2 0.1 pad_add_fusion.place_ref
  22.3 1.0 collective-permute-done.2
  23.3 0.7 pack.1
  24.0 47.2 %all-gather = bf16[3200,128]{1,0:T(8,128)(2,1)S(1)} all-gather(bf16[200,128]{1,0:T(8,128)(2,1)S(1)} %pack.1), channel_id=2, replica_groups=mesh['ylo'=2,'z'=16,'x'=4,'yhi'=2,'core'=2] {'z'}, dimensions={0}, use_global_device_ids=true | all-gather | bytes 870400 | tf_op jit(solution)/shard_map/all_gather | solution.py:315
  71.2 1.9 %collective-permute-start.3 = (bf16[16,200,128]{2,1,0:T(8,128)(2,1)S(1)}, bf16[16,200,128]{2,1,0:T(8,128)(2,1)S(1)}, u32[]{:S(2)}, u32[]{:S(2)}) collective-permute-start(bf16[16,200,128]{2,1,0:T(8,128)(2,1)S(1)} %bitcast.16), channel_id=1, source_target_pairs={{0,1},{1,0},{2,3},{3,2},{4,5},{5,4},{6,7},{7,6},{8,9},{9,8},{10,11... | collective-permute-start | bytes 2457608 | tf_op jit(solution)/shard_map/ppermute | solution.py:31
  73.2 2.3 %collective-permute-done.3.theirs_ref = bf16[16,200,128]{2,1,0:T(8,128)(2,1)S(1)} collective-permute-done((bf16[16,200,128]{2,1,0:T(8,128)(2,1)S(1)}, bf16[16,200,128]{2,1,0:T(8,128)(2,1)S(1)}, u32[]{:S(2)}, u32[]{:S(2)}) %collective-permute-start.3) | collective-permute-done | bytes 819232 | tf_op jit(solution)/shard_map/ppermute | solution.py:31
  75.5 5.2 %attend.1.near_ref = bf16[2,128,640]{2,1,0:T(8,128)(2,1)S(1)} custom-call(s32[6]{0:T(128)S(1)} %pad_add_fusion.place_ref, bf16[128,640]{1,0:T(8,128)(2,1)S(1)} %prepare.1.q_ref, bf16[128,640]{1,0:T(8,128)(2,1)} %collective-permute-done.1.far_ref, bf16[16,200,128]{2,1,0:T(8,128)(2,1)S(1)} %bitcast.17, bf16[16,200,128]{2,1,0:T(8,128)(2,1)S(1)} %collective-permute-done.3.theirs_ref), custom_call_target="tpu_custom_call" | custom-call | tf_op jit(solution)/shard_map/attend/pallas_call | solution.py:161
  80.7 3.5 %collective-permute-start.4 = (bf16[2,128,640]{2,1,0:T(8,128)(2,1)S(1)}, bf16[2,128,640]{2,1,0:T(8,128)(2,1)S(1)}, u32[]{:S(2)}, u32[]{:S(2)}) collective-permute-start(bf16[2,128,640]{2,1,0:T(8,128)(2,1)S(1)} %attend.1.near_ref), channel_id=1, source_target_pairs={{0,256},{256,0},{1,257},{257,1},{2,258},{258,2},{3,259},{259,3},{4... | collective-permute-start | bytes 983048 | tf_op jit(solution)/shard_map/ppermute | solution.py:31
  84.1 8.2 %collective-permute-done.4.far_ref = bf16[2,128,640]{2,1,0:T(8,128)(2,1)S(1)} collective-permute-done((bf16[2,128,640]{2,1,0:T(8,128)(2,1)S(1)}, bf16[2,128,640]{2,1,0:T(8,128)(2,1)S(1)}, u32[]{:S(2)}, u32[]{:S(2)}) %collective-permute-start.4) | collective-permute-done | bytes 327712 | tf_op jit(solution)/shard_map/ppermute | solution.py:31
  92.3 0.4 combine.1.own_ref
  92.7 1.9 %collective-permute-start.5 = (bf16[256,512]{1,0:T(8,128)(2,1)S(1)}, bf16[256,512]{1,0:T(8,128)(2,1)}, u32[]{:S(2)}, u32[]{:S(2)}) collective-permute-start(bf16[256,512]{1,0:T(8,128)(2,1)S(1)} %combine.1.own_ref), channel_id=1, source_target_pairs={{0,1},{1,0},{2,3},{3,2},{4,5},{5,4},{6,7},{7,6},{8,9},{9,8},{10,11... | collective-permute-start | bytes 786440 | tf_op jit(solution)/shard_map/ppermute | solution.py:31
  94.7 1.6 %collective-permute-done.5.other_hbm = bf16[256,512]{1,0:T(8,128)(2,1)} collective-permute-done((bf16[256,512]{1,0:T(8,128)(2,1)S(1)}, bf16[256,512]{1,0:T(8,128)(2,1)}, u32[]{:S(2)}, u32[]{:S(2)}) %collective-permute-start.5) | collective-permute-done | bytes 262176 | tf_op jit(solution)/shard_map/ppermute | solution.py:31
  96.3 2.5 %all-gather.4.cloned.1.call-done = bf16[16384,128]{1,0:T(8,128)(2,1)} async-done(((bf16[1024,128]{1,0:T(8,128)(2,1)}), bf16[16384,128]{1,0:T(8,128)(2,1)}) %all-gather.4.cloned.1.call-update) | async-done | bytes 4194320 | tf_op jit(solution)/shard_map/all_gather | solution.py:305
  98.8 5.3 %project.1 = bf16[2,4,2,128,256]{4,3,2,1,0:T(8,128)(2,1)S(1)} custom-call(bf16[256,512]{1,0:T(8,128)(2,1)S(1)} %combine.1.own_ref, bf16[256,512]{1,0:T(8,128)(2,1)} %collective-permute-done.5.other_hbm, bf16[16,1024,128]{2,1,0:T(8,128)(2,1)} %bitcast.21), custom_call_target="tpu_custom_call" | custom-call | tf_op jit(solution)/shard_map/project/pallas_call | solution.py:226
  104.0 20.0 %all_to_all.5.x_ref = bf16[8,2,128,256]{3,2,1,0:T(8,128)(2,1)S(1)} all-to-all(bf16[8,2,128,256]{3,2,1,0:T(8,128)(2,1)S(1)} %bitcast.15), channel_id=1, replica_groups=mesh['ylo'=2,'z'=16,'x'=4,'yhi'=2,'core'=2] {'x','yhi'}, dimensions={0} | all-to-all | bytes 2097152 | tf_op jit(solution)/shard_map/all_to_all | solution.py:323
  124.0 0.7 reduce.1
  124.7 4.3 %collective-permute-start.6 = (bf16[128,256]{1,0:T(8,128)(2,1)S(1)}, bf16[128,256]{1,0:T(8,128)(2,1)S(1)}, u32[]{:S(2)}, u32[]{:S(2)}) collective-permute-start(bf16[128,256]{1,0:T(8,128)(2,1)S(1)} %get-tuple-element.15), channel_id=1, source_target_pairs={{0,0},{1,1},{2,2},{3,3},{4,4},{5,5},{6,6},{7,7},{8,256},{9,257},{1... | collective-permute-start | bytes 196616 | tf_op jit(solution)/shard_map/ppermute | solution.py:40
  129.0 1.9 %collective-permute-start.7 = (bf16[128,256]{1,0:T(8,128)(2,1)S(1)}, bf16[128,256]{1,0:T(8,128)(2,1)S(1)}, u32[]{:S(2)}, u32[]{:S(2)}) collective-permute-start(bf16[128,256]{1,0:T(8,128)(2,1)S(1)} %get-tuple-element.16), channel_id=1, source_target_pairs={{0,1},{1,0},{2,3},{3,2},{4,5},{5,4},{6,7},{7,6},{8,257},{9,256},{1... | collective-permute-start | bytes 196616 | tf_op jit(solution)/shard_map/ppermute | solution.py:40
  130.9 2.4 %collective-permute-done.6.same_ref = bf16[128,256]{1,0:T(8,128)(2,1)S(1)} collective-permute-done((bf16[128,256]{1,0:T(8,128)(2,1)S(1)}, bf16[128,256]{1,0:T(8,128)(2,1)S(1)}, u32[]{:S(2)}, u32[]{:S(2)}) %collective-permute-start.6) | collective-permute-done | bytes 65568 | tf_op jit(solution)/shard_map/ppermute | solution.py:40
  133.3 3.7 %collective-permute-done.7.cross_ref = bf16[128,256]{1,0:T(8,128)(2,1)S(1)} collective-permute-done((bf16[128,256]{1,0:T(8,128)(2,1)S(1)}, bf16[128,256]{1,0:T(8,128)(2,1)S(1)}, u32[]{:S(2)}, u32[]{:S(2)}) %collective-permute-start.7) | collective-permute-done | bytes 65568 | tf_op jit(solution)/shard_map/ppermute | solution.py:40
  136.9 1.2 assemble.1
  (7 shorter events, 0.0 us)
Async XLA Ops:
  6.5 8.7 %copy-start = (bf16[200,8192]{1,0:T(8,128)(2,1)S(1)}, bf16[200,8192]{1,0:T(8,128)(2,1)}, u32[]{:S(2)}) copy-start(bf16[200,8192]{1,0:T(8,128)(2,1)} %param.9) | copy-start | bytes 9830404
  6.5 92.2 %all-gather.4.cloned.1.call-start = ((), (), s32[]{:S(2)}) async-start(), calls=%async_computation.1 | async-start | bytes 4456448 | tf_op jit(solution)/shard_map/all_gather | solution.py:305
  7.7 3.2 %collective-permute-start = (bf16[512,128]{1,0:T(8,128)(2,1)S(1)}, bf16[512,128]{1,0:T(8,128)(2,1)S(1)}, u32[]{:S(2)}, u32[]{:S(2)}) collective-permute-start(bf16[512,128]{1,0:T(8,128)(2,1)S(1)} %get-tuple-element.18), channel_id=1, source_target_pairs={{0,1},{1,0},{2,3},{3,2},{4,5},{5,4},{6,7},{7,6},{8,9},{9,8},{10,11... | collective-permute-start | bytes 393224 | tf_op jit(solution)/shard_map/ppermute | solution.py:31
  11.7 10.5 %copy-start.2 = (s32[4]{0:T(128)S(1)}, s32[4]{0:T(128)}, u32[]{:S(2)}) copy-start(s32[4]{0:T(128)} %param.14) | copy-start | bytes 52
  11.7 11.6 %copy-start.1 = (f32[128]{0:T(128)S(1)}, f32[128]{0:T(128)}, u32[]{:S(2)}) copy-start(f32[128]{0:T(128)} %param.13) | copy-start | bytes 1540
  11.7 8.5 %collective-permute-start.1 = (bf16[128,640]{1,0:T(8,128)(2,1)S(1)}, bf16[128,640]{1,0:T(8,128)(2,1)}, u32[]{:S(2)}, u32[]{:S(2)}) collective-permute-start(bf16[128,640]{1,0:T(8,128)(2,1)S(1)} %prepare.1.q_ref), channel_id=1, source_target_pairs={{0,256},{256,0},{1,257},{257,1},{2,258},{258,2},{3,259},{259,3},{4... | collective-permute-start | bytes 491528 | tf_op jit(solution)/shard_map/ppermute | solution.py:31
  20.3 3.0 %collective-permute-start.2 = (f32[200]{0:T(256)S(1)}, f32[200]{0:T(256)S(1)}, u32[]{:S(2)}, u32[]{:S(2)}) collective-permute-start(f32[200]{0:T(256)S(1)} %multiply_reduce_fusion), channel_id=1, source_target_pairs={{0,1},{1,0},{2,3},{3,2},{4,5},{5,4},{6,7},{7,6},{8,9},{9,8},{10,11... | collective-permute-start | bytes 2408 | tf_op jit(solution)/shard_map/ppermute | solution.py:31
  71.2 4.2 %collective-permute-start.3 = (bf16[16,200,128]{2,1,0:T(8,128)(2,1)S(1)}, bf16[16,200,128]{2,1,0:T(8,128)(2,1)S(1)}, u32[]{:S(2)}, u32[]{:S(2)}) collective-permute-start(bf16[16,200,128]{2,1,0:T(8,128)(2,1)S(1)} %bitcast.16), channel_id=1, source_target_pairs={{0,1},{1,0},{2,3},{3,2},{4,5},{5,4},{6,7},{7,6},{8,9},{9,8},{10,11... | collective-permute-start | bytes 2457608 | tf_op jit(solution)/shard_map/ppermute | solution.py:31
  80.7 11.6 %collective-permute-start.4 = (bf16[2,128,640]{2,1,0:T(8,128)(2,1)S(1)}, bf16[2,128,640]{2,1,0:T(8,128)(2,1)S(1)}, u32[]{:S(2)}, u32[]{:S(2)}) collective-permute-start(bf16[2,128,640]{2,1,0:T(8,128)(2,1)S(1)} %attend.1.near_ref), channel_id=1, source_target_pairs={{0,256},{256,0},{1,257},{257,1},{2,258},{258,2},{3,259},{259,3},{4... | collective-permute-start | bytes 983048 | tf_op jit(solution)/shard_map/ppermute | solution.py:31
  92.7 3.6 %collective-permute-start.5 = (bf16[256,512]{1,0:T(8,128)(2,1)S(1)}, bf16[256,512]{1,0:T(8,128)(2,1)}, u32[]{:S(2)}, u32[]{:S(2)}) collective-permute-start(bf16[256,512]{1,0:T(8,128)(2,1)S(1)} %combine.1.own_ref), channel_id=1, source_target_pairs={{0,1},{1,0},{2,3},{3,2},{4,5},{5,4},{6,7},{7,6},{8,9},{9,8},{10,11... | collective-permute-start | bytes 786440 | tf_op jit(solution)/shard_map/ppermute | solution.py:31
  124.7 8.6 %collective-permute-start.6 = (bf16[128,256]{1,0:T(8,128)(2,1)S(1)}, bf16[128,256]{1,0:T(8,128)(2,1)S(1)}, u32[]{:S(2)}, u32[]{:S(2)}) collective-permute-start(bf16[128,256]{1,0:T(8,128)(2,1)S(1)} %get-tuple-element.15), channel_id=1, source_target_pairs={{0,0},{1,1},{2,2},{3,3},{4,4},{5,5},{6,6},{7,7},{8,256},{9,257},{1... | collective-permute-start | bytes 196616 | tf_op jit(solution)/shard_map/ppermute | solution.py:40
  129.0 8.0 %collective-permute-start.7 = (bf16[128,256]{1,0:T(8,128)(2,1)S(1)}, bf16[128,256]{1,0:T(8,128)(2,1)S(1)}, u32[]{:S(2)}, u32[]{:S(2)}) collective-permute-start(bf16[128,256]{1,0:T(8,128)(2,1)S(1)} %get-tuple-element.16), channel_id=1, source_target_pairs={{0,1},{1,0},{2,3},{3,2},{4,5},{5,4},{6,7},{7,6},{8,257},{9,256},{1... | collective-permute-start | bytes 196616 | tf_op jit(solution)/shard_map/ppermute | solution.py:40
Sparse Core Ops, SparseCore 0:
  11.8 86.9 all-gather.3

commit v6 on v5

--- a/solution.py
+++ b/solution.py
@@ -31,11 +31,11 @@
     return lax.ppermute(value, axis, [(0, 1), (1, 0)])
 
 
-def placed(value, flip):
+def placed(value):
     pairs = []
     for source in range(512):
         core, yhi, x, z = source % 2, source // 2 % 2, source // 4 % 4, source // 16 % 16
-        target = flat(x // 2, z, 2 * (source // 256) + x % 2, yhi, core ^ flip)
+        target = flat(x // 2, z, 2 * (source // 256) + x % 2, yhi, core)
         pairs.append((source, target))
     return lax.ppermute(value, AXES, pairs)
 
@@ -244,48 +244,25 @@
     )
 
 
-def reduce_kernel(place_ref, x_ref, same_ref, cross_ref):
-    sums = []
+def reduce_kernel(x_ref, o_ref):
     for core in range(2):
-        total = x_ref[0, core].astype(F32)
+        total = x_ref[core].astype(F32)
         for source in range(1, 8):
-            total = total + x_ref[source, core].astype(F32)
-        sums.append(total)
-    first = place_ref[0] == 0
-    same_ref[...] = jnp.where(first, sums[0], sums[1]).astype(BF)
-    cross_ref[...] = jnp.where(first, sums[1], sums[0]).astype(BF)
-
-
-def reduce(place, parts):
+            total = total + x_ref[2 * source + core].astype(F32)
+        total = total.astype(BF)
+        o_ref[:, core * HD : (core + 1) * HD] = total[:, :HD]
+        o_ref[:, (2 + core) * HD : (3 + core) * HD] = total[:, HD:]
+
+
+def reduce(parts):
     return pl.pallas_call(
         reduce_kernel,
-        in_specs=[smem(), vmem()],
-        out_specs=[vmem(), vmem()],
-        out_shape=[jax.ShapeDtypeStruct((ROWS, 2 * HD), BF)] * 2,
+        in_specs=[vmem()],
+        out_specs=vmem(),
+        out_shape=jax.ShapeDtypeStruct((ROWS, WIDTH), BF),
         compiler_params=params(4),
         name="reduce",
-    )(place, parts)
-
-
-def assemble_kernel(place_ref, same_ref, cross_ref, o_ref):
-    first = place_ref[0] == 0
-    same, cross = same_ref[...].astype(F32), cross_ref[...].astype(F32)
-    even = jnp.where(first, same, cross).astype(BF)
-    odd = jnp.where(first, cross, same).astype(BF)
-    o_ref[:, 0:HD] = even[:, :HD]
-    o_ref[:, HD : 2 * HD] = odd[:, :HD]
-    o_ref[:, 2 * HD : 3 * HD] = even[:, HD:]
-    o_ref[:, 3 * HD :] = odd[:, HD:]
-
-
-def assemble(place, same, cross):
-    return pl.pallas_call(
-        assemble_kernel,
-        in_specs=[smem(), vmem(), vmem()],
-        out_shape=jax.ShapeDtypeStruct((ROWS, WIDTH), BF),
-        compiler_params=params(4),
-        name="assemble",
-    )(place, same, cross)
+    )(parts)
 
 
 def local(queries, vision, kv_weight, out_weight, q_gain, k_gain, tile_counts, spans):
@@ -319,10 +296,9 @@
     own = combine(partial, swapped(partial, "ylo"))
     other = swapped(own, "core")
 
-    product = project(own, other, weight).reshape(8, 2, ROWS, 2 * HD)
-    parts = lax.all_to_all(product, ("x", "yhi"), 0, 0, tiled=True)
-    same, cross = reduce(place, parts)
-    return assemble(place, placed(same, 0), placed(cross, 1))
+    product = project(own, other, weight).reshape(16, ROWS, 2 * HD)
+    parts = lax.all_to_all(product, ("x", "yhi", "core"), 0, 0, tiled=True)
+    return placed(reduce(parts))
 
 
 def solution(mesh):

time: 146 us -> 145 us (level)
  starting transfers between devices: 20.8 us -> 17.7 us
  blocking collectives: 67.2 us -> 70.1 us
  Pallas kernels: 14.7 us -> 12.9 us
    ppermute x2 -> x1, starting transfers between devices: 6.17 us -> 3.02 us  [placed(): return lax.ppermute(value, AXES, pairs)]
    all_to_all x1, blocking collectives: 20 us -> 22.8 us  [local(): parts = lax.all_to_all(product, ('x', 'yhi', 'core'), 0, 0, tiled=True)]
    pallas_call x2 -> x1, Pallas kernels: 1.91 us -> 0.14 us  [reduce(): pl.pallas_call(reduce_kernel, in_specs=[vmem()], out_specs=vmem(), out_sh...]
    ppermute x2 -> x1, waiting for transfers between devices: 6.06 us -> 6.24 us  [placed(): return lax.ppermute(value, AXES, pairs)]
  transfers between devices with their start and end apart: 9 -> 8, of which waited for: 9 -> 8; matrix products, arithmetic and copies ran while one was open for 2% -> 2% of each run, Pallas kernels for 5% -> 5%
where the time goes in v6:
time: 145 us; the launch traced here: 144 us
  blocking collectives  70.1 us (48%)
  waiting for transfers between devices  24.3 us (17%)
  starting transfers between devices  17.7 us (12%)
  between operations  13.5 us (9%)
  Pallas kernels  12.9 us (9%)
  matrix products  2.65 us (2%)
  local copies, waits for them, and re-layouts  1.81 us (1%)
    all_gather x1, blocking collectives, local(): mine = lax.all_gather(local_pair, 'z', axis=0, tiled=False)  47.2 us
    all_to_all x1, blocking collectives, local(): parts = lax.all_to_all(product, ('x', 'yhi', 'core'), 0, 0, tiled=True)  22.8 us
    ppermute x6, waiting for transfers between devices, swapped(): return lax.ppermute(value, axis, [(0, 1), (1, 0)])  15.5 us
    ppermute x6, starting transfers between devices, swapped(): return lax.ppermute(value, axis, [(0, 1), (1, 0)])  14.7 us
    ppermute x1, waiting for transfers between devices, placed(): return lax.ppermute(value, AXES, pairs)  6.24 us
    pallas_call x1, Pallas kernels, project(): pl.pallas_call(project_kernel, in_specs=[vmem(), hbm, hbm], out_specs=hbm...  5.27 us
    pallas_call x1, Pallas kernels, attend(): pl.pallas_call(attend_kernel, in_specs=[smem(), vmem(), vmem(), vmem(), v...  5.19 us
    ppermute x1, starting transfers between devices, placed(): return lax.ppermute(value, AXES, pairs)  3.02 us
  transfers between devices with their start and end apart: 8, of which 8 were waited for; matrix products, arithmetic and copies ran while one was open for 2% of the time, Pallas kernels for 5%

profile of v6, /device:TPU:6, one launch (start us, length us, event | category | flops | bytes accessed | tf_op | source)
XLA Modules:
  0.0 143.8 jit_solution(985804928686501541)
XLA Ops:
  6.5 1.1 constant_dynamic-slice_fusion
  7.7 1.9 %collective-permute-start = (bf16[512,128]{1,0:T(8,128)(2,1)S(1)}, bf16[512,128]{1,0:T(8,128)(2,1)S(1)}, u32[]{:S(2)}, u32[]{:S(2)}) collective-permute-start(bf16[512,128]{1,0:T(8,128)(2,1)S(1)} %get-tuple-element.14), channel_id=1, source_target_pairs={{0,1},{1,0},{2,3},{3,2},{4,5},{5,4},{6,7},{7,6},{8,9},{9,8},{10,11... | collective-permute-start | bytes 393224 | tf_op jit(solution)/shard_map/ppermute | solution.py:31
  9.6 1.2 prepare.1.q_ref
  10.8 0.1 collective-permute-done
  10.9 0.7 pad_maximum_fusion
  11.6 0.0 all-gather.4.cloned.1.call-update
  11.7 0.0 copy-start.2
  11.7 0.0 copy-start.1
  11.7 3.5 %collective-permute-start.1 = (bf16[128,640]{1,0:T(8,128)(2,1)S(1)}, bf16[128,640]{1,0:T(8,128)(2,1)}, u32[]{:S(2)}, u32[]{:S(2)}) collective-permute-start(bf16[128,640]{1,0:T(8,128)(2,1)S(1)} %prepare.1.q_ref), channel_id=1, source_target_pairs={{0,256},{256,0},{1,257},{257,1},{2,258},{258,2},{3,259},{259,3},{4... | collective-permute-start | bytes 491528 | tf_op jit(solution)/shard_map/ppermute | solution.py:31
  15.2 2.7 %fusion.x_ref = f32[200,128]{1,0:T(8,128)S(1)} fusion(bf16[200,8192]{1,0:T(8,128)(2,1)S(1)} %copy-done, bf16[128,8192]{1,0:T(8,128)(2,1)} %bitcast.22), kind=kOutput, calls=%fused_computation.5 | convolution fusion | flops 419430400 | bytes 5476352 | tf_op jit(solution)/shard_map/dot_general | solution.py:285
  17.9 2.3 %collective-permute-done.1.far_ref = bf16[128,640]{1,0:T(8,128)(2,1)} collective-permute-done((bf16[128,640]{1,0:T(8,128)(2,1)S(1)}, bf16[128,640]{1,0:T(8,128)(2,1)}, u32[]{:S(2)}, u32[]{:S(2)}) %collective-permute-start.1) | collective-permute-done | bytes 163872 | tf_op jit(solution)/shard_map/ppermute | solution.py:31
  20.2 0.1 multiply_reduce_fusion
  20.3 1.9 %collective-permute-start.2 = (f32[200]{0:T(256)S(1)}, f32[200]{0:T(256)S(1)}, u32[]{:S(2)}, u32[]{:S(2)}) collective-permute-start(f32[200]{0:T(256)S(1)} %multiply_reduce_fusion), channel_id=1, source_target_pairs={{0,1},{1,0},{2,3},{3,2},{4,5},{5,4},{6,7},{7,6},{8,9},{9,8},{10,11... | collective-permute-start | bytes 2408 | tf_op jit(solution)/shard_map/ppermute | solution.py:31
  22.2 0.1 pad_add_fusion.place_ref
  22.3 1.0 collective-permute-done.2
  23.3 0.7 pack.1
  24.0 47.2 %all-gather = bf16[3200,128]{1,0:T(8,128)(2,1)S(1)} all-gather(bf16[200,128]{1,0:T(8,128)(2,1)S(1)} %pack.1), channel_id=2, replica_groups=mesh['ylo'=2,'z'=16,'x'=4,'yhi'=2,'core'=2] {'z'}, dimensions={0}, use_global_device_ids=true | all-gather | bytes 870400 | tf_op jit(solution)/shard_map/all_gather | solution.py:292
  71.2 1.9 %collective-permute-start.3 = (bf16[16,200,128]{2,1,0:T(8,128)(2,1)S(1)}, bf16[16,200,128]{2,1,0:T(8,128)(2,1)S(1)}, u32[]{:S(2)}, u32[]{:S(2)}) collective-permute-start(bf16[16,200,128]{2,1,0:T(8,128)(2,1)S(1)} %bitcast.16), channel_id=1, source_target_pairs={{0,1},{1,0},{2,3},{3,2},{4,5},{5,4},{6,7},{7,6},{8,9},{9,8},{10,11... | collective-permute-start | bytes 2457608 | tf_op jit(solution)/shard_map/ppermute | solution.py:31
  73.2 2.3 %collective-permute-done.3.theirs_ref = bf16[16,200,128]{2,1,0:T(8,128)(2,1)S(1)} collective-permute-done((bf16[16,200,128]{2,1,0:T(8,128)(2,1)S(1)}, bf16[16,200,128]{2,1,0:T(8,128)(2,1)S(1)}, u32[]{:S(2)}, u32[]{:S(2)}) %collective-permute-start.3) | collective-permute-done | bytes 819232 | tf_op jit(solution)/shard_map/ppermute | solution.py:31
  75.5 5.2 %attend.1.near_ref = bf16[2,128,640]{2,1,0:T(8,128)(2,1)S(1)} custom-call(s32[6]{0:T(128)S(1)} %pad_add_fusion.place_ref, bf16[128,640]{1,0:T(8,128)(2,1)S(1)} %prepare.1.q_ref, bf16[128,640]{1,0:T(8,128)(2,1)} %collective-permute-done.1.far_ref, bf16[16,200,128]{2,1,0:T(8,128)(2,1)S(1)} %bitcast.17, bf16[16,200,128]{2,1,0:T(8,128)(2,1)S(1)} %collective-permute-done.3.theirs_ref), custom_call_target="tpu_custom_call" | custom-call | tf_op jit(solution)/shard_map/attend/pallas_call | solution.py:161
  80.7 3.5 %collective-permute-start.4 = (bf16[2,128,640]{2,1,0:T(8,128)(2,1)S(1)}, bf16[2,128,640]{2,1,0:T(8,128)(2,1)S(1)}, u32[]{:S(2)}, u32[]{:S(2)}) collective-permute-start(bf16[2,128,640]{2,1,0:T(8,128)(2,1)S(1)} %attend.1.near_ref), channel_id=1, source_target_pairs={{0,256},{256,0},{1,257},{257,1},{2,258},{258,2},{3,259},{259,3},{4... | collective-permute-start | bytes 983048 | tf_op jit(solution)/shard_map/ppermute | solution.py:31
  84.2 8.1 %collective-permute-done.4.far_ref = bf16[2,128,640]{2,1,0:T(8,128)(2,1)S(1)} collective-permute-done((bf16[2,128,640]{2,1,0:T(8,128)(2,1)S(1)}, bf16[2,128,640]{2,1,0:T(8,128)(2,1)S(1)}, u32[]{:S(2)}, u32[]{:S(2)}) %collective-permute-start.4) | collective-permute-done | bytes 327712 | tf_op jit(solution)/shard_map/ppermute | solution.py:31
  92.3 0.4 combine.1.own_ref
  92.7 1.9 %collective-permute-start.5 = (bf16[256,512]{1,0:T(8,128)(2,1)S(1)}, bf16[256,512]{1,0:T(8,128)(2,1)}, u32[]{:S(2)}, u32[]{:S(2)}) collective-permute-start(bf16[256,512]{1,0:T(8,128)(2,1)S(1)} %combine.1.own_ref), channel_id=1, source_target_pairs={{0,1},{1,0},{2,3},{3,2},{4,5},{5,4},{6,7},{7,6},{8,9},{9,8},{10,11... | collective-permute-start | bytes 786440 | tf_op jit(solution)/shard_map/ppermute | solution.py:31
  94.6 1.6 %collective-permute-done.5.other_hbm = bf16[256,512]{1,0:T(8,128)(2,1)} collective-permute-done((bf16[256,512]{1,0:T(8,128)(2,1)S(1)}, bf16[256,512]{1,0:T(8,128)(2,1)}, u32[]{:S(2)}, u32[]{:S(2)}) %collective-permute-start.5) | collective-permute-done | bytes 262176 | tf_op jit(solution)/shard_map/ppermute | solution.py:31
  96.3 2.5 %all-gather.4.cloned.1.call-done = bf16[16384,128]{1,0:T(8,128)(2,1)} async-done(((bf16[1024,128]{1,0:T(8,128)(2,1)}), bf16[16384,128]{1,0:T(8,128)(2,1)}) %all-gather.4.cloned.1.call-update) | async-done | bytes 4194320 | tf_op jit(solution)/shard_map/all_gather | solution.py:282
  98.8 5.3 %project.1 = bf16[2,4,2,128,256]{4,3,2,1,0:T(8,128)(2,1)S(1)} custom-call(bf16[256,512]{1,0:T(8,128)(2,1)S(1)} %combine.1.own_ref, bf16[256,512]{1,0:T(8,128)(2,1)} %collective-permute-done.5.other_hbm, bf16[16,1024,128]{2,1,0:T(8,128)(2,1)} %bitcast.21), custom_call_target="tpu_custom_call" | custom-call | tf_op jit(solution)/shard_map/project/pallas_call | solution.py:226
  104.0 22.8 %all_to_all.5.x_ref = bf16[16,128,256]{2,1,0:T(8,128)(2,1)S(1)} all-to-all(bf16[16,128,256]{2,1,0:T(8,128)(2,1)S(1)} %bitcast.15), channel_id=1, replica_groups=mesh['ylo'=2,'z'=16,'x'=4,'yhi'=2,'core'=2] {'x','yhi','core'}, dimensions={0} | all-to-all | bytes 2097152 | tf_op jit(solution)/shard_map/all_to_all | solution.py:300
  126.9 0.1 reduce.1
  127.0 3.0 %collective-permute-start.6 = (bf16[128,512]{1,0:T(8,128)(2,1)S(1)}, bf16[128,512]{1,0:T(8,128)(2,1)S(1)}, u32[]{:S(2)}, u32[]{:S(2)}) collective-permute-start(bf16[128,512]{1,0:T(8,128)(2,1)S(1)} %reduce.1), channel_id=1, source_target_pairs={{0,0},{1,1},{2,2},{3,3},{4,4},{5,5},{6,6},{7,7},{8,256},{9,257},{1... | collective-permute-start | bytes 393224 | tf_op jit(solution)/shard_map/ppermute | solution.py:40
  130.0 6.2 %collective-permute-done.6 = bf16[128,512]{1,0:T(8,128)(2,1)S(1)} collective-permute-done((bf16[128,512]{1,0:T(8,128)(2,1)S(1)}, bf16[128,512]{1,0:T(8,128)(2,1)S(1)}, u32[]{:S(2)}, u32[]{:S(2)}) %collective-permute-start.6) | collective-permute-done | bytes 131104 | tf_op jit(solution)/shard_map/ppermute | solution.py:40
  136.3 0.7 copy.10
  (5 shorter events, 0.0 us)
Async XLA Ops:
  6.5 8.7 %copy-start = (bf16[200,8192]{1,0:T(8,128)(2,1)S(1)}, bf16[200,8192]{1,0:T(8,128)(2,1)}, u32[]{:S(2)}) copy-start(bf16[200,8192]{1,0:T(8,128)(2,1)} %param.9) | copy-start | bytes 9830404
  6.5 92.2 %all-gather.4.cloned.1.call-start = ((), (), s32[]{:S(2)}) async-start(), calls=%async_computation.1 | async-start | bytes 4456448 | tf_op jit(solution)/shard_map/all_gather | solution.py:282
  7.7 3.2 %collective-permute-start = (bf16[512,128]{1,0:T(8,128)(2,1)S(1)}, bf16[512,128]{1,0:T(8,128)(2,1)S(1)}, u32[]{:S(2)}, u32[]{:S(2)}) collective-permute-start(bf16[512,128]{1,0:T(8,128)(2,1)S(1)} %get-tuple-element.14), channel_id=1, source_target_pairs={{0,1},{1,0},{2,3},{3,2},{4,5},{5,4},{6,7},{7,6},{8,9},{9,8},{10,11... | collective-permute-start | bytes 393224 | tf_op jit(solution)/shard_map/ppermute | solution.py:31
  11.7 10.5 %copy-start.2 = (s32[4]{0:T(128)S(1)}, s32[4]{0:T(128)}, u32[]{:S(2)}) copy-start(s32[4]{0:T(128)} %param.14) | copy-start | bytes 52
  11.7 11.6 %copy-start.1 = (f32[128]{0:T(128)S(1)}, f32[128]{0:T(128)}, u32[]{:S(2)}) copy-start(f32[128]{0:T(128)} %param.13) | copy-start | bytes 1540
  11.7 8.5 %collective-permute-start.1 = (bf16[128,640]{1,0:T(8,128)(2,1)S(1)}, bf16[128,640]{1,0:T(8,128)(2,1)}, u32[]{:S(2)}, u32[]{:S(2)}) collective-permute-start(bf16[128,640]{1,0:T(8,128)(2,1)S(1)} %prepare.1.q_ref), channel_id=1, source_target_pairs={{0,256},{256,0},{1,257},{257,1},{2,258},{258,2},{3,259},{259,3},{4... | collective-permute-start | bytes 491528 | tf_op jit(solution)/shard_map/ppermute | solution.py:31
  20.3 3.0 %collective-permute-start.2 = (f32[200]{0:T(256)S(1)}, f32[200]{0:T(256)S(1)}, u32[]{:S(2)}, u32[]{:S(2)}) collective-permute-start(f32[200]{0:T(256)S(1)} %multiply_reduce_fusion), channel_id=1, source_target_pairs={{0,1},{1,0},{2,3},{3,2},{4,5},{5,4},{6,7},{7,6},{8,9},{9,8},{10,11... | collective-permute-start | bytes 2408 | tf_op jit(solution)/shard_map/ppermute | solution.py:31
  71.2 4.2 %collective-permute-start.3 = (bf16[16,200,128]{2,1,0:T(8,128)(2,1)S(1)}, bf16[16,200,128]{2,1,0:T(8,128)(2,1)S(1)}, u32[]{:S(2)}, u32[]{:S(2)}) collective-permute-start(bf16[16,200,128]{2,1,0:T(8,128)(2,1)S(1)} %bitcast.16), channel_id=1, source_target_pairs={{0,1},{1,0},{2,3},{3,2},{4,5},{5,4},{6,7},{7,6},{8,9},{9,8},{10,11... | collective-permute-start | bytes 2457608 | tf_op jit(solution)/shard_map/ppermute | solution.py:31
  80.7 11.6 %collective-permute-start.4 = (bf16[2,128,640]{2,1,0:T(8,128)(2,1)S(1)}, bf16[2,128,640]{2,1,0:T(8,128)(2,1)S(1)}, u32[]{:S(2)}, u32[]{:S(2)}) collective-permute-start(bf16[2,128,640]{2,1,0:T(8,128)(2,1)S(1)} %attend.1.near_ref), channel_id=1, source_target_pairs={{0,256},{256,0},{1,257},{257,1},{2,258},{258,2},{3,259},{259,3},{4... | collective-permute-start | bytes 983048 | tf_op jit(solution)/shard_map/ppermute | solution.py:31
  92.7 3.6 %collective-permute-start.5 = (bf16[256,512]{1,0:T(8,128)(2,1)S(1)}, bf16[256,512]{1,0:T(8,128)(2,1)}, u32[]{:S(2)}, u32[]{:S(2)}) collective-permute-start(bf16[256,512]{1,0:T(8,128)(2,1)S(1)} %combine.1.own_ref), channel_id=1, source_target_pairs={{0,1},{1,0},{2,3},{3,2},{4,5},{5,4},{6,7},{7,6},{8,9},{9,8},{10,11... | collective-permute-start | bytes 786440 | tf_op jit(solution)/shard_map/ppermute | solution.py:31
  127.0 9.3 %collective-permute-start.6 = (bf16[128,512]{1,0:T(8,128)(2,1)S(1)}, bf16[128,512]{1,0:T(8,128)(2,1)S(1)}, u32[]{:S(2)}, u32[]{:S(2)}) collective-permute-start(bf16[128,512]{1,0:T(8,128)(2,1)S(1)} %reduce.1), channel_id=1, source_target_pairs={{0,0},{1,1},{2,2},{3,3},{4,4},{5,5},{6,6},{7,7},{8,256},{9,257},{1... | collective-permute-start | bytes 393224 | tf_op jit(solution)/shard_map/ppermute | solution.py:40
Sparse Core Ops, SparseCore 0:
  11.8 86.9 all-gather.3

commit v7 on v6

--- a/solution.py
+++ b/solution.py
@@ -11,8 +11,8 @@
 TILES = 4
 EPSILON = 1e-05
 NEG = -1e30
-AXES = ("ylo", "z", "x", "yhi", "core")
-SIZES = (2, 16, 4, 2, 2)
+AXES = ("ylo", "z", "xh", "xl", "yhi", "core")
+SIZES = (2, 16, 2, 2, 2, 2)
 ROWS = 128
 HEADS = 4
 WIDTH = HEADS * HD
@@ -191,67 +191,15 @@
     )(near, far)
 
 
-def project_kernel(own_ref, other_hbm, w_hbm, o_hbm, a_s, w_s, o_s, in_sem, out_sem):
-    steps = BLOCKS // 2
-    other = pltpu.make_async_copy(other_hbm, a_s, in_sem.at[steps])
-    other.start()
-    fetch = [
-        pltpu.make_async_copy(
-            w_hbm.at[pl.ds(2 * step, 2)], w_s.at[pl.ds(2 * step, 2)], in_sem.at[step]
-        )
-        for step in range(steps)
-    ]
-    for copy in fetch:
-        copy.start()
-    other.wait()
-    attended = jnp.concatenate([own_ref[...], a_s[...]], axis=1)
-    drain = []
-    for step in range(steps):
-        fetch[step].wait()
-        weight = jnp.concatenate([w_s[2 * step], w_s[2 * step + 1]], axis=1)
-        result = jnp.dot(attended, weight, preferred_element_type=F32).astype(BF)
-        o_s[step, 0] = result[:ROWS]
-        o_s[step, 1] = result[ROWS:]
-        copy = pltpu.make_async_copy(
-            o_s.at[step], o_hbm.at[:, step // 2, step % 2], out_sem.at[step]
-        )
-        copy.start()
-        drain.append(copy)
-    for copy in drain:
-        copy.wait()
-
-
-def project(own, other, weight):
-    hbm = pl.BlockSpec(memory_space=pltpu.HBM)
-    return pl.pallas_call(
-        project_kernel,
-        in_specs=[vmem(), hbm, hbm],
-        out_specs=hbm,
-        out_shape=jax.ShapeDtypeStruct((2, 4, 2, ROWS, 2 * HD), BF),
-        scratch_shapes=[
-            pltpu.VMEM((2 * ROWS, WIDTH), BF),
-            pltpu.VMEM((BLOCKS, 2 * WIDTH, HD), BF),
-            pltpu.VMEM((8, 2, ROWS, 2 * HD), BF),
-            pltpu.SemaphoreType.DMA((9,)),
-            pltpu.SemaphoreType.DMA((8,)),
-        ],
-        compiler_params=params(12),
-        name="project",
-    )(
-        own,
-        pltpu.with_memory_space_constraint(other, pltpu.HBM),
-        pltpu.with_memory_space_constraint(weight, pltpu.HBM),
-    )
-
-
 def reduce_kernel(x_ref, o_ref):
     for core in range(2):
-        total = x_ref[core].astype(F32)
-        for source in range(1, 8):
-            total = total + x_ref[2 * source + core].astype(F32)
-        total = total.astype(BF)
-        o_ref[:, core * HD : (core + 1) * HD] = total[:, :HD]
-        o_ref[:, (2 + core) * HD : (3 + core) * HD] = total[:, HD:]
+        for side in range(2):
+            total = jnp.zeros((HD, ROWS), F32)
+            for source in range(16):
+                if source // 2 % 2 == core:
+                    total = total + x_ref[source, side].astype(F32)
+            begin = (2 * side + core) * HD
+            o_ref[:, begin : begin + HD] = total.T.astype(BF)
 
 
 def reduce(parts):
@@ -296,14 +244,17 @@
     own = combine(partial, swapped(partial, "ylo"))
     other = swapped(own, "core")
 
-    product = project(own, other, weight).reshape(16, ROWS, 2 * HD)
-    parts = lax.all_to_all(product, ("x", "yhi", "core"), 0, 0, tiled=True)
+    attended = jnp.concatenate([own, other], axis=1).reshape(2, ROWS, 2 * WIDTH)
+    split = weight.reshape(8, 2, 2 * WIDTH, HD)
+    product = jnp.einsum("rmk,jtkn->jrtnm", attended, split, preferred_element_type=F32)
+    product = product.astype(BF).reshape(16, 2, HD, ROWS)
+    parts = lax.all_to_all(product, ("xl", "yhi", "core", "xh"), 0, 0, tiled=True)
     return placed(reduce(parts))
 
 
 def solution(mesh):
     split = Mesh(mesh.devices.reshape(SIZES), AXES)
-    seq, head = ("ylo", "z"), ("x", "yhi", "core")
+    seq, head = ("ylo", "z"), ("xh", "xl", "yhi", "core")
     return jax.shard_map(
         local,
         mesh=split,

time: 145 us -> 144 us (level)
  Pallas kernels: 12.9 us -> 7.68 us
  matrix products: 2.65 us -> 6.26 us
    pallas_call x1 -> x0, Pallas kernels: 5.27 us -> none  [project(): pl.pallas_call(project_kernel, in_specs=[vmem(), hbm, hbm], out_specs=hbm...]
    dot_general x0 -> x1, matrix products: none -> 3.6 us  [local(): jnp.einsum('rmk,jtkn->jrtnm', attended, split, preferred_element_type=F32)]
  transfers between devices with their start and end apart: 8 -> 8, of which waited for: 8 -> 8; matrix products, arithmetic and copies ran while one was open for 2% -> 3% of each run, Pallas kernels for 5% -> 5%
where the time goes in v7:
time: 144 us; the launch traced here: 143 us
  blocking collectives  70.3 us (49%)
  waiting for transfers between devices  23.9 us (17%)
  starting transfers between devices  17.8 us (12%)
  between operations  13.6 us (9%)
  Pallas kernels  7.68 us (5%)
  matrix products  6.26 us (4%)
  local copies, waits for them, and re-layouts  1.88 us (1%)
  other arithmetic  1.77 us (1%)
    all_gather x1, blocking collectives, local(): mine = lax.all_gather(local_pair, 'z', axis=0, tiled=False)  47.2 us
    all_to_all x1, blocking collectives, local(): lax.all_to_all(product, ('xl', 'yhi', 'core', 'xh'), 0, 0, tiled=True)  23.1 us
    ppermute x6, waiting for transfers between devices, swapped(): return lax.ppermute(value, axis, [(0, 1), (1, 0)])  15.4 us
    ppermute x6, starting transfers between devices, swapped(): return lax.ppermute(value, axis, [(0, 1), (1, 0)])  14.7 us
    ppermute x1, waiting for transfers between devices, placed(): return lax.ppermute(value, AXES, pairs)  6.73 us
    pallas_call x1, Pallas kernels, attend(): pl.pallas_call(attend_kernel, in_specs=[smem(), vmem(), vmem(), vmem(), v...  5.19 us
    dot_general x1, matrix products, local(): jnp.einsum('rmk,jtkn->jrtnm', attended, split, preferred_element_type=F32)  3.6 us
    ppermute x1, starting transfers between devices, placed(): return lax.ppermute(value, AXES, pairs)  3.14 us
  transfers between devices with their start and end apart: 8, of which 8 were waited for; matrix products, arithmetic and copies ran while one was open for 3% of the time, Pallas kernels for 5%

profile of v7, /device:TPU:6, one launch (start us, length us, event | category | flops | bytes accessed | tf_op | source)
XLA Modules:
  0.0 143.2 jit_solution(12709259509831657268)
XLA Ops:
  6.5 1.1 constant_dynamic-slice_fusion.1
  7.7 1.9 %collective-permute-start = (bf16[512,128]{1,0:T(8,128)(2,1)S(1)}, bf16[512,128]{1,0:T(8,128)(2,1)S(1)}, u32[]{:S(2)}, u32[]{:S(2)}) collective-permute-start(bf16[512,128]{1,0:T(8,128)(2,1)S(1)} %get-tuple-element.14), channel_id=1, source_target_pairs={{0,1},{1,0},{2,3},{3,2},{4,5},{5,4},{6,7},{7,6},{8,9},{9,8},{10,11... | collective-permute-start | bytes 393224 | tf_op jit(solution)/shard_map/ppermute | solution.py:31
  9.6 1.2 prepare.1.q_ref
  10.8 0.1 collective-permute-done
  10.9 0.7 pad_maximum_fusion.1
  11.6 0.0 all-gather.4.cloned.1.call-update
  11.7 3.5 %collective-permute-start.1 = (bf16[128,640]{1,0:T(8,128)(2,1)S(1)}, bf16[128,640]{1,0:T(8,128)(2,1)}, u32[]{:S(2)}, u32[]{:S(2)}) collective-permute-start(bf16[128,640]{1,0:T(8,128)(2,1)S(1)} %prepare.1.q_ref), channel_id=1, source_target_pairs={{0,256},{256,0},{1,257},{257,1},{2,258},{258,2},{3,259},{259,3},{4... | collective-permute-start | bytes 491528 | tf_op jit(solution)/shard_map/ppermute | solution.py:31
  15.2 2.7 %fusion.1.x_ref = f32[200,128]{1,0:T(8,128)S(1)} fusion(bf16[200,8192]{1,0:T(8,128)(2,1)S(1)} %copy-done, bf16[128,8192]{1,0:T(8,128)(2,1)} %bitcast.34), kind=kOutput, calls=%fused_computation.8 | convolution fusion | flops 419430400 | bytes 5476352 | tf_op jit(solution)/shard_map/dot_general | solution.py:233
  17.9 2.3 %collective-permute-done.1.far_ref = bf16[128,640]{1,0:T(8,128)(2,1)} collective-permute-done((bf16[128,640]{1,0:T(8,128)(2,1)S(1)}, bf16[128,640]{1,0:T(8,128)(2,1)}, u32[]{:S(2)}, u32[]{:S(2)}) %collective-permute-start.1) | collective-permute-done | bytes 163872 | tf_op jit(solution)/shard_map/ppermute | solution.py:31
  20.2 0.1 multiply_reduce_fusion
  20.3 1.9 %collective-permute-start.2 = (f32[200]{0:T(256)S(1)}, f32[200]{0:T(256)S(1)}, u32[]{:S(2)}, u32[]{:S(2)}) collective-permute-start(f32[200]{0:T(256)S(1)} %multiply_reduce_fusion), channel_id=1, source_target_pairs={{0,1},{1,0},{2,3},{3,2},{4,5},{5,4},{6,7},{7,6},{8,9},{9,8},{10,11... | collective-permute-start | bytes 2408 | tf_op jit(solution)/shard_map/ppermute | solution.py:31
  22.2 0.1 pad_add_fusion.place_ref
  22.3 1.0 collective-permute-done.2
  23.3 0.7 pack.1
  24.0 47.2 %all-gather.1 = bf16[3200,128]{1,0:T(8,128)(2,1)S(1)} all-gather(bf16[200,128]{1,0:T(8,128)(2,1)S(1)} %pack.1), channel_id=3, replica_groups=mesh['ylo'=2,'z'=16,'xh'=2,'xl'=2,'yhi'=2,'core'=2] {'z'}, dimensions={0}, use_global_device_ids=true | all-gather | bytes 870400 | tf_op jit(solution)/shard_map/all_gather | solution.py:240
  71.2 1.9 %collective-permute-start.3 = (bf16[16,200,128]{2,1,0:T(8,128)(2,1)S(1)}, bf16[16,200,128]{2,1,0:T(8,128)(2,1)S(1)}, u32[]{:S(2)}, u32[]{:S(2)}) collective-permute-start(bf16[16,200,128]{2,1,0:T(8,128)(2,1)S(1)} %bitcast.28), channel_id=1, source_target_pairs={{0,1},{1,0},{2,3},{3,2},{4,5},{5,4},{6,7},{7,6},{8,9},{9,8},{10,11... | collective-permute-start | bytes 2457608 | tf_op jit(solution)/shard_map/ppermute | solution.py:31
  73.2 2.3 %collective-permute-done.3.theirs_ref = bf16[16,200,128]{2,1,0:T(8,128)(2,1)S(1)} collective-permute-done((bf16[16,200,128]{2,1,0:T(8,128)(2,1)S(1)}, bf16[16,200,128]{2,1,0:T(8,128)(2,1)S(1)}, u32[]{:S(2)}, u32[]{:S(2)}) %collective-permute-start.3) | collective-permute-done | bytes 819232 | tf_op jit(solution)/shard_map/ppermute | solution.py:31
  75.5 5.2 %attend.1.near_ref = bf16[2,128,640]{2,1,0:T(8,128)(2,1)S(1)} custom-call(s32[6]{0:T(128)S(1)} %pad_add_fusion.place_ref, bf16[128,640]{1,0:T(8,128)(2,1)S(1)} %prepare.1.q_ref, bf16[128,640]{1,0:T(8,128)(2,1)} %collective-permute-done.1.far_ref, bf16[16,200,128]{2,1,0:T(8,128)(2,1)S(1)} %bitcast.29, bf16[16,200,128]{2,1,0:T(8,128)(2,1)S(1)} %collective-permute-done.3.theirs_ref), custom_call_target="tpu_custom_call" | custom-call | tf_op jit(solution)/shard_map/attend/pallas_call | solution.py:161
  80.7 3.5 %collective-permute-start.4 = (bf16[2,128,640]{2,1,0:T(8,128)(2,1)S(1)}, bf16[2,128,640]{2,1,0:T(8,128)(2,1)S(1)}, u32[]{:S(2)}, u32[]{:S(2)}) collective-permute-start(bf16[2,128,640]{2,1,0:T(8,128)(2,1)S(1)} %attend.1.near_ref), channel_id=1, source_target_pairs={{0,256},{256,0},{1,257},{257,1},{2,258},{258,2},{3,259},{259,3},{4... | collective-permute-start | bytes 983048 | tf_op jit(solution)/shard_map/ppermute | solution.py:31
  84.2 8.1 %collective-permute-done.4.far_ref = bf16[2,128,640]{2,1,0:T(8,128)(2,1)S(1)} collective-permute-done((bf16[2,128,640]{2,1,0:T(8,128)(2,1)S(1)}, bf16[2,128,640]{2,1,0:T(8,128)(2,1)S(1)}, u32[]{:S(2)}, u32[]{:S(2)}) %collective-permute-start.4) | collective-permute-done | bytes 327712 | tf_op jit(solution)/shard_map/ppermute | solution.py:31
  92.3 0.4 combine.1
  92.7 1.9 %collective-permute-start.5 = (bf16[256,512]{1,0:T(8,128)(2,1)S(1)}, bf16[256,512]{1,0:T(8,128)(2,1)S(1)}, u32[]{:S(2)}, u32[]{:S(2)}) collective-permute-start(bf16[256,512]{1,0:T(8,128)(2,1)S(1)} %combine.1), channel_id=1, source_target_pairs={{0,1},{1,0},{2,3},{3,2},{4,5},{5,4},{6,7},{7,6},{8,9},{9,8},{10,11... | collective-permute-start | bytes 786440 | tf_op jit(solution)/shard_map/ppermute | solution.py:31
  94.6 1.5 %collective-permute-done.5 = bf16[256,512]{1,0:T(8,128)(2,1)S(1)} collective-permute-done((bf16[256,512]{1,0:T(8,128)(2,1)S(1)}, bf16[256,512]{1,0:T(8,128)(2,1)S(1)}, u32[]{:S(2)}, u32[]{:S(2)}) %collective-permute-start.5) | collective-permute-done | bytes 262176 | tf_op jit(solution)/shard_map/ppermute | solution.py:31
  96.1 0.9 pad_maximum_fusion
  97.0 1.8 %all-gather.4.cloned.1.call-done = bf16[16384,128]{1,0:T(8,128)(2,1)} async-done(((bf16[1024,128]{1,0:T(8,128)(2,1)}), bf16[16384,128]{1,0:T(8,128)(2,1)}) %all-gather.4.cloned.1.call-update) | async-done | bytes 4194320 | tf_op jit(solution)/shard_map/all_gather | solution.py:230
  98.8 3.6 %fusion = bf16[8,2,2,128,128]{4,3,1,2,0:T(8,128)(2,1)S(1)} fusion(bf16[8,2,1024,128,1]{3,2,4,1,0:T(8,128)(2,1)} %bitcast.38, bf16[2,128,1024,1,1]{2,1,0,4,3:T(8,128)(2,1)} %bitcast.35), kind=kOutput, calls=%fused_computation.1 | convolution fusion | flops 1074266112 | bytes 5767168 | tf_op jit(solution)/shard_map/rmk,jtkn->jrtnm/dot_general | solution.py:249
  102.4 0.1 copy.11
  102.5 23.1 %all_to_all.5.x_ref = bf16[16,2,128,128]{3,2,1,0:T(8,128)(2,1)S(1)} all-to-all(bf16[16,2,128,128]{3,2,1,0:T(8,128)(2,1)S(1)} %bitcast.33), channel_id=1, replica_groups=mesh['ylo'=2,'z'=16,'xh'=2,'xl'=2,'yhi'=2,'core'=2] {'xl','yhi','core','..., dimensions={0} | all-to-all | bytes 2097152 | tf_op jit(solution)/shard_map/all_to_all | solution.py:251
  125.6 0.2 reduce.1
  125.8 3.1 %collective-permute-start.6 = (bf16[128,512]{1,0:T(8,128)(2,1)S(1)}, bf16[128,512]{1,0:T(8,128)(2,1)S(1)}, u32[]{:S(2)}, u32[]{:S(2)}) collective-permute-start(bf16[128,512]{1,0:T(8,128)(2,1)S(1)} %reduce.1), channel_id=1, source_target_pairs={{0,0},{1,1},{2,2},{3,3},{4,4},{5,5},{6,6},{7,7},{8,256},{9,257},{1... | collective-permute-start | bytes 393224 | tf_op jit(solution)/shard_map/ppermute | solution.py:40
  128.9 6.7 %collective-permute-done.6 = bf16[128,512]{1,0:T(8,128)(2,1)S(1)} collective-permute-done((bf16[128,512]{1,0:T(8,128)(2,1)S(1)}, bf16[128,512]{1,0:T(8,128)(2,1)S(1)}, u32[]{:S(2)}, u32[]{:S(2)}) %collective-permute-start.6) | collective-permute-done | bytes 131104 | tf_op jit(solution)/shard_map/ppermute | solution.py:40
  135.7 0.7 copy.17
  (7 shorter events, 0.0 us)
Async XLA Ops:
  6.5 8.7 %copy-start = (bf16[200,8192]{1,0:T(8,128)(2,1)S(1)}, bf16[200,8192]{1,0:T(8,128)(2,1)}, u32[]{:S(2)}) copy-start(bf16[200,8192]{1,0:T(8,128)(2,1)} %param.9) | copy-start | bytes 9830404
  6.5 92.2 %all-gather.4.cloned.1.call-start = ((), (), s32[]{:S(2)}) async-start(), calls=%async_computation.1 | async-start | bytes 4456448 | tf_op jit(solution)/shard_map/all_gather | solution.py:230
  7.7 3.2 %collective-permute-start = (bf16[512,128]{1,0:T(8,128)(2,1)S(1)}, bf16[512,128]{1,0:T(8,128)(2,1)S(1)}, u32[]{:S(2)}, u32[]{:S(2)}) collective-permute-start(bf16[512,128]{1,0:T(8,128)(2,1)S(1)} %get-tuple-element.14), channel_id=1, source_target_pairs={{0,1},{1,0},{2,3},{3,2},{4,5},{5,4},{6,7},{7,6},{8,9},{9,8},{10,11... | collective-permute-start | bytes 393224 | tf_op jit(solution)/shard_map/ppermute | solution.py:31
  11.7 10.5 %copy-start.2 = (s32[4]{0:T(128)S(1)}, s32[4]{0:T(128)}, u32[]{:S(2)}) copy-start(s32[4]{0:T(128)} %param.14) | copy-start | bytes 52
  11.7 11.6 %copy-start.1 = (f32[128]{0:T(128)S(1)}, f32[128]{0:T(128)}, u32[]{:S(2)}) copy-start(f32[128]{0:T(128)} %param.13) | copy-start | bytes 1540
  11.7 8.5 %collective-permute-start.1 = (bf16[128,640]{1,0:T(8,128)(2,1)S(1)}, bf16[128,640]{1,0:T(8,128)(2,1)}, u32[]{:S(2)}, u32[]{:S(2)}) collective-permute-start(bf16[128,640]{1,0:T(8,128)(2,1)S(1)} %prepare.1.q_ref), channel_id=1, source_target_pairs={{0,256},{256,0},{1,257},{257,1},{2,258},{258,2},{3,259},{259,3},{4... | collective-permute-start | bytes 491528 | tf_op jit(solution)/shard_map/ppermute | solution.py:31
  20.3 3.0 %collective-permute-start.2 = (f32[200]{0:T(256)S(1)}, f32[200]{0:T(256)S(1)}, u32[]{:S(2)}, u32[]{:S(2)}) collective-permute-start(f32[200]{0:T(256)S(1)} %multiply_reduce_fusion), channel_id=1, source_target_pairs={{0,1},{1,0},{2,3},{3,2},{4,5},{5,4},{6,7},{7,6},{8,9},{9,8},{10,11... | collective-permute-start | bytes 2408 | tf_op jit(solution)/shard_map/ppermute | solution.py:31
  71.2 4.2 %collective-permute-start.3 = (bf16[16,200,128]{2,1,0:T(8,128)(2,1)S(1)}, bf16[16,200,128]{2,1,0:T(8,128)(2,1)S(1)}, u32[]{:S(2)}, u32[]{:S(2)}) collective-permute-start(bf16[16,200,128]{2,1,0:T(8,128)(2,1)S(1)} %bitcast.28), channel_id=1, source_target_pairs={{0,1},{1,0},{2,3},{3,2},{4,5},{5,4},{6,7},{7,6},{8,9},{9,8},{10,11... | collective-permute-start | bytes 2457608 | tf_op jit(solution)/shard_map/ppermute | solution.py:31
  80.7 11.6 %collective-permute-start.4 = (bf16[2,128,640]{2,1,0:T(8,128)(2,1)S(1)}, bf16[2,128,640]{2,1,0:T(8,128)(2,1)S(1)}, u32[]{:S(2)}, u32[]{:S(2)}) collective-permute-start(bf16[2,128,640]{2,1,0:T(8,128)(2,1)S(1)} %attend.1.near_ref), channel_id=1, source_target_pairs={{0,256},{256,0},{1,257},{257,1},{2,258},{258,2},{3,259},{259,3},{4... | collective-permute-start | bytes 983048 | tf_op jit(solution)/shard_map/ppermute | solution.py:31
  92.7 3.4 %collective-permute-start.5 = (bf16[256,512]{1,0:T(8,128)(2,1)S(1)}, bf16[256,512]{1,0:T(8,128)(2,1)S(1)}, u32[]{:S(2)}, u32[]{:S(2)}) collective-permute-start(bf16[256,512]{1,0:T(8,128)(2,1)S(1)} %combine.1), channel_id=1, source_target_pairs={{0,1},{1,0},{2,3},{3,2},{4,5},{5,4},{6,7},{7,6},{8,9},{9,8},{10,11... | collective-permute-start | bytes 786440 | tf_op jit(solution)/shard_map/ppermute | solution.py:31
  125.8 9.9 %collective-permute-start.6 = (bf16[128,512]{1,0:T(8,128)(2,1)S(1)}, bf16[128,512]{1,0:T(8,128)(2,1)S(1)}, u32[]{:S(2)}, u32[]{:S(2)}) collective-permute-start(bf16[128,512]{1,0:T(8,128)(2,1)S(1)} %reduce.1), channel_id=1, source_target_pairs={{0,0},{1,1},{2,2},{3,3},{4,4},{5,5},{6,6},{7,7},{8,256},{9,257},{1... | collective-permute-start | bytes 393224 | tf_op jit(solution)/shard_map/ppermute | solution.py:40
Sparse Core Ops, SparseCore 0:
  11.8 86.9 all-gather.3

commit v8 on v7

--- a/solution.py
+++ b/solution.py
@@ -80,43 +80,10 @@
     )(*(pltpu.with_memory_space_constraint(value, pltpu.HBM) for value in inputs))
 
 
-def column(row, count):
-    width = row.shape[1]
-    across = lax.broadcasted_iota(jnp.int32, (count, width), 1)
-    down = lax.broadcasted_iota(jnp.int32, (count, width), 0)
-    return jnp.sum(jnp.where(across == down, row, 0.0), axis=1, keepdims=True)
-
-
-def pack_kernel(place_ref, x_ref, own_ref, other_ref, gain_ref, o_ref):
-    mean_sq = (column(own_ref[...], LOCAL) + column(other_ref[...], LOCAL)) / HD
-    gain = gain_ref[...]
-    gain = jnp.where(place_ref[0] == 0, gain, jnp.concatenate([gain[:, HD // 2 :]] * 2, axis=1))
-    lane = lax.broadcasted_iota(jnp.int32, (LOCAL, HD), 1)
-    field = x_ref[...]
-    key = field / jnp.sqrt(mean_sq + EPSILON) * gain
-    o_ref[...] = jnp.where(lane < HD // 2, key, field).astype(BF)
-
-
-def pack(place, projected, own_squares, other_squares, k_gain):
-    return pl.pallas_call(
-        pack_kernel,
-        in_specs=[smem(), vmem(), vmem(), vmem(), vmem()],
-        out_specs=vmem(),
-        out_shape=jax.ShapeDtypeStruct((LOCAL, HD), BF),
-        compiler_params=params(4),
-        name="pack",
-    )(
-        place,
-        projected,
-        own_squares.reshape(1, LOCAL),
-        other_squares.reshape(1, LOCAL),
-        k_gain.reshape(1, HD),
-    )
-
-
-def attend_kernel(place_ref, q_ref, far_ref, mine_ref, theirs_ref, o_ref, key_s, value_s):
+def attend_kernel(place_ref, q_ref, far_ref, gain_ref, mine_ref, theirs_ref, o_ref, key_s, value_s):
     core, ylo = place_ref[0], place_ref[1]
     half = HD // 2
+    gain = gain_ref[...]
     lane = lax.broadcasted_iota(jnp.int32, (LOCAL, HD), 1)
     item = lax.broadcasted_iota(jnp.int32, (LOCAL, HD), 0)
     for block in range(BLOCKS):
@@ -124,7 +91,9 @@
         mine, theirs = mine_ref[block], theirs_ref[block]
         left = jnp.where(core == 0, mine, theirs)
         right = jnp.where(core == 0, theirs, mine)
-        key_s[rows, :HD] = jnp.concatenate([left[:, :half], right[:, :half]], axis=1)
+        key = jnp.concatenate([left[:, :half], right[:, :half]], axis=1).astype(F32)
+        mean_sq = jnp.mean(key * key, axis=1, keepdims=True)
+        key_s[rows, :HD] = (key * lax.rsqrt(mean_sq + EPSILON) * gain).astype(BF)
         value_s[rows, :HD] = jnp.concatenate([left[:, half:], right[:, half:]], axis=1)
         tile = 2 * ylo + block // 8
         absent = item + (block % 8) * LOCAL >= place_ref[2 + tile]
@@ -157,16 +126,16 @@
     o_ref[1 - ylo, :, WIDTH:] = packed[ROWS:]
 
 
-def attend(place, query, far, mine, theirs):
+def attend(place, query, far, k_gain, mine, theirs):
     return pl.pallas_call(
         attend_kernel,
-        in_specs=[smem(), vmem(), vmem(), vmem(), vmem()],
+        in_specs=[smem(), vmem(), vmem(), vmem(), vmem(), vmem()],
         out_specs=vmem(),
         out_shape=jax.ShapeDtypeStruct((2, ROWS, WIDTH + HD), BF),
         scratch_shapes=[pltpu.VMEM((SLOTS, 2 * HD), BF), pltpu.VMEM((SLOTS, 2 * HD), BF)],
         compiler_params=params(32),
         name="attend",
-    )(place, query, far, mine, theirs)
+    )(place, query, far, k_gain.reshape(1, HD), mine, theirs)
 
 
 def combine_kernel(near_ref, far_ref, o_ref):
@@ -216,7 +185,6 @@
 def local(queries, vision, kv_weight, out_weight, q_gain, k_gain, tile_counts, spans):
     core = lax.axis_index("core")
     ylo = lax.axis_index("ylo")
-    half = HD // 2
 
     place = jnp.concatenate([jnp.stack([core, ylo]).astype(jnp.int32), tile_counts])
 
@@ -232,15 +200,12 @@
     both = jnp.transpose(kv_weight, (0, 2, 1)).reshape(HD, vision.shape[1])
     projected = lax.dot_general(
         vision, both, (((1,), (1,)), ((), ())), preferred_element_type=F32
-    )
+    ).astype(BF)
     projected, far = lax.optimization_barrier((projected, far))
-    key_raw = projected[:, :half]
-    own_squares = jnp.sum(key_raw * key_raw, axis=1)
-    local_pair = pack(place, projected, own_squares, swapped(own_squares, "core"), k_gain)
-    mine = lax.all_gather(local_pair, "z", axis=0, tiled=False)
+    mine = lax.all_gather(projected, "z", axis=0, tiled=False)
     theirs = swapped(mine, "core")
 
-    partial = attend(place, query, far, mine, theirs)
+    partial = attend(place, query, far, k_gain, mine, theirs)
     own = combine(partial, swapped(partial, "ylo"))
     other = swapped(own, "core")
 

time: 144 us -> 146 us (1.014)
  Pallas kernels: 7.68 us -> 10.7 us
  waiting for transfers between devices: 23.9 us -> 21.1 us
  blocking collectives: 70.3 us -> 72.9 us
  starting transfers between devices: 17.8 us -> 16 us
  local copies, waits for them, and re-layouts: 1.88 us -> 3.46 us
    pallas_call x1, Pallas kernels: 5.19 us -> 8.93 us  [attend(): pl.pallas_call(attend_kernel, in_specs=[smem(), vmem(), vmem(), vmem(), v...]
    all_gather x1, blocking collectives: 47.2 us -> 49.3 us  [local(): mine = lax.all_gather(projected, 'z', axis=0, tiled=False)]
    ppermute x6 -> x5, starting transfers between devices: 14.7 us -> 12.7 us  [swapped(): return lax.ppermute(value, axis, [(0, 1), (1, 0)])]
    all_gather x1, waiting for transfers between devices: 1.76 us -> 0.01 us  [local(): weight = lax.all_gather(pair, 'z', axis=0, tiled=False)]
    unnamed x7 -> x11, local copies, waits for them, and re-layouts: 0.67 us -> 2.25 us
    ppermute x6 -> x5, waiting for transfers between devices: 15.4 us -> 14.6 us  [swapped(): return lax.ppermute(value, axis, [(0, 1), (1, 0)])]
  transfers between devices with their start and end apart: 8 -> 7, of which waited for: 8 -> 6; matrix products, arithmetic and copies ran while one was open for 3% -> 2% of each run, Pallas kernels for 5% -> 7%
where the time goes in v8:
time: 146 us
  blocking collectives  72.9 us (50%)
  waiting for transfers between devices  21.1 us (14%)
  starting transfers between devices  16 us (11%)
  between operations  13.5 us (9%)
  Pallas kernels  10.7 us (7%)
  matrix products  6.26 us (4%)
  local copies, waits for them, and re-layouts  3.46 us (2%)
  other arithmetic  1.68 us (1%)
    all_gather x1, blocking collectives, local(): mine = lax.all_gather(projected, 'z', axis=0, tiled=False)  49.3 us
    all_to_all x1, blocking collectives, local(): lax.all_to_all(product, ('xl', 'yhi', 'core', 'xh'), 0, 0, tiled=True)  23.6 us
    ppermute x5, waiting for transfers between devices, swapped(): return lax.ppermute(value, axis, [(0, 1), (1, 0)])  14.6 us
    ppermute x5, starting transfers between devices, swapped(): return lax.ppermute(value, axis, [(0, 1), (1, 0)])  12.7 us
    pallas_call x1, Pallas kernels, attend(): pl.pallas_call(attend_kernel, in_specs=[smem(), vmem(), vmem(), vmem(), v...  8.93 us
    ppermute x1, waiting for transfers between devices, placed(): return lax.ppermute(value, AXES, pairs)  6.48 us
    dot_general x1, matrix products, local(): jnp.einsum('rmk,jtkn->jrtnm', attended, split, preferred_element_type=F32)  3.6 us
    ppermute x1, starting transfers between devices, placed(): return lax.ppermute(value, AXES, pairs)  3.39 us
  transfers between devices with their start and end apart: 7, of which 6 were waited for; matrix products, arithmetic and copies ran while one was open for 2% of the time, Pallas kernels for 7%

profile of v8, /device:TPU:6, one launch (start us, length us, event | category | flops | bytes accessed | tf_op | source)
XLA Modules:
  0.0 145.7 jit_solution(8135382448594322647)
XLA Ops:
  6.5 0.0 copy-start
  6.5 1.1 constant_dynamic-slice_fusion.1
  7.7 1.9 %collective-permute-start = (bf16[512,128]{1,0:T(8,128)(2,1)S(1)}, bf16[512,128]{1,0:T(8,128)(2,1)S(1)}, u32[]{:S(2)}, u32[]{:S(2)}) collective-permute-start(bf16[512,128]{1,0:T(8,128)(2,1)S(1)} %get-tuple-element.14), channel_id=1, source_target_pairs={{0,1},{1,0},{2,3},{3,2},{4,5},{5,4},{6,7},{7,6},{8,9},{9,8},{10,11... | collective-permute-start | bytes 393224 | tf_op jit(solution)/shard_map/ppermute | solution.py:31
  9.6 1.2 prepare.1.q_ref
  10.8 0.1 collective-permute-done
  10.9 0.7 pad_maximum_fusion.1
  11.7 0.0 all-gather.4.cloned.1.call-update
  11.7 3.5 %collective-permute-start.1 = (bf16[128,640]{1,0:T(8,128)(2,1)S(1)}, bf16[128,640]{1,0:T(8,128)(2,1)S(1)}, u32[]{:S(2)}, u32[]{:S(2)}) collective-permute-start(bf16[128,640]{1,0:T(8,128)(2,1)S(1)} %prepare.1.q_ref), channel_id=1, source_target_pairs={{0,256},{256,0},{1,257},{257,1},{2,258},{258,2},{3,259},{259,3},{4... | collective-permute-start | bytes 491528 | tf_op jit(solution)/shard_map/ppermute | solution.py:31
  15.2 0.0 copy-start.4
  15.2 0.0 copy-start.3
  15.2 2.7 %convolution_convert_fusion.1 = bf16[200,128]{1,0:T(8,128)(2,1)S(1)} fusion(bf16[200,8192]{1,0:T(8,128)(2,1)S(1)} %copy-done, bf16[128,8192]{1,0:T(8,128)(2,1)} %bitcast.28), kind=kOutput, calls=%fused_computation.2 | convolution fusion | flops 419456000 | bytes 5425152 | tf_op jit(solution)/shard_map/dot_general | solution.py:201
  17.9 2.2 %collective-permute-done.1.far_ref = bf16[128,640]{1,0:T(8,128)(2,1)S(1)} collective-permute-done((bf16[128,640]{1,0:T(8,128)(2,1)S(1)}, bf16[128,640]{1,0:T(8,128)(2,1)S(1)}, u32[]{:S(2)}, u32[]{:S(2)}) %collective-permute-start.1) | collective-permute-done | bytes 163872 | tf_op jit(solution)/shard_map/ppermute | solution.py:31
  20.1 0.7 copy-done.1
  20.7 49.3 %all-gather.1 = bf16[3200,128]{1,0:T(8,128)(2,1)} all-gather(bf16[200,128]{1,0:T(8,128)(2,1)S(1)} %convolution_convert_fusion.1), channel_id=3, replica_groups=mesh['ylo'=2,'z'=16,'xh'=2,'xl'=2,'yhi'=2,'core'=2] {'z'}, dimensions={0}, use_global_device_ids=true | all-gather | bytes 870400 | tf_op jit(solution)/shard_map/all_gather | solution.py:205
  70.0 1.9 %collective-permute-start.2 = (bf16[16,200,128]{2,1,0:T(8,128)(2,1)}, bf16[16,200,128]{2,1,0:T(8,128)(2,1)}, u32[]{:S(2)}, u32[]{:S(2)}) collective-permute-start(bf16[16,200,128]{2,1,0:T(8,128)(2,1)} %bitcast.9.mine_ref), channel_id=1, source_target_pairs={{0,1},{1,0},{2,3},{3,2},{4,5},{5,4},{6,7},{7,6},{8,9},{9,8},{10,11... | collective-permute-start | bytes 2457608 | tf_op jit(solution)/shard_map/ppermute | solution.py:31
  71.9 0.1 pad_add_fusion.place_ref
  72.0 2.5 %collective-permute-done.2.theirs_ref = bf16[16,200,128]{2,1,0:T(8,128)(2,1)} collective-permute-done((bf16[16,200,128]{2,1,0:T(8,128)(2,1)}, bf16[16,200,128]{2,1,0:T(8,128)(2,1)}, u32[]{:S(2)}, u32[]{:S(2)}) %collective-permute-start.2) | collective-permute-done | bytes 819232 | tf_op jit(solution)/shard_map/ppermute | solution.py:31
  74.6 0.9 copy-done.2
  75.5 8.9 %attend.1.near_ref = bf16[2,128,640]{2,1,0:T(8,128)(2,1)S(1)} custom-call(s32[6]{0:T(128)S(1)} %pad_add_fusion.place_ref, bf16[128,640]{1,0:T(8,128)(2,1)S(1)} %prepare.1.q_ref, bf16[128,640]{1,0:T(8,128)(2,1)S(1)} %copy-done.2, f32[1,128]{1,0:T(1,128)S(1)} %bitcast.26, bf16[16,200,128]{2,1,0:T(8,128)(2,1)} %bitcast.9.mine_ref, ...), custom_call_target="tpu_custom_call" | custom-call | tf_op jit(solution)/shard_map/attend/pallas_call | solution.py:130
  84.4 3.4 %collective-permute-start.3 = (bf16[2,128,640]{2,1,0:T(8,128)(2,1)S(1)}, bf16[2,128,640]{2,1,0:T(8,128)(2,1)S(1)}, u32[]{:S(2)}, u32[]{:S(2)}) collective-permute-start(bf16[2,128,640]{2,1,0:T(8,128)(2,1)S(1)} %attend.1.near_ref), channel_id=1, source_target_pairs={{0,256},{256,0},{1,257},{257,1},{2,258},{258,2},{3,259},{259,3},{4... | collective-permute-start | bytes 983048 | tf_op jit(solution)/shard_map/ppermute | solution.py:31
  87.8 8.2 %collective-permute-done.3.far_ref = bf16[2,128,640]{2,1,0:T(8,128)(2,1)S(1)} collective-permute-done((bf16[2,128,640]{2,1,0:T(8,128)(2,1)S(1)}, bf16[2,128,640]{2,1,0:T(8,128)(2,1)S(1)}, u32[]{:S(2)}, u32[]{:S(2)}) %collective-permute-start.3) | collective-permute-done | bytes 327712 | tf_op jit(solution)/shard_map/ppermute | solution.py:31
  96.1 0.4 combine.1
  96.5 1.9 %collective-permute-start.4 = (bf16[256,512]{1,0:T(8,128)(2,1)S(1)}, bf16[256,512]{1,0:T(8,128)(2,1)S(1)}, u32[]{:S(2)}, u32[]{:S(2)}) collective-permute-start(bf16[256,512]{1,0:T(8,128)(2,1)S(1)} %combine.1), channel_id=1, source_target_pairs={{0,1},{1,0},{2,3},{3,2},{4,5},{5,4},{6,7},{7,6},{8,9},{9,8},{10,11... | collective-permute-start | bytes 786440 | tf_op jit(solution)/shard_map/ppermute | solution.py:31
  98.4 1.5 %collective-permute-done.4 = bf16[256,512]{1,0:T(8,128)(2,1)S(1)} collective-permute-done((bf16[256,512]{1,0:T(8,128)(2,1)S(1)}, bf16[256,512]{1,0:T(8,128)(2,1)S(1)}, u32[]{:S(2)}, u32[]{:S(2)}) %collective-permute-start.4) | collective-permute-done | bytes 262176 | tf_op jit(solution)/shard_map/ppermute | solution.py:31
  99.9 0.9 pad_maximum_fusion
  100.8 3.6 %fusion = bf16[8,2,2,128,128]{4,3,1,2,0:T(8,128)(2,1)S(1)} fusion(bf16[8,2,1024,128,1]{3,2,4,1,0:T(8,128)(2,1)} %bitcast.32, bf16[2,128,1024,1,1]{2,1,0,4,3:T(8,128)(2,1)} %bitcast.29), kind=kOutput, calls=%fused_computation.1 | convolution fusion | flops 1074266112 | bytes 5767168 | tf_op jit(solution)/shard_map/rmk,jtkn->jrtnm/dot_general | solution.py:214
  104.4 0.1 copy.11
  104.5 23.6 %all_to_all.5.x_ref = bf16[16,2,128,128]{3,2,1,0:T(8,128)(2,1)S(1)} all-to-all(bf16[16,2,128,128]{3,2,1,0:T(8,128)(2,1)S(1)} %bitcast.27), channel_id=1, replica_groups=mesh['ylo'=2,'z'=16,'xh'=2,'xl'=2,'yhi'=2,'core'=2] {'xl','yhi','core','..., dimensions={0} | all-to-all | bytes 2097152 | tf_op jit(solution)/shard_map/all_to_all | solution.py:216
  128.1 0.2 reduce.1
  128.3 3.4 %collective-permute-start.5 = (bf16[128,512]{1,0:T(8,128)(2,1)S(1)}, bf16[128,512]{1,0:T(8,128)(2,1)S(1)}, u32[]{:S(2)}, u32[]{:S(2)}) collective-permute-start(bf16[128,512]{1,0:T(8,128)(2,1)S(1)} %reduce.1), channel_id=1, source_target_pairs={{0,0},{1,1},{2,2},{3,3},{4,4},{5,5},{6,6},{7,7},{8,256},{9,257},{1... | collective-permute-start | bytes 393224 | tf_op jit(solution)/shard_map/ppermute | solution.py:40
  131.7 6.5 %collective-permute-done.5 = bf16[128,512]{1,0:T(8,128)(2,1)S(1)} collective-permute-done((bf16[128,512]{1,0:T(8,128)(2,1)S(1)}, bf16[128,512]{1,0:T(8,128)(2,1)S(1)}, u32[]{:S(2)}, u32[]{:S(2)}) %collective-permute-start.5) | collective-permute-done | bytes 131104 | tf_op jit(solution)/shard_map/ppermute | solution.py:40
  138.2 0.7 copy.17
  (7 shorter events, 0.0 us)
Async XLA Ops:
  6.5 8.7 %copy-start = (bf16[200,8192]{1,0:T(8,128)(2,1)S(1)}, bf16[200,8192]{1,0:T(8,128)(2,1)}, u32[]{:S(2)}) copy-start(bf16[200,8192]{1,0:T(8,128)(2,1)} %param.9) | copy-start | bytes 9830404
  6.5 94.2 %all-gather.4.cloned.1.call-start = ((), (), s32[]{:S(2)}) async-start(), calls=%async_computation.1 | async-start | bytes 4456448 | tf_op jit(solution)/shard_map/all_gather | solution.py:198
  7.7 3.2 %collective-permute-start = (bf16[512,128]{1,0:T(8,128)(2,1)S(1)}, bf16[512,128]{1,0:T(8,128)(2,1)S(1)}, u32[]{:S(2)}, u32[]{:S(2)}) collective-permute-start(bf16[512,128]{1,0:T(8,128)(2,1)S(1)} %get-tuple-element.14), channel_id=1, source_target_pairs={{0,1},{1,0},{2,3},{3,2},{4,5},{5,4},{6,7},{7,6},{8,9},{9,8},{10,11... | collective-permute-start | bytes 393224 | tf_op jit(solution)/shard_map/ppermute | solution.py:31
  11.7 8.4 %collective-permute-start.1 = (bf16[128,640]{1,0:T(8,128)(2,1)S(1)}, bf16[128,640]{1,0:T(8,128)(2,1)S(1)}, u32[]{:S(2)}, u32[]{:S(2)}) collective-permute-start(bf16[128,640]{1,0:T(8,128)(2,1)S(1)} %prepare.1.q_ref), channel_id=1, source_target_pairs={{0,256},{256,0},{1,257},{257,1},{2,258},{258,2},{3,259},{259,3},{4... | collective-permute-start | bytes 491528 | tf_op jit(solution)/shard_map/ppermute | solution.py:31
  15.2 56.7 %copy-start.4 = (s32[4]{0:T(128)S(1)}, s32[4]{0:T(128)}, u32[]{:S(2)}) copy-start(s32[4]{0:T(128)} %param.14) | copy-start | bytes 52
  15.2 59.3 %copy-start.3 = (f32[128]{0:T(128)S(1)}, f32[128]{0:T(128)}, u32[]{:S(2)}) copy-start(f32[128]{0:T(128)} %param.13) | copy-start | bytes 1540
  20.1 0.7 copy-start.1
  70.0 4.6 %collective-permute-start.2 = (bf16[16,200,128]{2,1,0:T(8,128)(2,1)}, bf16[16,200,128]{2,1,0:T(8,128)(2,1)}, u32[]{:S(2)}, u32[]{:S(2)}) collective-permute-start(bf16[16,200,128]{2,1,0:T(8,128)(2,1)} %bitcast.9.mine_ref), channel_id=1, source_target_pairs={{0,1},{1,0},{2,3},{3,2},{4,5},{5,4},{6,7},{7,6},{8,9},{9,8},{10,11... | collective-permute-start | bytes 2457608 | tf_op jit(solution)/shard_map/ppermute | solution.py:31
  74.6 0.9 copy-start.2
  84.4 11.6 %collective-permute-start.3 = (bf16[2,128,640]{2,1,0:T(8,128)(2,1)S(1)}, bf16[2,128,640]{2,1,0:T(8,128)(2,1)S(1)}, u32[]{:S(2)}, u32[]{:S(2)}) collective-permute-start(bf16[2,128,640]{2,1,0:T(8,128)(2,1)S(1)} %attend.1.near_ref), channel_id=1, source_target_pairs={{0,256},{256,0},{1,257},{257,1},{2,258},{258,2},{3,259},{259,3},{4... | collective-permute-start | bytes 983048 | tf_op jit(solution)/shard_map/ppermute | solution.py:31
  96.5 3.4 %collective-permute-start.4 = (bf16[256,512]{1,0:T(8,128)(2,1)S(1)}, bf16[256,512]{1,0:T(8,128)(2,1)S(1)}, u32[]{:S(2)}, u32[]{:S(2)}) collective-permute-start(bf16[256,512]{1,0:T(8,128)(2,1)S(1)} %combine.1), channel_id=1, source_target_pairs={{0,1},{1,0},{2,3},{3,2},{4,5},{5,4},{6,7},{7,6},{8,9},{9,8},{10,11... | collective-permute-start | bytes 786440 | tf_op jit(solution)/shard_map/ppermute | solution.py:31
  128.3 9.9 %collective-permute-start.5 = (bf16[128,512]{1,0:T(8,128)(2,1)S(1)}, bf16[128,512]{1,0:T(8,128)(2,1)S(1)}, u32[]{:S(2)}, u32[]{:S(2)}) collective-permute-start(bf16[128,512]{1,0:T(8,128)(2,1)S(1)} %reduce.1), channel_id=1, source_target_pairs={{0,0},{1,1},{2,2},{3,3},{4,4},{5,5},{6,6},{7,7},{8,256},{9,257},{1... | collective-permute-start | bytes 393224 | tf_op jit(solution)/shard_map/ppermute | solution.py:40
Sparse Core Ops, SparseCore 0:
  11.8 86.3 all-gather.3

commit v9 on v7

--- a/solution.py
+++ b/solution.py
@@ -14,6 +14,7 @@
 AXES = ("ylo", "z", "xh", "xl", "yhi", "core")
 SIZES = (2, 16, 2, 2, 2, 2)
 ROWS = 128
+FULL = ROWS + 8
 HEADS = 4
 WIDTH = HEADS * HD
 LOCAL = 200
@@ -58,13 +59,11 @@
         columns = slice(head * HD, (head + 1) * HD)
         field = q_ref[:, columns].astype(F32)
         mean_sq = jnp.mean(field * field, axis=1, keepdims=True)
-        o_ref[:, columns] = (field / jnp.sqrt(mean_sq + EPSILON) * gain).astype(BF)
-    row = lax.broadcasted_iota(jnp.int32, (ROWS, HD), 0)
-    lane = lax.broadcasted_iota(jnp.int32, (ROWS, HD), 1)
-    begin = jnp.sum(jnp.where(row == lane, span_ref[0:1, :], 0), axis=1, keepdims=True)
-    end = jnp.sum(jnp.where(row == lane, span_ref[1:2, :], 0), axis=1, keepdims=True)
-    inside = (begin <= lane) & (lane < end)
-    o_ref[:, WIDTH:] = jnp.where((lane <= TILES) & ~inside, NEG, 0.0).astype(BF)
+        o_ref[:ROWS, columns] = (field / jnp.sqrt(mean_sq + EPSILON) * gain).astype(BF)
+    o_ref[ROWS:, :] = jnp.zeros((8, WIDTH), BF)
+    o_ref[ROWS:, :HD] = jnp.concatenate(
+        [span_ref[...].astype(F32), jnp.zeros((6, HD), F32)], axis=0
+    ).astype(BF)
 
 
 def prepare(queries, q_gain, spans):
@@ -73,8 +72,8 @@
         prepare_kernel,
         grid=(1,),
         in_specs=[pl.BlockSpec(value.shape, lambda i: (0, 0)) for value in inputs],
-        out_specs=pl.BlockSpec((ROWS, WIDTH + HD), lambda i: (0, 0)),
-        out_shape=jax.ShapeDtypeStruct((ROWS, WIDTH + HD), BF),
+        out_specs=pl.BlockSpec((FULL, WIDTH), lambda i: (0, 0)),
+        out_shape=jax.ShapeDtypeStruct((FULL, WIDTH), BF),
         compiler_params=params(4),
         name="prepare",
     )(*(pltpu.with_memory_space_constraint(value, pltpu.HBM) for value in inputs))
@@ -112,6 +111,15 @@
         other_squares.reshape(1, LOCAL),
         k_gain.reshape(1, HD),
     )
+
+
+def masked(rows):
+    rows = rows.astype(F32)
+    begin, end = column(rows[0:1], ROWS), column(rows[1:2], ROWS)
+    lane = lax.broadcasted_iota(jnp.int32, (ROWS, HD), 1)
+    place = lane.astype(F32)
+    inside = (begin <= place) & (place < end)
+    return jnp.where((lane <= TILES) & ~inside, NEG, 0.0).astype(BF)
 
 
 def attend_kernel(place_ref, q_ref, far_ref, mine_ref, theirs_ref, o_ref, key_s, value_s):
@@ -132,12 +140,12 @@
             (lane == tile) | ((lane == TILES) & absent), 1.0, 0.0
         ).astype(BF)
     value_s[:, HD:] = jnp.ones((SLOTS, HD), BF)
-    query_ext = jnp.concatenate([q_ref[:, WIDTH:], far_ref[:, WIDTH:]], axis=0)
+    query_ext = jnp.concatenate([masked(q_ref[ROWS:, :HD]), masked(far_ref[ROWS:, :HD])], axis=0)
     wide = lax.broadcasted_iota(jnp.int32, (2 * ROWS, HD), 1)
     totals = jnp.zeros((2 * ROWS, HD), F32)
     for head in range(HEADS):
         columns = slice(head * HD, (head + 1) * HD)
-        query = jnp.concatenate([q_ref[:, columns], far_ref[:, columns]], axis=0)
+        query = jnp.concatenate([q_ref[:ROWS, columns], far_ref[:ROWS, columns]], axis=0)
         scores = lax.dot_general(
             jnp.concatenate([query, query_ext], axis=1),
             key_s[...],
@@ -147,14 +155,18 @@
         weights = jnp.exp2(scores * (math.log2(math.e) / math.sqrt(HD))).astype(BF)
         result = jnp.dot(weights, value_s[...], preferred_element_type=F32)
         numer = result[:, :HD].astype(BF)
-        o_ref[ylo, :, columns] = numer[:ROWS]
-        o_ref[1 - ylo, :, columns] = numer[ROWS:]
+        o_ref[ylo, :ROWS, columns] = numer[:ROWS]
+        o_ref[1 - ylo, :ROWS, columns] = numer[ROWS:]
         totals = jnp.where(wide % HEADS == head, result[:, HD:], totals)
-    high = totals.astype(BF)
-    low = (totals - high.astype(F32)).astype(BF)
-    packed = jnp.where(wide < HEADS, high.astype(F32), low.astype(F32)).astype(BF)
-    o_ref[ylo, :, WIDTH:] = packed[:ROWS]
-    o_ref[1 - ylo, :, WIDTH:] = packed[ROWS:]
+    sums = totals.T[:8]
+    high = sums.astype(BF).astype(F32)
+    part = lax.broadcasted_iota(jnp.int32, (8, 2 * ROWS), 0)
+    packed = jnp.where(part < HEADS, high, sums - high).astype(BF)
+    empty = jnp.zeros((8, WIDTH), BF)
+    o_ref[ylo, ROWS:, :] = empty
+    o_ref[1 - ylo, ROWS:, :] = empty
+    o_ref[ylo, ROWS:, :HD] = packed[:, :ROWS]
+    o_ref[1 - ylo, ROWS:, :HD] = packed[:, ROWS:]
 
 
 def attend(place, query, far, mine, theirs):
@@ -162,7 +174,7 @@
         attend_kernel,
         in_specs=[smem(), vmem(), vmem(), vmem(), vmem()],
         out_specs=vmem(),
-        out_shape=jax.ShapeDtypeStruct((2, ROWS, WIDTH + HD), BF),
+        out_shape=jax.ShapeDtypeStruct((2, FULL, WIDTH), BF),
         scratch_shapes=[pltpu.VMEM((SLOTS, 2 * HD), BF), pltpu.VMEM((SLOTS, 2 * HD), BF)],
         compiler_params=params(32),
         name="attend",
@@ -171,13 +183,15 @@
 
 def combine_kernel(near_ref, far_ref, o_ref):
     for block in range(2):
-        summed = near_ref[block].astype(F32) + far_ref[block].astype(F32)
+        totals = near_ref[block, ROWS:, :HD].astype(F32) + far_ref[block, ROWS:, :HD].astype(F32)
+        totals = totals[:HEADS] + totals[HEADS:]
+        rows = slice(block * ROWS, (block + 1) * ROWS)
         for head in range(HEADS):
             columns = slice(head * HD, (head + 1) * HD)
-            high = summed[:, WIDTH + head : WIDTH + head + 1]
-            low = summed[:, WIDTH + HEADS + head : WIDTH + HEADS + head + 1]
-            rows = slice(block * ROWS, (block + 1) * ROWS)
-            o_ref[rows, columns] = (summed[:, columns] / (high + low)).astype(BF)
+            summed = near_ref[block, :ROWS, columns].astype(F32)
+            summed = summed + far_ref[block, :ROWS, columns].astype(F32)
+            total = column(totals[head : head + 1], ROWS)
+            o_ref[rows, columns] = (summed / total).astype(BF)
 
 
 def combine(near, far):

time: 144 us -> 144 us (level)
  no operation moved by 1% of the time
where the time goes in v9:
time: 144 us; the launch traced here: 143 us
  blocking collectives  71.7 us (50%)
  waiting for transfers between devices  23 us (16%)
  starting transfers between devices  17.3 us (12%)
  between operations  13.5 us (9%)
  Pallas kernels  7.7 us (5%)
  matrix products  6.26 us (4%)
  local copies, waits for them, and re-layouts  1.88 us (1%)
  other arithmetic  1.77 us (1%)
    all_gather x1, blocking collectives, local(): mine = lax.all_gather(local_pair, 'z', axis=0, tiled=False)  48.6 us
    all_to_all x1, blocking collectives, local(): lax.all_to_all(product, ('xl', 'yhi', 'core', 'xh'), 0, 0, tiled=True)  23.1 us
    ppermute x6, waiting for transfers between devices, swapped(): return lax.ppermute(value, axis, [(0, 1), (1, 0)])  14.9 us
    ppermute x6, starting transfers between devices, swapped(): return lax.ppermute(value, axis, [(0, 1), (1, 0)])  13.5 us
    ppermute x1, waiting for transfers between devices, placed(): return lax.ppermute(value, AXES, pairs)  6.12 us
    pallas_call x1, Pallas kernels, attend(): pl.pallas_call(attend_kernel, in_specs=[smem(), vmem(), vmem(), vmem(), v...  5.45 us
    ppermute x1, starting transfers between devices, placed(): return lax.ppermute(value, AXES, pairs)  3.75 us
    dot_general x1, matrix products, local(): jnp.einsum('rmk,jtkn->jrtnm', attended, split, preferred_element_type=F32)  3.6 us
  transfers between devices with their start and end apart: 8, of which 8 were waited for; matrix products, arithmetic and copies ran while one was open for 3% of the time, Pallas kernels for 5%

profile of v9, /device:TPU:6, one launch (start us, length us, event | category | flops | bytes accessed | tf_op | source)
XLA Modules:
  0.0 143.2 jit_solution(18299222949599973368)
XLA Ops:
  6.5 1.1 constant_dynamic-slice_fusion.1
  7.7 1.9 %collective-permute-start = (bf16[512,128]{1,0:T(8,128)(2,1)S(1)}, bf16[512,128]{1,0:T(8,128)(2,1)S(1)}, u32[]{:S(2)}, u32[]{:S(2)}) collective-permute-start(bf16[512,128]{1,0:T(8,128)(2,1)S(1)} %get-tuple-element.14), channel_id=1, source_target_pairs={{0,1},{1,0},{2,3},{3,2},{4,5},{5,4},{6,7},{7,6},{8,9},{9,8},{10,11... | collective-permute-start | bytes 393224 | tf_op jit(solution)/shard_map/ppermute | solution.py:32
  9.6 1.1 prepare.1.q_ref
  10.7 0.2 collective-permute-done
  10.9 0.7 pad_maximum_fusion.1
  11.6 0.0 all-gather.4.cloned.1.call-update
  11.7 3.5 %collective-permute-start.1 = (bf16[136,512]{1,0:T(8,128)(2,1)S(1)}, bf16[136,512]{1,0:T(8,128)(2,1)}, u32[]{:S(2)}, u32[]{:S(2)}) collective-permute-start(bf16[136,512]{1,0:T(8,128)(2,1)S(1)} %prepare.1.q_ref), channel_id=1, source_target_pairs={{0,256},{256,0},{1,257},{257,1},{2,258},{258,2},{3,259},{259,3},{4... | collective-permute-start | bytes 417800 | tf_op jit(solution)/shard_map/ppermute | solution.py:32
  15.2 2.7 %fusion.1.x_ref = f32[200,128]{1,0:T(8,128)S(1)} fusion(bf16[200,8192]{1,0:T(8,128)(2,1)S(1)} %copy-done, bf16[128,8192]{1,0:T(8,128)(2,1)} %bitcast.34), kind=kOutput, calls=%fused_computation.8 | convolution fusion | flops 419430400 | bytes 5476352 | tf_op jit(solution)/shard_map/dot_general | solution.py:247
  17.9 1.7 %collective-permute-done.1.far_ref = bf16[136,512]{1,0:T(8,128)(2,1)} collective-permute-done((bf16[136,512]{1,0:T(8,128)(2,1)S(1)}, bf16[136,512]{1,0:T(8,128)(2,1)}, u32[]{:S(2)}, u32[]{:S(2)}) %collective-permute-start.1) | collective-permute-done | bytes 139296 | tf_op jit(solution)/shard_map/ppermute | solution.py:32
  19.6 0.1 multiply_reduce_fusion
  19.7 1.9 %collective-permute-start.2 = (f32[200]{0:T(256)S(1)}, f32[200]{0:T(256)S(1)}, u32[]{:S(2)}, u32[]{:S(2)}) collective-permute-start(f32[200]{0:T(256)S(1)} %multiply_reduce_fusion), channel_id=1, source_target_pairs={{0,1},{1,0},{2,3},{3,2},{4,5},{5,4},{6,7},{7,6},{8,9},{9,8},{10,11... | collective-permute-start | bytes 2408 | tf_op jit(solution)/shard_map/ppermute | solution.py:32
  21.6 0.1 pad_add_fusion.place_ref
  21.7 1.0 collective-permute-done.2
  22.7 0.7 pack.1
  23.4 48.6 %all-gather.1 = bf16[3200,128]{1,0:T(8,128)(2,1)S(1)} all-gather(bf16[200,128]{1,0:T(8,128)(2,1)S(1)} %pack.1), channel_id=3, replica_groups=mesh['ylo'=2,'z'=16,'xh'=2,'xl'=2,'yhi'=2,'core'=2] {'z'}, dimensions={0}, use_global_device_ids=true | all-gather | bytes 870400 | tf_op jit(solution)/shard_map/all_gather | solution.py:254
  72.0 1.9 %collective-permute-start.3 = (bf16[16,200,128]{2,1,0:T(8,128)(2,1)S(1)}, bf16[16,200,128]{2,1,0:T(8,128)(2,1)S(1)}, u32[]{:S(2)}, u32[]{:S(2)}) collective-permute-start(bf16[16,200,128]{2,1,0:T(8,128)(2,1)S(1)} %bitcast.28), channel_id=1, source_target_pairs={{0,1},{1,0},{2,3},{3,2},{4,5},{5,4},{6,7},{7,6},{8,9},{9,8},{10,11... | collective-permute-start | bytes 2457608 | tf_op jit(solution)/shard_map/ppermute | solution.py:32
  73.9 2.3 %collective-permute-done.3.theirs_ref = bf16[16,200,128]{2,1,0:T(8,128)(2,1)S(1)} collective-permute-done((bf16[16,200,128]{2,1,0:T(8,128)(2,1)S(1)}, bf16[16,200,128]{2,1,0:T(8,128)(2,1)S(1)}, u32[]{:S(2)}, u32[]{:S(2)}) %collective-permute-start.3) | collective-permute-done | bytes 819232 | tf_op jit(solution)/shard_map/ppermute | solution.py:32
  76.2 5.5 %attend.1.near_ref = bf16[2,136,512]{2,1,0:T(8,128)(2,1)S(1)} custom-call(s32[6]{0:T(128)S(1)} %pad_add_fusion.place_ref, bf16[136,512]{1,0:T(8,128)(2,1)S(1)} %prepare.1.q_ref, bf16[136,512]{1,0:T(8,128)(2,1)} %collective-permute-done.1.far_ref, bf16[16,200,128]{2,1,0:T(8,128)(2,1)S(1)} %bitcast.29, bf16[16,200,128]{2,1,0:T(8,128)(2,1)S(1)} %collective-permute-done.3.theirs_ref), custom_call_target="tpu_custom_call" | custom-call | tf_op jit(solution)/shard_map/attend/pallas_call | solution.py:173
  81.7 2.4 %collective-permute-start.4 = (bf16[2,136,512]{2,1,0:T(8,128)(2,1)S(1)}, bf16[2,136,512]{2,1,0:T(8,128)(2,1)S(1)}, u32[]{:S(2)}, u32[]{:S(2)}) collective-permute-start(bf16[2,136,512]{2,1,0:T(8,128)(2,1)S(1)} %attend.1.near_ref), channel_id=1, source_target_pairs={{0,256},{256,0},{1,257},{257,1},{2,258},{258,2},{3,259},{259,3},{4... | collective-permute-start | bytes 835592 | tf_op jit(solution)/shard_map/ppermute | solution.py:32
  84.1 8.2 %collective-permute-done.4.far_ref = bf16[2,136,512]{2,1,0:T(8,128)(2,1)S(1)} collective-permute-done((bf16[2,136,512]{2,1,0:T(8,128)(2,1)S(1)}, bf16[2,136,512]{2,1,0:T(8,128)(2,1)S(1)}, u32[]{:S(2)}, u32[]{:S(2)}) %collective-permute-start.4) | collective-permute-done | bytes 278560 | tf_op jit(solution)/shard_map/ppermute | solution.py:32
  92.3 0.2 combine.1
  92.5 1.9 %collective-permute-start.5 = (bf16[256,512]{1,0:T(8,128)(2,1)S(1)}, bf16[256,512]{1,0:T(8,128)(2,1)S(1)}, u32[]{:S(2)}, u32[]{:S(2)}) collective-permute-start(bf16[256,512]{1,0:T(8,128)(2,1)S(1)} %combine.1), channel_id=1, source_target_pairs={{0,1},{1,0},{2,3},{3,2},{4,5},{5,4},{6,7},{7,6},{8,9},{9,8},{10,11... | collective-permute-start | bytes 786440 | tf_op jit(solution)/shard_map/ppermute | solution.py:32
  94.4 1.5 %collective-permute-done.5 = bf16[256,512]{1,0:T(8,128)(2,1)S(1)} collective-permute-done((bf16[256,512]{1,0:T(8,128)(2,1)S(1)}, bf16[256,512]{1,0:T(8,128)(2,1)S(1)}, u32[]{:S(2)}, u32[]{:S(2)}) %collective-permute-start.5) | collective-permute-done | bytes 262176 | tf_op jit(solution)/shard_map/ppermute | solution.py:32
  95.9 0.9 pad_maximum_fusion
  96.8 1.9 %all-gather.4.cloned.1.call-done = bf16[16384,128]{1,0:T(8,128)(2,1)} async-done(((bf16[1024,128]{1,0:T(8,128)(2,1)}), bf16[16384,128]{1,0:T(8,128)(2,1)}) %all-gather.4.cloned.1.call-update) | async-done | bytes 4194320 | tf_op jit(solution)/shard_map/all_gather | solution.py:244
  98.7 3.6 %fusion = bf16[8,2,2,128,128]{4,3,1,2,0:T(8,128)(2,1)S(1)} fusion(bf16[8,2,1024,128,1]{3,2,4,1,0:T(8,128)(2,1)} %bitcast.38, bf16[2,128,1024,1,1]{2,1,0,4,3:T(8,128)(2,1)} %bitcast.35), kind=kOutput, calls=%fused_computation.1 | convolution fusion | flops 1074266112 | bytes 5767168 | tf_op jit(solution)/shard_map/rmk,jtkn->jrtnm/dot_general | solution.py:263
  102.3 0.1 copy.11
  102.4 23.1 %all_to_all.5.x_ref = bf16[16,2,128,128]{3,2,1,0:T(8,128)(2,1)S(1)} all-to-all(bf16[16,2,128,128]{3,2,1,0:T(8,128)(2,1)S(1)} %bitcast.33), channel_id=1, replica_groups=mesh['ylo'=2,'z'=16,'xh'=2,'xl'=2,'yhi'=2,'core'=2] {'xl','yhi','core','..., dimensions={0} | all-to-all | bytes 2097152 | tf_op jit(solution)/shard_map/all_to_all | solution.py:265
  125.6 0.2 reduce.1
  125.8 3.7 %collective-permute-start.6 = (bf16[128,512]{1,0:T(8,128)(2,1)S(1)}, bf16[128,512]{1,0:T(8,128)(2,1)S(1)}, u32[]{:S(2)}, u32[]{:S(2)}) collective-permute-start(bf16[128,512]{1,0:T(8,128)(2,1)S(1)} %reduce.1), channel_id=1, source_target_pairs={{0,0},{1,1},{2,2},{3,3},{4,4},{5,5},{6,6},{7,7},{8,256},{9,257},{1... | collective-permute-start | bytes 393224 | tf_op jit(solution)/shard_map/ppermute | solution.py:41
  129.5 6.1 %collective-permute-done.6 = bf16[128,512]{1,0:T(8,128)(2,1)S(1)} collective-permute-done((bf16[128,512]{1,0:T(8,128)(2,1)S(1)}, bf16[128,512]{1,0:T(8,128)(2,1)S(1)}, u32[]{:S(2)}, u32[]{:S(2)}) %collective-permute-start.6) | collective-permute-done | bytes 131104 | tf_op jit(solution)/shard_map/ppermute | solution.py:41
  135.7 0.7 copy.17
  (7 shorter events, 0.0 us)
Async XLA Ops:
  6.5 8.7 %copy-start = (bf16[200,8192]{1,0:T(8,128)(2,1)S(1)}, bf16[200,8192]{1,0:T(8,128)(2,1)}, u32[]{:S(2)}) copy-start(bf16[200,8192]{1,0:T(8,128)(2,1)} %param.9) | copy-start | bytes 9830404
  6.5 92.2 %all-gather.4.cloned.1.call-start = ((), (), s32[]{:S(2)}) async-start(), calls=%async_computation.1 | async-start | bytes 4456448 | tf_op jit(solution)/shard_map/all_gather | solution.py:244
  7.7 3.2 %collective-permute-start = (bf16[512,128]{1,0:T(8,128)(2,1)S(1)}, bf16[512,128]{1,0:T(8,128)(2,1)S(1)}, u32[]{:S(2)}, u32[]{:S(2)}) collective-permute-start(bf16[512,128]{1,0:T(8,128)(2,1)S(1)} %get-tuple-element.14), channel_id=1, source_target_pairs={{0,1},{1,0},{2,3},{3,2},{4,5},{5,4},{6,7},{7,6},{8,9},{9,8},{10,11... | collective-permute-start | bytes 393224 | tf_op jit(solution)/shard_map/ppermute | solution.py:32
  11.7 10.0 %copy-start.2 = (s32[4]{0:T(128)S(1)}, s32[4]{0:T(128)}, u32[]{:S(2)}) copy-start(s32[4]{0:T(128)} %param.14) | copy-start | bytes 52
  11.7 11.1 %copy-start.1 = (f32[128]{0:T(128)S(1)}, f32[128]{0:T(128)}, u32[]{:S(2)}) copy-start(f32[128]{0:T(128)} %param.13) | copy-start | bytes 1540
  11.7 7.9 %collective-permute-start.1 = (bf16[136,512]{1,0:T(8,128)(2,1)S(1)}, bf16[136,512]{1,0:T(8,128)(2,1)}, u32[]{:S(2)}, u32[]{:S(2)}) collective-permute-start(bf16[136,512]{1,0:T(8,128)(2,1)S(1)} %prepare.1.q_ref), channel_id=1, source_target_pairs={{0,256},{256,0},{1,257},{257,1},{2,258},{258,2},{3,259},{259,3},{4... | collective-permute-start | bytes 417800 | tf_op jit(solution)/shard_map/ppermute | solution.py:32
  19.7 3.0 %collective-permute-start.2 = (f32[200]{0:T(256)S(1)}, f32[200]{0:T(256)S(1)}, u32[]{:S(2)}, u32[]{:S(2)}) collective-permute-start(f32[200]{0:T(256)S(1)} %multiply_reduce_fusion), channel_id=1, source_target_pairs={{0,1},{1,0},{2,3},{3,2},{4,5},{5,4},{6,7},{7,6},{8,9},{9,8},{10,11... | collective-permute-start | bytes 2408 | tf_op jit(solution)/shard_map/ppermute | solution.py:32
  72.0 4.2 %collective-permute-start.3 = (bf16[16,200,128]{2,1,0:T(8,128)(2,1)S(1)}, bf16[16,200,128]{2,1,0:T(8,128)(2,1)S(1)}, u32[]{:S(2)}, u32[]{:S(2)}) collective-permute-start(bf16[16,200,128]{2,1,0:T(8,128)(2,1)S(1)} %bitcast.28), channel_id=1, source_target_pairs={{0,1},{1,0},{2,3},{3,2},{4,5},{5,4},{6,7},{7,6},{8,9},{9,8},{10,11... | collective-permute-start | bytes 2457608 | tf_op jit(solution)/shard_map/ppermute | solution.py:32
  81.7 10.6 %collective-permute-start.4 = (bf16[2,136,512]{2,1,0:T(8,128)(2,1)S(1)}, bf16[2,136,512]{2,1,0:T(8,128)(2,1)S(1)}, u32[]{:S(2)}, u32[]{:S(2)}) collective-permute-start(bf16[2,136,512]{2,1,0:T(8,128)(2,1)S(1)} %attend.1.near_ref), channel_id=1, source_target_pairs={{0,256},{256,0},{1,257},{257,1},{2,258},{258,2},{3,259},{259,3},{4... | collective-permute-start | bytes 835592 | tf_op jit(solution)/shard_map/ppermute | solution.py:32
  92.5 3.4 %collective-permute-start.5 = (bf16[256,512]{1,0:T(8,128)(2,1)S(1)}, bf16[256,512]{1,0:T(8,128)(2,1)S(1)}, u32[]{:S(2)}, u32[]{:S(2)}) collective-permute-start(bf16[256,512]{1,0:T(8,128)(2,1)S(1)} %combine.1), channel_id=1, source_target_pairs={{0,1},{1,0},{2,3},{3,2},{4,5},{5,4},{6,7},{7,6},{8,9},{9,8},{10,11... | collective-permute-start | bytes 786440 | tf_op jit(solution)/shard_map/ppermute | solution.py:32
  125.8 9.9 %collective-permute-start.6 = (bf16[128,512]{1,0:T(8,128)(2,1)S(1)}, bf16[128,512]{1,0:T(8,128)(2,1)S(1)}, u32[]{:S(2)}, u32[]{:S(2)}) collective-permute-start(bf16[128,512]{1,0:T(8,128)(2,1)S(1)} %reduce.1), channel_id=1, source_target_pairs={{0,0},{1,1},{2,2},{3,3},{4,4},{5,5},{6,6},{7,7},{8,256},{9,257},{1... | collective-permute-start | bytes 393224 | tf_op jit(solution)/shard_map/ppermute | solution.py:41
Sparse Core Ops, SparseCore 0:
  11.8 86.8 all-gather.3

commit v10 on v9

--- a/solution.py
+++ b/solution.py
@@ -205,6 +205,36 @@
     )(near, far)
 
 
+def merge_kernel(core_ref, own_ref, got_ref, o_ref, sem):
+    begin = pl.multiple_of(core_ref[0] * HD, HD)
+    copies = []
+    for index, source in enumerate((own_ref, got_ref)):
+        copy = pltpu.make_async_copy(
+            source.at[:, pl.ds(begin, HD)], o_ref.at[pl.ds(index * WIDTH, WIDTH)], sem.at[index]
+        )
+        copy.start()
+        copies.append(copy)
+    for copy in copies:
+        copy.wait()
+
+
+def merge(place, own, got):
+    hbm = pl.BlockSpec(memory_space=pltpu.HBM)
+    return pl.pallas_call(
+        merge_kernel,
+        in_specs=[smem(), hbm, hbm],
+        out_specs=hbm,
+        out_shape=jax.ShapeDtypeStruct((2 * WIDTH, HD), BF),
+        scratch_shapes=[pltpu.SemaphoreType.DMA((2,))],
+        compiler_params=params(4),
+        name="merge",
+    )(
+        place,
+        pltpu.with_memory_space_constraint(own, pltpu.HBM),
+        pltpu.with_memory_space_constraint(got, pltpu.HBM),
+    )
+
+
 def reduce_kernel(x_ref, o_ref):
     for core in range(2):
         for side in range(2):
@@ -236,10 +266,8 @@
 
     query = prepare(queries, q_gain, spans)
 
-    kept = lax.dynamic_slice_in_dim(out_weight, core * HD, HD, axis=1)
-    sent = lax.dynamic_slice_in_dim(out_weight, (1 - core) * HD, HD, axis=1)
-    got, query = lax.optimization_barrier((swapped(sent, "core"), query))
-    pair = jnp.concatenate([kept, got], axis=0)
+    got, query = lax.optimization_barrier((swapped(out_weight, "core"), query))
+    pair = merge(jnp.reshape(core, (1,)).astype(jnp.int32), out_weight, got)
     far = swapped(query, "ylo")
     weight = lax.all_gather(pair, "z", axis=0, tiled=False)
 

time: 144 us -> 152 us (1.056)
  Pallas kernels: 7.7 us -> 16.8 us
  starting transfers between devices: 17.3 us -> 19.6 us
  blocking collectives: 71.7 us -> 70 us
    pallas_call x0 -> x1, Pallas kernels: none -> 9.06 us  [merge(): pl.pallas_call(merge_kernel, in_specs=[smem(), hbm, hbm], out_specs=hbm,...]
    ppermute x6, starting transfers between devices: 13.5 us -> 15.5 us  [swapped(): return lax.ppermute(value, axis, [(0, 1), (1, 0)])]
  transfers between devices with their start and end apart: 8 -> 8, of which waited for: 8 -> 8; matrix products, arithmetic and copies ran while one was open for 3% -> 2% of each run, Pallas kernels for 5% -> 5%
where the time goes in v10:
time: 152 us; the launch traced here: 151 us
  blocking collectives  70 us (46%)
  waiting for transfers between devices  22.6 us (15%)
  starting transfers between devices  19.6 us (13%)
  Pallas kernels  16.8 us (11%)
  between operations  13.6 us (9%)
  matrix products  6.26 us (4%)
    all_gather x1, blocking collectives, local(): mine = lax.all_gather(local_pair, 'z', axis=0, tiled=False)  47.1 us
    all_to_all x1, blocking collectives, local(): lax.all_to_all(product, ('xl', 'yhi', 'core', 'xh'), 0, 0, tiled=True)  22.9 us
    ppermute x6, starting transfers between devices, swapped(): return lax.ppermute(value, axis, [(0, 1), (1, 0)])  15.5 us
    ppermute x6, waiting for transfers between devices, swapped(): return lax.ppermute(value, axis, [(0, 1), (1, 0)])  14 us
    pallas_call x1, Pallas kernels, merge(): pl.pallas_call(merge_kernel, in_specs=[smem(), hbm, hbm], out_specs=hbm,...  9.06 us
    ppermute x1, waiting for transfers between devices, placed(): return lax.ppermute(value, AXES, pairs)  5.82 us
    pallas_call x1, Pallas kernels, attend(): pl.pallas_call(attend_kernel, in_specs=[smem(), vmem(), vmem(), vmem(), v...  5.45 us
    ppermute x1, starting transfers between devices, placed(): return lax.ppermute(value, AXES, pairs)  4.04 us
  transfers between devices with their start and end apart: 8, of which 8 were waited for; matrix products, arithmetic and copies ran while one was open for 2% of the time, Pallas kernels for 5%

profile of v10, /device:TPU:6, one launch (start us, length us, event | category | flops | bytes accessed | tf_op | source)
XLA Modules:
  0.0 150.5 jit_solution(7015585220700379845)
XLA Ops:
  6.5 2.2 %collective-permute-start = (bf16[512,256]{1,0:T(8,128)(2,1)}, bf16[512,256]{1,0:T(8,128)(2,1)}, u32[]{:S(2)}, u32[]{:S(2)}) collective-permute-start(bf16[512,256]{1,0:T(8,128)(2,1)} %own_ref.1), channel_id=1, source_target_pairs={{0,1},{1,0},{2,3},{3,2},{4,5},{5,4},{6,7},{7,6},{8,9},{9,8},{10,11... | collective-permute-start | bytes 786440 | tf_op jit(solution)/shard_map/ppermute | solution.py:32
  8.7 1.1 prepare.1.q_ref
  9.9 0.7 collective-permute-done.got_ref
  10.6 9.1 %merge.1 = bf16[1024,128]{1,0:T(8,128)(2,1)} custom-call(s32[1]{0:T(128)} %bitcast.core_ref, bf16[512,256]{1,0:T(8,128)(2,1)} %own_ref.1, bf16[512,256]{1,0:T(8,128)(2,1)} %collective-permute-done.got_ref), custom_call_target="tpu_custom_call" | custom-call | tf_op jit(solution)/shard_map/merge/pallas_call | solution.py:223
  19.6 0.0 all-gather.4.cloned.1.call-update
  19.7 0.0 copy-start.1
  19.7 3.5 %collective-permute-start.1 = (bf16[136,512]{1,0:T(8,128)(2,1)S(1)}, bf16[136,512]{1,0:T(8,128)(2,1)}, u32[]{:S(2)}, u32[]{:S(2)}) collective-permute-start(bf16[136,512]{1,0:T(8,128)(2,1)S(1)} %prepare.1.q_ref), channel_id=1, source_target_pairs={{0,256},{256,0},{1,257},{257,1},{2,258},{258,2},{3,259},{259,3},{4... | collective-permute-start | bytes 417800 | tf_op jit(solution)/shard_map/ppermute | solution.py:32
  23.2 2.7 %fusion.1.x_ref = f32[200,128]{1,0:T(8,128)S(1)} fusion(bf16[200,8192]{1,0:T(8,128)(2,1)S(1)} %copy-done, bf16[128,8192]{1,0:T(8,128)(2,1)} %bitcast.34), kind=kOutput, calls=%fused_computation.5 | convolution fusion | flops 419430400 | bytes 5476352 | tf_op jit(solution)/shard_map/dot_general | solution.py:275
  25.9 1.5 %collective-permute-done.1.far_ref = bf16[136,512]{1,0:T(8,128)(2,1)} collective-permute-done((bf16[136,512]{1,0:T(8,128)(2,1)S(1)}, bf16[136,512]{1,0:T(8,128)(2,1)}, u32[]{:S(2)}, u32[]{:S(2)}) %collective-permute-start.1) | collective-permute-done | bytes 139296 | tf_op jit(solution)/shard_map/ppermute | solution.py:32
  27.4 0.1 multiply_reduce_fusion
  27.5 1.9 %collective-permute-start.2 = (f32[200]{0:T(256)S(1)}, f32[200]{0:T(256)S(1)}, u32[]{:S(2)}, u32[]{:S(2)}) collective-permute-start(f32[200]{0:T(256)S(1)} %multiply_reduce_fusion), channel_id=1, source_target_pairs={{0,1},{1,0},{2,3},{3,2},{4,5},{5,4},{6,7},{7,6},{8,9},{9,8},{10,11... | collective-permute-start | bytes 2408 | tf_op jit(solution)/shard_map/ppermute | solution.py:32
  29.4 0.1 pad_add_fusion.place_ref
  29.5 1.0 collective-permute-done.2
  30.5 0.7 pack.1
  31.2 47.1 %all-gather.1 = bf16[3200,128]{1,0:T(8,128)(2,1)S(1)} all-gather(bf16[200,128]{1,0:T(8,128)(2,1)S(1)} %pack.1), channel_id=3, replica_groups=mesh['ylo'=2,'z'=16,'xh'=2,'xl'=2,'yhi'=2,'core'=2] {'z'}, dimensions={0}, use_global_device_ids=true | all-gather | bytes 870400 | tf_op jit(solution)/shard_map/all_gather | solution.py:282
  78.3 1.9 %collective-permute-start.3 = (bf16[16,200,128]{2,1,0:T(8,128)(2,1)S(1)}, bf16[16,200,128]{2,1,0:T(8,128)(2,1)S(1)}, u32[]{:S(2)}, u32[]{:S(2)}) collective-permute-start(bf16[16,200,128]{2,1,0:T(8,128)(2,1)S(1)} %bitcast.28), channel_id=1, source_target_pairs={{0,1},{1,0},{2,3},{3,2},{4,5},{5,4},{6,7},{7,6},{8,9},{9,8},{10,11... | collective-permute-start | bytes 2457608 | tf_op jit(solution)/shard_map/ppermute | solution.py:32
  80.2 2.3 %collective-permute-done.3.theirs_ref = bf16[16,200,128]{2,1,0:T(8,128)(2,1)S(1)} collective-permute-done((bf16[16,200,128]{2,1,0:T(8,128)(2,1)S(1)}, bf16[16,200,128]{2,1,0:T(8,128)(2,1)S(1)}, u32[]{:S(2)}, u32[]{:S(2)}) %collective-permute-start.3) | collective-permute-done | bytes 819232 | tf_op jit(solution)/shard_map/ppermute | solution.py:32
  82.5 5.5 %attend.1.near_ref = bf16[2,136,512]{2,1,0:T(8,128)(2,1)S(1)} custom-call(s32[6]{0:T(128)S(1)} %pad_add_fusion.place_ref, bf16[136,512]{1,0:T(8,128)(2,1)S(1)} %prepare.1.q_ref, bf16[136,512]{1,0:T(8,128)(2,1)} %collective-permute-done.1.far_ref, bf16[16,200,128]{2,1,0:T(8,128)(2,1)S(1)} %bitcast.29, bf16[16,200,128]{2,1,0:T(8,128)(2,1)S(1)} %collective-permute-done.3.theirs_ref), custom_call_target="tpu_custom_call" | custom-call | tf_op jit(solution)/shard_map/attend/pallas_call | solution.py:173
  88.0 4.1 %collective-permute-start.4 = (bf16[2,136,512]{2,1,0:T(8,128)(2,1)S(1)}, bf16[2,136,512]{2,1,0:T(8,128)(2,1)S(1)}, u32[]{:S(2)}, u32[]{:S(2)}) collective-permute-start(bf16[2,136,512]{2,1,0:T(8,128)(2,1)S(1)} %attend.1.near_ref), channel_id=1, source_target_pairs={{0,256},{256,0},{1,257},{257,1},{2,258},{258,2},{3,259},{259,3},{4... | collective-permute-start | bytes 835592 | tf_op jit(solution)/shard_map/ppermute | solution.py:32
  92.1 6.9 %collective-permute-done.4.far_ref = bf16[2,136,512]{2,1,0:T(8,128)(2,1)S(1)} collective-permute-done((bf16[2,136,512]{2,1,0:T(8,128)(2,1)S(1)}, bf16[2,136,512]{2,1,0:T(8,128)(2,1)S(1)}, u32[]{:S(2)}, u32[]{:S(2)}) %collective-permute-start.4) | collective-permute-done | bytes 278560 | tf_op jit(solution)/shard_map/ppermute | solution.py:32
  99.1 0.2 combine.1
  99.3 1.9 %collective-permute-start.5 = (bf16[256,512]{1,0:T(8,128)(2,1)S(1)}, bf16[256,512]{1,0:T(8,128)(2,1)S(1)}, u32[]{:S(2)}, u32[]{:S(2)}) collective-permute-start(bf16[256,512]{1,0:T(8,128)(2,1)S(1)} %combine.1), channel_id=1, source_target_pairs={{0,1},{1,0},{2,3},{3,2},{4,5},{5,4},{6,7},{7,6},{8,9},{9,8},{10,11... | collective-permute-start | bytes 786440 | tf_op jit(solution)/shard_map/ppermute | solution.py:32
  101.2 1.5 collective-permute-done.5
  102.7 0.9 pad_maximum_fusion
  103.6 2.7 %all-gather.4.cloned.1.call-done = bf16[16384,128]{1,0:T(8,128)(2,1)} async-done(((bf16[1024,128]{1,0:T(8,128)(2,1)}), bf16[16384,128]{1,0:T(8,128)(2,1)}) %all-gather.4.cloned.1.call-update) | async-done | bytes 4194320 | tf_op jit(solution)/shard_map/all_gather | solution.py:272
  106.3 3.6 %fusion = bf16[8,2,2,128,128]{4,3,1,2,0:T(8,128)(2,1)S(1)} fusion(bf16[8,2,1024,128,1]{3,2,4,1,0:T(8,128)(2,1)} %bitcast.38, bf16[2,128,1024,1,1]{2,1,0,4,3:T(8,128)(2,1)} %bitcast.35), kind=kOutput, calls=%fused_computation.1 | convolution fusion | flops 1074266112 | bytes 5767168 | tf_op jit(solution)/shard_map/rmk,jtkn->jrtnm/dot_general | solution.py:291
  109.9 0.1 copy.10
  110.0 22.9 %all_to_all.5.x_ref = bf16[16,2,128,128]{3,2,1,0:T(8,128)(2,1)S(1)} all-to-all(bf16[16,2,128,128]{3,2,1,0:T(8,128)(2,1)S(1)} %bitcast.33), channel_id=1, replica_groups=mesh['ylo'=2,'z'=16,'xh'=2,'xl'=2,'yhi'=2,'core'=2] {'xl','yhi','core','..., dimensions={0} | all-to-all | bytes 2097152 | tf_op jit(solution)/shard_map/all_to_all | solution.py:293
  132.9 0.2 reduce.1
  133.2 4.0 %collective-permute-start.6 = (bf16[128,512]{1,0:T(8,128)(2,1)S(1)}, bf16[128,512]{1,0:T(8,128)(2,1)S(1)}, u32[]{:S(2)}, u32[]{:S(2)}) collective-permute-start(bf16[128,512]{1,0:T(8,128)(2,1)S(1)} %reduce.1), channel_id=1, source_target_pairs={{0,0},{1,1},{2,2},{3,3},{4,4},{5,5},{6,6},{7,7},{8,256},{9,257},{1... | collective-permute-start | bytes 393224 | tf_op jit(solution)/shard_map/ppermute | solution.py:41
  137.2 5.8 %collective-permute-done.6 = bf16[128,512]{1,0:T(8,128)(2,1)S(1)} collective-permute-done((bf16[128,512]{1,0:T(8,128)(2,1)S(1)}, bf16[128,512]{1,0:T(8,128)(2,1)S(1)}, u32[]{:S(2)}, u32[]{:S(2)}) %collective-permute-start.6) | collective-permute-done | bytes 131104 | tf_op jit(solution)/shard_map/ppermute | solution.py:41
  143.0 0.7 copy.16
  (6 shorter events, 0.0 us)
Async XLA Ops:
  6.5 16.6 %copy-start = (bf16[200,8192]{1,0:T(8,128)(2,1)S(1)}, bf16[200,8192]{1,0:T(8,128)(2,1)}, u32[]{:S(2)}) copy-start(bf16[200,8192]{1,0:T(8,128)(2,1)} %param.9) | copy-start | bytes 9830404
  6.5 99.8 %all-gather.4.cloned.1.call-start = ((), (), s32[]{:S(2)}) async-start(), calls=%async_computation.1 | async-start | bytes 4456448 | tf_op jit(solution)/shard_map/all_gather | solution.py:272
  6.5 4.0 %collective-permute-start = (bf16[512,256]{1,0:T(8,128)(2,1)}, bf16[512,256]{1,0:T(8,128)(2,1)}, u32[]{:S(2)}, u32[]{:S(2)}) collective-permute-start(bf16[512,256]{1,0:T(8,128)(2,1)} %own_ref.1), channel_id=1, source_target_pairs={{0,1},{1,0},{2,3},{3,2},{4,5},{5,4},{6,7},{7,6},{8,9},{9,8},{10,11... | collective-permute-start | bytes 786440 | tf_op jit(solution)/shard_map/ppermute | solution.py:32
  19.7 9.8 %copy-start.2 = (s32[4]{0:T(128)S(1)}, s32[4]{0:T(128)}, u32[]{:S(2)}) copy-start(s32[4]{0:T(128)} %param.14) | copy-start | bytes 52
  19.7 10.9 %copy-start.1 = (f32[128]{0:T(128)S(1)}, f32[128]{0:T(128)}, u32[]{:S(2)}) copy-start(f32[128]{0:T(128)} %param.13) | copy-start | bytes 1540
  19.7 7.7 %collective-permute-start.1 = (bf16[136,512]{1,0:T(8,128)(2,1)S(1)}, bf16[136,512]{1,0:T(8,128)(2,1)}, u32[]{:S(2)}, u32[]{:S(2)}) collective-permute-start(bf16[136,512]{1,0:T(8,128)(2,1)S(1)} %prepare.1.q_ref), channel_id=1, source_target_pairs={{0,256},{256,0},{1,257},{257,1},{2,258},{258,2},{3,259},{259,3},{4... | collective-permute-start | bytes 417800 | tf_op jit(solution)/shard_map/ppermute | solution.py:32
  27.5 3.0 %collective-permute-start.2 = (f32[200]{0:T(256)S(1)}, f32[200]{0:T(256)S(1)}, u32[]{:S(2)}, u32[]{:S(2)}) collective-permute-start(f32[200]{0:T(256)S(1)} %multiply_reduce_fusion), channel_id=1, source_target_pairs={{0,1},{1,0},{2,3},{3,2},{4,5},{5,4},{6,7},{7,6},{8,9},{9,8},{10,11... | collective-permute-start | bytes 2408 | tf_op jit(solution)/shard_map/ppermute | solution.py:32
  78.3 4.2 %collective-permute-start.3 = (bf16[16,200,128]{2,1,0:T(8,128)(2,1)S(1)}, bf16[16,200,128]{2,1,0:T(8,128)(2,1)S(1)}, u32[]{:S(2)}, u32[]{:S(2)}) collective-permute-start(bf16[16,200,128]{2,1,0:T(8,128)(2,1)S(1)} %bitcast.28), channel_id=1, source_target_pairs={{0,1},{1,0},{2,3},{3,2},{4,5},{5,4},{6,7},{7,6},{8,9},{9,8},{10,11... | collective-permute-start | bytes 2457608 | tf_op jit(solution)/shard_map/ppermute | solution.py:32
  88.0 11.1 %collective-permute-start.4 = (bf16[2,136,512]{2,1,0:T(8,128)(2,1)S(1)}, bf16[2,136,512]{2,1,0:T(8,128)(2,1)S(1)}, u32[]{:S(2)}, u32[]{:S(2)}) collective-permute-start(bf16[2,136,512]{2,1,0:T(8,128)(2,1)S(1)} %attend.1.near_ref), channel_id=1, source_target_pairs={{0,256},{256,0},{1,257},{257,1},{2,258},{258,2},{3,259},{259,3},{4... | collective-permute-start | bytes 835592 | tf_op jit(solution)/shard_map/ppermute | solution.py:32
  99.3 3.4 %collective-permute-start.5 = (bf16[256,512]{1,0:T(8,128)(2,1)S(1)}, bf16[256,512]{1,0:T(8,128)(2,1)S(1)}, u32[]{:S(2)}, u32[]{:S(2)}) collective-permute-start(bf16[256,512]{1,0:T(8,128)(2,1)S(1)} %combine.1), channel_id=1, source_target_pairs={{0,1},{1,0},{2,3},{3,2},{4,5},{5,4},{6,7},{7,6},{8,9},{9,8},{10,11... | collective-permute-start | bytes 786440 | tf_op jit(solution)/shard_map/ppermute | solution.py:32
  133.2 9.9 %collective-permute-start.6 = (bf16[128,512]{1,0:T(8,128)(2,1)S(1)}, bf16[128,512]{1,0:T(8,128)(2,1)S(1)}, u32[]{:S(2)}, u32[]{:S(2)}) collective-permute-start(bf16[128,512]{1,0:T(8,128)(2,1)S(1)} %reduce.1), channel_id=1, source_target_pairs={{0,0},{1,1},{2,2},{3,3},{4,4},{5,5},{6,6},{7,7},{8,256},{9,257},{1... | collective-permute-start | bytes 393224 | tf_op jit(solution)/shard_map/ppermute | solution.py:41
Sparse Core Ops, SparseCore 0:
  19.8 86.4 all-gather.3

commit v11 on v6

--- a/solution.py
+++ b/solution.py
@@ -191,34 +191,28 @@
     )(near, far)
 
 
-def project_kernel(own_ref, other_hbm, w_hbm, o_hbm, a_s, w_s, o_s, in_sem, out_sem):
-    steps = BLOCKS // 2
-    other = pltpu.make_async_copy(other_hbm, a_s, in_sem.at[steps])
+def project_kernel(own_ref, other_hbm, w_hbm, o_ref, a_s, w_s, sem):
+    steps = BLOCKS // 4
+    other = pltpu.make_async_copy(other_hbm, a_s.at[:, pl.ds(WIDTH, WIDTH)], sem.at[steps])
     other.start()
-    fetch = [
-        pltpu.make_async_copy(
-            w_hbm.at[pl.ds(2 * step, 2)], w_s.at[pl.ds(2 * step, 2)], in_sem.at[step]
-        )
-        for step in range(steps)
-    ]
-    for copy in fetch:
-        copy.start()
+    for step in range(steps):
+        blocks = pl.ds(4 * step, 4)
+        pltpu.make_async_copy(w_hbm.at[blocks], w_s.at[blocks], sem.at[step]).start()
+    a_s[:, :WIDTH] = own_ref[...]
     other.wait()
-    attended = jnp.concatenate([own_ref[...], a_s[...]], axis=1)
-    drain = []
-    for step in range(steps):
-        fetch[step].wait()
-        weight = jnp.concatenate([w_s[2 * step], w_s[2 * step + 1]], axis=1)
-        result = jnp.dot(attended, weight, preferred_element_type=F32).astype(BF)
-        o_s[step, 0] = result[:ROWS]
-        o_s[step, 1] = result[ROWS:]
-        copy = pltpu.make_async_copy(
-            o_s.at[step], o_hbm.at[:, step // 2, step % 2], out_sem.at[step]
-        )
-        copy.start()
-        drain.append(copy)
-    for copy in drain:
-        copy.wait()
+
+    def body(step, carry):
+        blocks = pl.ds(4 * step, 4)
+        pltpu.make_async_copy(w_hbm.at[blocks], w_s.at[blocks], sem.at[step]).wait()
+        for index in range(2):
+            block = 4 * step + 2 * index
+            weight = jnp.concatenate([w_s[block], w_s[block + 1]], axis=1)
+            result = jnp.dot(a_s[...], weight, preferred_element_type=F32).astype(BF)
+            o_ref[0, 2 * step + index] = result[:ROWS]
+            o_ref[1, 2 * step + index] = result[ROWS:]
+        return carry
+
+    lax.fori_loop(0, steps, body, 0)
 
 
 def project(own, other, weight):
@@ -226,14 +220,12 @@
     return pl.pallas_call(
         project_kernel,
         in_specs=[vmem(), hbm, hbm],
-        out_specs=hbm,
-        out_shape=jax.ShapeDtypeStruct((2, 4, 2, ROWS, 2 * HD), BF),
+        out_specs=vmem(),
+        out_shape=jax.ShapeDtypeStruct((2, 8, ROWS, 2 * HD), BF),
         scratch_shapes=[
-            pltpu.VMEM((2 * ROWS, WIDTH), BF),
+            pltpu.VMEM((2 * ROWS, 2 * WIDTH), BF),
             pltpu.VMEM((BLOCKS, 2 * WIDTH, HD), BF),
-            pltpu.VMEM((8, 2, ROWS, 2 * HD), BF),
-            pltpu.SemaphoreType.DMA((9,)),
-            pltpu.SemaphoreType.DMA((8,)),
+            pltpu.SemaphoreType.DMA((5,)),
         ],
         compiler_params=params(12),
         name="project",

time: 145 us -> 143 us (0.986)
  Pallas kernels: 12.9 us -> 10.7 us
    pallas_call x1, Pallas kernels: 5.27 us -> 3.12 us  [project(): pl.pallas_call(project_kernel, in_specs=[vmem(), hbm, hbm], out_specs=vme...]
where the time goes in v11:
time: 143 us; the launch traced here: 142 us
  blocking collectives  70.1 us (49%)
  waiting for transfers between devices  24.3 us (17%)
  starting transfers between devices  17.7 us (12%)
  between operations  13.5 us (9%)
  Pallas kernels  10.7 us (7%)
  matrix products  2.65 us (2%)
  local copies, waits for them, and re-layouts  1.81 us (1%)
    all_gather x1, blocking collectives, local(): mine = lax.all_gather(local_pair, 'z', axis=0, tiled=False)  47.2 us
    all_to_all x1, blocking collectives, local(): parts = lax.all_to_all(product, ('x', 'yhi', 'core'), 0, 0, tiled=True)  22.8 us
    ppermute x6, waiting for transfers between devices, swapped(): return lax.ppermute(value, axis, [(0, 1), (1, 0)])  15.5 us
    ppermute x6, starting transfers between devices, swapped(): return lax.ppermute(value, axis, [(0, 1), (1, 0)])  14.7 us
    ppermute x1, waiting for transfers between devices, placed(): return lax.ppermute(value, AXES, pairs)  6.24 us
    pallas_call x1, Pallas kernels, attend(): pl.pallas_call(attend_kernel, in_specs=[smem(), vmem(), vmem(), vmem(), v...  5.19 us
    pallas_call x1, Pallas kernels, project(): pl.pallas_call(project_kernel, in_specs=[vmem(), hbm, hbm], out_specs=vme...  3.12 us
    ppermute x1, starting transfers between devices, placed(): return lax.ppermute(value, AXES, pairs)  3.02 us
  transfers between devices with their start and end apart: 8, of which 8 were waited for; matrix products, arithmetic and copies ran while one was open for 2% of the time, Pallas kernels for 5%

profile of v11, /device:TPU:6, one launch (start us, length us, event | category | flops | bytes accessed | tf_op | source)
XLA Modules:
  0.0 141.6 jit_solution(3183891649937891397)
XLA Ops:
  6.5 1.1 constant_dynamic-slice_fusion
  7.7 1.9 %collective-permute-start = (bf16[512,128]{1,0:T(8,128)(2,1)S(1)}, bf16[512,128]{1,0:T(8,128)(2,1)S(1)}, u32[]{:S(2)}, u32[]{:S(2)}) collective-permute-start(bf16[512,128]{1,0:T(8,128)(2,1)S(1)} %get-tuple-element.14), channel_id=1, source_target_pairs={{0,1},{1,0},{2,3},{3,2},{4,5},{5,4},{6,7},{7,6},{8,9},{9,8},{10,11... | collective-permute-start | bytes 393224 | tf_op jit(solution)/shard_map/ppermute | solution.py:31
  9.6 1.2 prepare.1.q_ref
  10.8 0.1 collective-permute-done
  10.9 0.7 pad_maximum_fusion
  11.6 0.0 all-gather.4.cloned.1.call-update
  11.7 0.0 copy-start.2
  11.7 0.0 copy-start.1
  11.7 3.5 %collective-permute-start.1 = (bf16[128,640]{1,0:T(8,128)(2,1)S(1)}, bf16[128,640]{1,0:T(8,128)(2,1)}, u32[]{:S(2)}, u32[]{:S(2)}) collective-permute-start(bf16[128,640]{1,0:T(8,128)(2,1)S(1)} %prepare.1.q_ref), channel_id=1, source_target_pairs={{0,256},{256,0},{1,257},{257,1},{2,258},{258,2},{3,259},{259,3},{4... | collective-permute-start | bytes 491528 | tf_op jit(solution)/shard_map/ppermute | solution.py:31
  15.2 2.7 %fusion.x_ref = f32[200,128]{1,0:T(8,128)S(1)} fusion(bf16[200,8192]{1,0:T(8,128)(2,1)S(1)} %copy-done, bf16[128,8192]{1,0:T(8,128)(2,1)} %bitcast.22), kind=kOutput, calls=%fused_computation.5 | convolution fusion | flops 419430400 | bytes 5476352 | tf_op jit(solution)/shard_map/dot_general | solution.py:277
  17.9 2.3 %collective-permute-done.1.far_ref = bf16[128,640]{1,0:T(8,128)(2,1)} collective-permute-done((bf16[128,640]{1,0:T(8,128)(2,1)S(1)}, bf16[128,640]{1,0:T(8,128)(2,1)}, u32[]{:S(2)}, u32[]{:S(2)}) %collective-permute-start.1) | collective-permute-done | bytes 163872 | tf_op jit(solution)/shard_map/ppermute | solution.py:31
  20.2 0.1 multiply_reduce_fusion
  20.3 1.9 %collective-permute-start.2 = (f32[200]{0:T(256)S(1)}, f32[200]{0:T(256)S(1)}, u32[]{:S(2)}, u32[]{:S(2)}) collective-permute-start(f32[200]{0:T(256)S(1)} %multiply_reduce_fusion), channel_id=1, source_target_pairs={{0,1},{1,0},{2,3},{3,2},{4,5},{5,4},{6,7},{7,6},{8,9},{9,8},{10,11... | collective-permute-start | bytes 2408 | tf_op jit(solution)/shard_map/ppermute | solution.py:31
  22.2 0.1 pad_add_fusion.place_ref
  22.3 1.0 collective-permute-done.2
  23.3 0.7 pack.1
  24.0 47.2 %all-gather = bf16[3200,128]{1,0:T(8,128)(2,1)S(1)} all-gather(bf16[200,128]{1,0:T(8,128)(2,1)S(1)} %pack.1), channel_id=2, replica_groups=mesh['ylo'=2,'z'=16,'x'=4,'yhi'=2,'core'=2] {'z'}, dimensions={0}, use_global_device_ids=true | all-gather | bytes 870400 | tf_op jit(solution)/shard_map/all_gather | solution.py:284
  71.2 1.9 %collective-permute-start.3 = (bf16[16,200,128]{2,1,0:T(8,128)(2,1)S(1)}, bf16[16,200,128]{2,1,0:T(8,128)(2,1)S(1)}, u32[]{:S(2)}, u32[]{:S(2)}) collective-permute-start(bf16[16,200,128]{2,1,0:T(8,128)(2,1)S(1)} %bitcast.16), channel_id=1, source_target_pairs={{0,1},{1,0},{2,3},{3,2},{4,5},{5,4},{6,7},{7,6},{8,9},{9,8},{10,11... | collective-permute-start | bytes 2457608 | tf_op jit(solution)/shard_map/ppermute | solution.py:31
  73.2 2.3 %collective-permute-done.3.theirs_ref = bf16[16,200,128]{2,1,0:T(8,128)(2,1)S(1)} collective-permute-done((bf16[16,200,128]{2,1,0:T(8,128)(2,1)S(1)}, bf16[16,200,128]{2,1,0:T(8,128)(2,1)S(1)}, u32[]{:S(2)}, u32[]{:S(2)}) %collective-permute-start.3) | collective-permute-done | bytes 819232 | tf_op jit(solution)/shard_map/ppermute | solution.py:31
  75.5 5.2 %attend.1.near_ref = bf16[2,128,640]{2,1,0:T(8,128)(2,1)S(1)} custom-call(s32[6]{0:T(128)S(1)} %pad_add_fusion.place_ref, bf16[128,640]{1,0:T(8,128)(2,1)S(1)} %prepare.1.q_ref, bf16[128,640]{1,0:T(8,128)(2,1)} %collective-permute-done.1.far_ref, bf16[16,200,128]{2,1,0:T(8,128)(2,1)S(1)} %bitcast.17, bf16[16,200,128]{2,1,0:T(8,128)(2,1)S(1)} %collective-permute-done.3.theirs_ref), custom_call_target="tpu_custom_call" | custom-call | tf_op jit(solution)/shard_map/attend/pallas_call | solution.py:161
  80.7 3.5 %collective-permute-start.4 = (bf16[2,128,640]{2,1,0:T(8,128)(2,1)S(1)}, bf16[2,128,640]{2,1,0:T(8,128)(2,1)S(1)}, u32[]{:S(2)}, u32[]{:S(2)}) collective-permute-start(bf16[2,128,640]{2,1,0:T(8,128)(2,1)S(1)} %attend.1.near_ref), channel_id=1, source_target_pairs={{0,256},{256,0},{1,257},{257,1},{2,258},{258,2},{3,259},{259,3},{4... | collective-permute-start | bytes 983048 | tf_op jit(solution)/shard_map/ppermute | solution.py:31
  84.2 8.1 %collective-permute-done.4.far_ref = bf16[2,128,640]{2,1,0:T(8,128)(2,1)S(1)} collective-permute-done((bf16[2,128,640]{2,1,0:T(8,128)(2,1)S(1)}, bf16[2,128,640]{2,1,0:T(8,128)(2,1)S(1)}, u32[]{:S(2)}, u32[]{:S(2)}) %collective-permute-start.4) | collective-permute-done | bytes 327712 | tf_op jit(solution)/shard_map/ppermute | solution.py:31
  92.3 0.4 combine.1.own_ref
  92.7 1.9 %collective-permute-start.5 = (bf16[256,512]{1,0:T(8,128)(2,1)S(1)}, bf16[256,512]{1,0:T(8,128)(2,1)}, u32[]{:S(2)}, u32[]{:S(2)}) collective-permute-start(bf16[256,512]{1,0:T(8,128)(2,1)S(1)} %combine.1.own_ref), channel_id=1, source_target_pairs={{0,1},{1,0},{2,3},{3,2},{4,5},{5,4},{6,7},{7,6},{8,9},{9,8},{10,11... | collective-permute-start | bytes 786440 | tf_op jit(solution)/shard_map/ppermute | solution.py:31
  94.6 1.6 %collective-permute-done.5.other_hbm = bf16[256,512]{1,0:T(8,128)(2,1)} collective-permute-done((bf16[256,512]{1,0:T(8,128)(2,1)S(1)}, bf16[256,512]{1,0:T(8,128)(2,1)}, u32[]{:S(2)}, u32[]{:S(2)}) %collective-permute-start.5) | collective-permute-done | bytes 262176 | tf_op jit(solution)/shard_map/ppermute | solution.py:31
  96.3 2.5 %all-gather.4.cloned.1.call-done = bf16[16384,128]{1,0:T(8,128)(2,1)} async-done(((bf16[1024,128]{1,0:T(8,128)(2,1)}), bf16[16384,128]{1,0:T(8,128)(2,1)}) %all-gather.4.cloned.1.call-update) | async-done | bytes 4194320 | tf_op jit(solution)/shard_map/all_gather | solution.py:274
  98.8 3.1 %project.1 = bf16[2,8,128,256]{3,2,1,0:T(8,128)(2,1)S(1)} custom-call(bf16[256,512]{1,0:T(8,128)(2,1)S(1)} %combine.1.own_ref, bf16[256,512]{1,0:T(8,128)(2,1)} %collective-permute-done.5.other_hbm, bf16[16,1024,128]{2,1,0:T(8,128)(2,1)} %bitcast.21), custom_call_target="tpu_custom_call" | custom-call | tf_op jit(solution)/shard_map/project/pallas_call | solution.py:220
  101.9 22.8 %all_to_all.5.x_ref = bf16[16,128,256]{2,1,0:T(8,128)(2,1)S(1)} all-to-all(bf16[16,128,256]{2,1,0:T(8,128)(2,1)S(1)} %bitcast.15), channel_id=1, replica_groups=mesh['ylo'=2,'z'=16,'x'=4,'yhi'=2,'core'=2] {'x','yhi','core'}, dimensions={0} | all-to-all | bytes 2097152 | tf_op jit(solution)/shard_map/all_to_all | solution.py:292
  124.7 0.1 reduce.1
  124.9 3.0 %collective-permute-start.6 = (bf16[128,512]{1,0:T(8,128)(2,1)S(1)}, bf16[128,512]{1,0:T(8,128)(2,1)S(1)}, u32[]{:S(2)}, u32[]{:S(2)}) collective-permute-start(bf16[128,512]{1,0:T(8,128)(2,1)S(1)} %reduce.1), channel_id=1, source_target_pairs={{0,0},{1,1},{2,2},{3,3},{4,4},{5,5},{6,6},{7,7},{8,256},{9,257},{1... | collective-permute-start | bytes 393224 | tf_op jit(solution)/shard_map/ppermute | solution.py:40
  127.9 6.2 %collective-permute-done.6 = bf16[128,512]{1,0:T(8,128)(2,1)S(1)} collective-permute-done((bf16[128,512]{1,0:T(8,128)(2,1)S(1)}, bf16[128,512]{1,0:T(8,128)(2,1)S(1)}, u32[]{:S(2)}, u32[]{:S(2)}) %collective-permute-start.6) | collective-permute-done | bytes 131104 | tf_op jit(solution)/shard_map/ppermute | solution.py:40
  134.1 0.7 copy.10
  (5 shorter events, 0.0 us)
Async XLA Ops:
  6.5 8.7 %copy-start = (bf16[200,8192]{1,0:T(8,128)(2,1)S(1)}, bf16[200,8192]{1,0:T(8,128)(2,1)}, u32[]{:S(2)}) copy-start(bf16[200,8192]{1,0:T(8,128)(2,1)} %param.9) | copy-start | bytes 9830404
  6.5 92.2 %all-gather.4.cloned.1.call-start = ((), (), s32[]{:S(2)}) async-start(), calls=%async_computation.1 | async-start | bytes 4456448 | tf_op jit(solution)/shard_map/all_gather | solution.py:274
  7.7 3.2 %collective-permute-start = (bf16[512,128]{1,0:T(8,128)(2,1)S(1)}, bf16[512,128]{1,0:T(8,128)(2,1)S(1)}, u32[]{:S(2)}, u32[]{:S(2)}) collective-permute-start(bf16[512,128]{1,0:T(8,128)(2,1)S(1)} %get-tuple-element.14), channel_id=1, source_target_pairs={{0,1},{1,0},{2,3},{3,2},{4,5},{5,4},{6,7},{7,6},{8,9},{9,8},{10,11... | collective-permute-start | bytes 393224 | tf_op jit(solution)/shard_map/ppermute | solution.py:31
  11.7 10.5 %copy-start.2 = (s32[4]{0:T(128)S(1)}, s32[4]{0:T(128)}, u32[]{:S(2)}) copy-start(s32[4]{0:T(128)} %param.14) | copy-start | bytes 52
  11.7 11.6 %copy-start.1 = (f32[128]{0:T(128)S(1)}, f32[128]{0:T(128)}, u32[]{:S(2)}) copy-start(f32[128]{0:T(128)} %param.13) | copy-start | bytes 1540
  11.7 8.5 %collective-permute-start.1 = (bf16[128,640]{1,0:T(8,128)(2,1)S(1)}, bf16[128,640]{1,0:T(8,128)(2,1)}, u32[]{:S(2)}, u32[]{:S(2)}) collective-permute-start(bf16[128,640]{1,0:T(8,128)(2,1)S(1)} %prepare.1.q_ref), channel_id=1, source_target_pairs={{0,256},{256,0},{1,257},{257,1},{2,258},{258,2},{3,259},{259,3},{4... | collective-permute-start | bytes 491528 | tf_op jit(solution)/shard_map/ppermute | solution.py:31
  20.3 3.0 %collective-permute-start.2 = (f32[200]{0:T(256)S(1)}, f32[200]{0:T(256)S(1)}, u32[]{:S(2)}, u32[]{:S(2)}) collective-permute-start(f32[200]{0:T(256)S(1)} %multiply_reduce_fusion), channel_id=1, source_target_pairs={{0,1},{1,0},{2,3},{3,2},{4,5},{5,4},{6,7},{7,6},{8,9},{9,8},{10,11... | collective-permute-start | bytes 2408 | tf_op jit(solution)/shard_map/ppermute | solution.py:31
  71.2 4.2 %collective-permute-start.3 = (bf16[16,200,128]{2,1,0:T(8,128)(2,1)S(1)}, bf16[16,200,128]{2,1,0:T(8,128)(2,1)S(1)}, u32[]{:S(2)}, u32[]{:S(2)}) collective-permute-start(bf16[16,200,128]{2,1,0:T(8,128)(2,1)S(1)} %bitcast.16), channel_id=1, source_target_pairs={{0,1},{1,0},{2,3},{3,2},{4,5},{5,4},{6,7},{7,6},{8,9},{9,8},{10,11... | collective-permute-start | bytes 2457608 | tf_op jit(solution)/shard_map/ppermute | solution.py:31
  80.7 11.6 %collective-permute-start.4 = (bf16[2,128,640]{2,1,0:T(8,128)(2,1)S(1)}, bf16[2,128,640]{2,1,0:T(8,128)(2,1)S(1)}, u32[]{:S(2)}, u32[]{:S(2)}) collective-permute-start(bf16[2,128,640]{2,1,0:T(8,128)(2,1)S(1)} %attend.1.near_ref), channel_id=1, source_target_pairs={{0,256},{256,0},{1,257},{257,1},{2,258},{258,2},{3,259},{259,3},{4... | collective-permute-start | bytes 983048 | tf_op jit(solution)/shard_map/ppermute | solution.py:31
  92.7 3.6 %collective-permute-start.5 = (bf16[256,512]{1,0:T(8,128)(2,1)S(1)}, bf16[256,512]{1,0:T(8,128)(2,1)}, u32[]{:S(2)}, u32[]{:S(2)}) collective-permute-start(bf16[256,512]{1,0:T(8,128)(2,1)S(1)} %combine.1.own_ref), channel_id=1, source_target_pairs={{0,1},{1,0},{2,3},{3,2},{4,5},{5,4},{6,7},{7,6},{8,9},{9,8},{10,11... | collective-permute-start | bytes 786440 | tf_op jit(solution)/shard_map/ppermute | solution.py:31
  124.9 9.3 %collective-permute-start.6 = (bf16[128,512]{1,0:T(8,128)(2,1)S(1)}, bf16[128,512]{1,0:T(8,128)(2,1)S(1)}, u32[]{:S(2)}, u32[]{:S(2)}) collective-permute-start(bf16[128,512]{1,0:T(8,128)(2,1)S(1)} %reduce.1), channel_id=1, source_target_pairs={{0,0},{1,1},{2,2},{3,3},{4,4},{5,5},{6,6},{7,7},{8,256},{9,257},{1... | collective-permute-start | bytes 393224 | tf_op jit(solution)/shard_map/ppermute | solution.py:40
Sparse Core Ops, SparseCore 0:
  11.8 86.9 all-gather.3

commit v12 on v11

--- a/solution.py
+++ b/solution.py
@@ -35,7 +35,9 @@
     pairs = []
     for source in range(512):
         core, yhi, x, z = source % 2, source // 2 % 2, source // 4 % 4, source // 16 % 16
-        target = flat(x // 2, z, 2 * (source // 256) + x % 2, yhi, core)
+        ylo = source // 256
+        stays = x // 2 == ylo
+        target = source if stays else flat(1 - ylo, z, 3 - x, yhi, core)
         pairs.append((source, target))
     return lax.ppermute(value, AXES, pairs)
 
@@ -191,7 +193,7 @@
     )(near, far)
 
 
-def project_kernel(own_ref, other_hbm, w_hbm, o_ref, a_s, w_s, sem):
+def project_kernel(place_ref, own_ref, other_hbm, w_hbm, o_ref, a_s, w_s, sem):
     steps = BLOCKS // 4
     other = pltpu.make_async_copy(other_hbm, a_s.at[:, pl.ds(WIDTH, WIDTH)], sem.at[steps])
     other.start()
@@ -200,6 +202,7 @@
         pltpu.make_async_copy(w_hbm.at[blocks], w_s.at[blocks], sem.at[step]).start()
     a_s[:, :WIDTH] = own_ref[...]
     other.wait()
+    ylo = place_ref[1]
 
     def body(step, carry):
         blocks = pl.ds(4 * step, 4)
@@ -208,18 +211,19 @@
             block = 4 * step + 2 * index
             weight = jnp.concatenate([w_s[block], w_s[block + 1]], axis=1)
             result = jnp.dot(a_s[...], weight, preferred_element_type=F32).astype(BF)
-            o_ref[0, 2 * step + index] = result[:ROWS]
-            o_ref[1, 2 * step + index] = result[ROWS:]
+            group = 2 * step + index
+            o_ref[0, (group + 4 * ylo) & 7] = result[:ROWS]
+            o_ref[1, (group + 4 - 4 * ylo) & 7] = result[ROWS:]
         return carry
 
     lax.fori_loop(0, steps, body, 0)
 
 
-def project(own, other, weight):
+def project(place, own, other, weight):
     hbm = pl.BlockSpec(memory_space=pltpu.HBM)
     return pl.pallas_call(
         project_kernel,
-        in_specs=[vmem(), hbm, hbm],
+        in_specs=[smem(), vmem(), hbm, hbm],
         out_specs=vmem(),
         out_shape=jax.ShapeDtypeStruct((2, 8, ROWS, 2 * HD), BF),
         scratch_shapes=[
@@ -230,6 +234,7 @@
         compiler_params=params(12),
         name="project",
     )(
+        place,
         own,
         pltpu.with_memory_space_constraint(other, pltpu.HBM),
         pltpu.with_memory_space_constraint(weight, pltpu.HBM),
@@ -288,7 +293,7 @@
     own = combine(partial, swapped(partial, "ylo"))
     other = swapped(own, "core")
 
-    product = project(own, other, weight).reshape(16, ROWS, 2 * HD)
+    product = project(place, own, other, weight).reshape(16, ROWS, 2 * HD)
     parts = lax.all_to_all(product, ("x", "yhi", "core"), 0, 0, tiled=True)
     return placed(reduce(parts))
 

time: 143 us -> 143 us (level)
  no operation moved by 1% of the time
where the time goes in v12:
time: 143 us; the launch traced here: 142 us
  blocking collectives  70.1 us (49%)
  waiting for transfers between devices  23.1 us (16%)
  starting transfers between devices  18.6 us (13%)
  between operations  13.5 us (9%)
  Pallas kernels  11.3 us (8%)
  matrix products  2.65 us (2%)
  local copies, waits for them, and re-layouts  1.81 us (1%)
    all_gather x1, blocking collectives, local(): mine = lax.all_gather(local_pair, 'z', axis=0, tiled=False)  47.2 us
    all_to_all x1, blocking collectives, local(): parts = lax.all_to_all(product, ('x', 'yhi', 'core'), 0, 0, tiled=True)  22.8 us
    ppermute x6, waiting for transfers between devices, swapped(): return lax.ppermute(value, axis, [(0, 1), (1, 0)])  15.5 us
    ppermute x6, starting transfers between devices, swapped(): return lax.ppermute(value, axis, [(0, 1), (1, 0)])  14.6 us
    pallas_call x1, Pallas kernels, attend(): pl.pallas_call(attend_kernel, in_specs=[smem(), vmem(), vmem(), vmem(), v...  5.21 us
    ppermute x1, waiting for transfers between devices, placed(): return lax.ppermute(value, AXES, pairs)  5.03 us
    ppermute x1, starting transfers between devices, placed(): return lax.ppermute(value, AXES, pairs)  3.93 us
    pallas_call x1, Pallas kernels, project(): pl.pallas_call(project_kernel, in_specs=[smem(), vmem(), hbm, hbm], out_s...  3.66 us
  transfers between devices with their start and end apart: 8, of which 8 were waited for; matrix products, arithmetic and copies ran while one was open for 2% of the time, Pallas kernels for 5%

profile of v12, /device:TPU:6, one launch (start us, length us, event | category | flops | bytes accessed | tf_op | source)
XLA Modules:
  0.0 141.9 jit_solution(8501858939561633542)
XLA Ops:
  6.5 1.1 constant_dynamic-slice_fusion
  7.7 1.9 %collective-permute-start = (bf16[512,128]{1,0:T(8,128)(2,1)S(1)}, bf16[512,128]{1,0:T(8,128)(2,1)S(1)}, u32[]{:S(2)}, u32[]{:S(2)}) collective-permute-start(bf16[512,128]{1,0:T(8,128)(2,1)S(1)} %get-tuple-element.14), channel_id=1, source_target_pairs={{0,1},{1,0},{2,3},{3,2},{4,5},{5,4},{6,7},{7,6},{8,9},{9,8},{10,11... | collective-permute-start | bytes 393224 | tf_op jit(solution)/shard_map/ppermute | solution.py:31
  9.6 1.2 prepare.1.q_ref
  10.8 0.1 collective-permute-done
  10.9 0.7 pad_maximum_fusion
  11.6 0.0 all-gather.4.cloned.1.call-update
  11.7 0.0 copy-start.2
  11.7 0.0 copy-start.1
  11.7 3.5 %collective-permute-start.1 = (bf16[128,640]{1,0:T(8,128)(2,1)S(1)}, bf16[128,640]{1,0:T(8,128)(2,1)}, u32[]{:S(2)}, u32[]{:S(2)}) collective-permute-start(bf16[128,640]{1,0:T(8,128)(2,1)S(1)} %prepare.1.q_ref), channel_id=1, source_target_pairs={{0,256},{256,0},{1,257},{257,1},{2,258},{258,2},{3,259},{259,3},{4... | collective-permute-start | bytes 491528 | tf_op jit(solution)/shard_map/ppermute | solution.py:31
  15.2 2.7 %fusion.x_ref = f32[200,128]{1,0:T(8,128)S(1)} fusion(bf16[200,8192]{1,0:T(8,128)(2,1)S(1)} %copy-done, bf16[128,8192]{1,0:T(8,128)(2,1)} %bitcast.22), kind=kOutput, calls=%fused_computation.5 | convolution fusion | flops 419430400 | bytes 5476352 | tf_op jit(solution)/shard_map/dot_general | solution.py:282
  17.9 2.3 %collective-permute-done.1.far_ref = bf16[128,640]{1,0:T(8,128)(2,1)} collective-permute-done((bf16[128,640]{1,0:T(8,128)(2,1)S(1)}, bf16[128,640]{1,0:T(8,128)(2,1)}, u32[]{:S(2)}, u32[]{:S(2)}) %collective-permute-start.1) | collective-permute-done | bytes 163872 | tf_op jit(solution)/shard_map/ppermute | solution.py:31
  20.2 0.1 multiply_reduce_fusion
  20.3 1.9 %collective-permute-start.2 = (f32[200]{0:T(256)S(1)}, f32[200]{0:T(256)S(1)}, u32[]{:S(2)}, u32[]{:S(2)}) collective-permute-start(f32[200]{0:T(256)S(1)} %multiply_reduce_fusion), channel_id=1, source_target_pairs={{0,1},{1,0},{2,3},{3,2},{4,5},{5,4},{6,7},{7,6},{8,9},{9,8},{10,11... | collective-permute-start | bytes 2408 | tf_op jit(solution)/shard_map/ppermute | solution.py:31
  22.2 0.1 pad_add_fusion.place_ref
  22.3 1.0 collective-permute-done.2
  23.3 0.7 pack.1
  24.0 47.2 %all-gather = bf16[3200,128]{1,0:T(8,128)(2,1)S(1)} all-gather(bf16[200,128]{1,0:T(8,128)(2,1)S(1)} %pack.1), channel_id=2, replica_groups=mesh['ylo'=2,'z'=16,'x'=4,'yhi'=2,'core'=2] {'z'}, dimensions={0}, use_global_device_ids=true | all-gather | bytes 870400 | tf_op jit(solution)/shard_map/all_gather | solution.py:289
  71.2 1.9 %collective-permute-start.3 = (bf16[16,200,128]{2,1,0:T(8,128)(2,1)S(1)}, bf16[16,200,128]{2,1,0:T(8,128)(2,1)S(1)}, u32[]{:S(2)}, u32[]{:S(2)}) collective-permute-start(bf16[16,200,128]{2,1,0:T(8,128)(2,1)S(1)} %bitcast.16), channel_id=1, source_target_pairs={{0,1},{1,0},{2,3},{3,2},{4,5},{5,4},{6,7},{7,6},{8,9},{9,8},{10,11... | collective-permute-start | bytes 2457608 | tf_op jit(solution)/shard_map/ppermute | solution.py:31
  73.2 2.3 %collective-permute-done.3.theirs_ref = bf16[16,200,128]{2,1,0:T(8,128)(2,1)S(1)} collective-permute-done((bf16[16,200,128]{2,1,0:T(8,128)(2,1)S(1)}, bf16[16,200,128]{2,1,0:T(8,128)(2,1)S(1)}, u32[]{:S(2)}, u32[]{:S(2)}) %collective-permute-start.3) | collective-permute-done | bytes 819232 | tf_op jit(solution)/shard_map/ppermute | solution.py:31
  75.5 5.2 %attend.1.near_ref = bf16[2,128,640]{2,1,0:T(8,128)(2,1)S(1)} custom-call(s32[6]{0:T(128)S(1)} %pad_add_fusion.place_ref, bf16[128,640]{1,0:T(8,128)(2,1)S(1)} %prepare.1.q_ref, bf16[128,640]{1,0:T(8,128)(2,1)} %collective-permute-done.1.far_ref, bf16[16,200,128]{2,1,0:T(8,128)(2,1)S(1)} %bitcast.17, bf16[16,200,128]{2,1,0:T(8,128)(2,1)S(1)} %collective-permute-done.3.theirs_ref), custom_call_target="tpu_custom_call" | custom-call | tf_op jit(solution)/shard_map/attend/pallas_call | solution.py:163
  80.7 3.5 %collective-permute-start.4 = (bf16[2,128,640]{2,1,0:T(8,128)(2,1)S(1)}, bf16[2,128,640]{2,1,0:T(8,128)(2,1)S(1)}, u32[]{:S(2)}, u32[]{:S(2)}) collective-permute-start(bf16[2,128,640]{2,1,0:T(8,128)(2,1)S(1)} %attend.1.near_ref), channel_id=1, source_target_pairs={{0,256},{256,0},{1,257},{257,1},{2,258},{258,2},{3,259},{259,3},{4... | collective-permute-start | bytes 983048 | tf_op jit(solution)/shard_map/ppermute | solution.py:31
  84.2 8.2 %collective-permute-done.4.far_ref = bf16[2,128,640]{2,1,0:T(8,128)(2,1)S(1)} collective-permute-done((bf16[2,128,640]{2,1,0:T(8,128)(2,1)S(1)}, bf16[2,128,640]{2,1,0:T(8,128)(2,1)S(1)}, u32[]{:S(2)}, u32[]{:S(2)}) %collective-permute-start.4) | collective-permute-done | bytes 327712 | tf_op jit(solution)/shard_map/ppermute | solution.py:31
  92.3 0.4 combine.1.own_ref
  92.7 1.9 %collective-permute-start.5 = (bf16[256,512]{1,0:T(8,128)(2,1)S(1)}, bf16[256,512]{1,0:T(8,128)(2,1)}, u32[]{:S(2)}, u32[]{:S(2)}) collective-permute-start(bf16[256,512]{1,0:T(8,128)(2,1)S(1)} %combine.1.own_ref), channel_id=1, source_target_pairs={{0,1},{1,0},{2,3},{3,2},{4,5},{5,4},{6,7},{7,6},{8,9},{9,8},{10,11... | collective-permute-start | bytes 786440 | tf_op jit(solution)/shard_map/ppermute | solution.py:31
  94.7 1.6 %collective-permute-done.5.other_hbm = bf16[256,512]{1,0:T(8,128)(2,1)} collective-permute-done((bf16[256,512]{1,0:T(8,128)(2,1)S(1)}, bf16[256,512]{1,0:T(8,128)(2,1)}, u32[]{:S(2)}, u32[]{:S(2)}) %collective-permute-start.5) | collective-permute-done | bytes 262176 | tf_op jit(solution)/shard_map/ppermute | solution.py:31
  96.3 2.5 %all-gather.4.cloned.1.call-done = bf16[16384,128]{1,0:T(8,128)(2,1)} async-done(((bf16[1024,128]{1,0:T(8,128)(2,1)}), bf16[16384,128]{1,0:T(8,128)(2,1)}) %all-gather.4.cloned.1.call-update) | async-done | bytes 4194320 | tf_op jit(solution)/shard_map/all_gather | solution.py:279
  98.8 3.7 %project.1 = bf16[2,8,128,256]{3,2,1,0:T(8,128)(2,1)S(1)} custom-call(s32[6]{0:T(128)S(1)} %pad_add_fusion.place_ref, bf16[256,512]{1,0:T(8,128)(2,1)S(1)} %combine.1.own_ref, bf16[256,512]{1,0:T(8,128)(2,1)} %collective-permute-done.5.other_hbm, bf16[16,1024,128]{2,1,0:T(8,128)(2,1)} %bitcast.21), custom_call_target="tpu_custom_call" | custom-call | tf_op jit(solution)/shard_map/project/pallas_call | solution.py:224
  102.4 22.8 %all_to_all.5.x_ref = bf16[16,128,256]{2,1,0:T(8,128)(2,1)S(1)} all-to-all(bf16[16,128,256]{2,1,0:T(8,128)(2,1)S(1)} %bitcast.15), channel_id=1, replica_groups=mesh['ylo'=2,'z'=16,'x'=4,'yhi'=2,'core'=2] {'x','yhi','core'}, dimensions={0} | all-to-all | bytes 2097152 | tf_op jit(solution)/shard_map/all_to_all | solution.py:297
  125.3 0.1 reduce.1
  125.4 3.9 %collective-permute-start.6 = (bf16[128,512]{1,0:T(8,128)(2,1)S(1)}, bf16[128,512]{1,0:T(8,128)(2,1)S(1)}, u32[]{:S(2)}, u32[]{:S(2)}) collective-permute-start(bf16[128,512]{1,0:T(8,128)(2,1)S(1)} %reduce.1), channel_id=1, source_target_pairs={{0,0},{1,1},{2,2},{3,3},{4,4},{5,5},{6,6},{7,7},{8,260},{9,261},{1... | collective-permute-start | bytes 393224 | tf_op jit(solution)/shard_map/ppermute | solution.py:42
  129.3 5.0 %collective-permute-done.6 = bf16[128,512]{1,0:T(8,128)(2,1)S(1)} collective-permute-done((bf16[128,512]{1,0:T(8,128)(2,1)S(1)}, bf16[128,512]{1,0:T(8,128)(2,1)S(1)}, u32[]{:S(2)}, u32[]{:S(2)}) %collective-permute-start.6) | collective-permute-done | bytes 131104 | tf_op jit(solution)/shard_map/ppermute | solution.py:42
  134.4 0.7 copy.10
  (5 shorter events, 0.0 us)
Async XLA Ops:
  6.5 8.7 %copy-start = (bf16[200,8192]{1,0:T(8,128)(2,1)S(1)}, bf16[200,8192]{1,0:T(8,128)(2,1)}, u32[]{:S(2)}) copy-start(bf16[200,8192]{1,0:T(8,128)(2,1)} %param.9) | copy-start | bytes 9830404
  6.5 92.2 %all-gather.4.cloned.1.call-start = ((), (), s32[]{:S(2)}) async-start(), calls=%async_computation.1 | async-start | bytes 4456448 | tf_op jit(solution)/shard_map/all_gather | solution.py:279
  7.7 3.2 %collective-permute-start = (bf16[512,128]{1,0:T(8,128)(2,1)S(1)}, bf16[512,128]{1,0:T(8,128)(2,1)S(1)}, u32[]{:S(2)}, u32[]{:S(2)}) collective-permute-start(bf16[512,128]{1,0:T(8,128)(2,1)S(1)} %get-tuple-element.14), channel_id=1, source_target_pairs={{0,1},{1,0},{2,3},{3,2},{4,5},{5,4},{6,7},{7,6},{8,9},{9,8},{10,11... | collective-permute-start | bytes 393224 | tf_op jit(solution)/shard_map/ppermute | solution.py:31
  11.7 10.5 %copy-start.2 = (s32[4]{0:T(128)S(1)}, s32[4]{0:T(128)}, u32[]{:S(2)}) copy-start(s32[4]{0:T(128)} %param.14) | copy-start | bytes 52
  11.7 11.6 %copy-start.1 = (f32[128]{0:T(128)S(1)}, f32[128]{0:T(128)}, u32[]{:S(2)}) copy-start(f32[128]{0:T(128)} %param.13) | copy-start | bytes 1540
  11.7 8.5 %collective-permute-start.1 = (bf16[128,640]{1,0:T(8,128)(2,1)S(1)}, bf16[128,640]{1,0:T(8,128)(2,1)}, u32[]{:S(2)}, u32[]{:S(2)}) collective-permute-start(bf16[128,640]{1,0:T(8,128)(2,1)S(1)} %prepare.1.q_ref), channel_id=1, source_target_pairs={{0,256},{256,0},{1,257},{257,1},{2,258},{258,2},{3,259},{259,3},{4... | collective-permute-start | bytes 491528 | tf_op jit(solution)/shard_map/ppermute | solution.py:31
  20.3 3.0 %collective-permute-start.2 = (f32[200]{0:T(256)S(1)}, f32[200]{0:T(256)S(1)}, u32[]{:S(2)}, u32[]{:S(2)}) collective-permute-start(f32[200]{0:T(256)S(1)} %multiply_reduce_fusion), channel_id=1, source_target_pairs={{0,1},{1,0},{2,3},{3,2},{4,5},{5,4},{6,7},{7,6},{8,9},{9,8},{10,11... | collective-permute-start | bytes 2408 | tf_op jit(solution)/shard_map/ppermute | solution.py:31
  71.2 4.2 %collective-permute-start.3 = (bf16[16,200,128]{2,1,0:T(8,128)(2,1)S(1)}, bf16[16,200,128]{2,1,0:T(8,128)(2,1)S(1)}, u32[]{:S(2)}, u32[]{:S(2)}) collective-permute-start(bf16[16,200,128]{2,1,0:T(8,128)(2,1)S(1)} %bitcast.16), channel_id=1, source_target_pairs={{0,1},{1,0},{2,3},{3,2},{4,5},{5,4},{6,7},{7,6},{8,9},{9,8},{10,11... | collective-permute-start | bytes 2457608 | tf_op jit(solution)/shard_map/ppermute | solution.py:31
  80.7 11.6 %collective-permute-start.4 = (bf16[2,128,640]{2,1,0:T(8,128)(2,1)S(1)}, bf16[2,128,640]{2,1,0:T(8,128)(2,1)S(1)}, u32[]{:S(2)}, u32[]{:S(2)}) collective-permute-start(bf16[2,128,640]{2,1,0:T(8,128)(2,1)S(1)} %attend.1.near_ref), channel_id=1, source_target_pairs={{0,256},{256,0},{1,257},{257,1},{2,258},{258,2},{3,259},{259,3},{4... | collective-permute-start | bytes 983048 | tf_op jit(solution)/shard_map/ppermute | solution.py:31
  92.7 3.6 %collective-permute-start.5 = (bf16[256,512]{1,0:T(8,128)(2,1)S(1)}, bf16[256,512]{1,0:T(8,128)(2,1)}, u32[]{:S(2)}, u32[]{:S(2)}) collective-permute-start(bf16[256,512]{1,0:T(8,128)(2,1)S(1)} %combine.1.own_ref), channel_id=1, source_target_pairs={{0,1},{1,0},{2,3},{3,2},{4,5},{5,4},{6,7},{7,6},{8,9},{9,8},{10,11... | collective-permute-start | bytes 786440 | tf_op jit(solution)/shard_map/ppermute | solution.py:31
  125.4 9.0 %collective-permute-start.6 = (bf16[128,512]{1,0:T(8,128)(2,1)S(1)}, bf16[128,512]{1,0:T(8,128)(2,1)S(1)}, u32[]{:S(2)}, u32[]{:S(2)}) collective-permute-start(bf16[128,512]{1,0:T(8,128)(2,1)S(1)} %reduce.1), channel_id=1, source_target_pairs={{0,0},{1,1},{2,2},{3,3},{4,4},{5,5},{6,6},{7,7},{8,260},{9,261},{1... | collective-permute-start | bytes 393224 | tf_op jit(solution)/shard_map/ppermute | solution.py:42
Sparse Core Ops, SparseCore 0:
  11.8 86.9 all-gather.3

commit v13 on v12

--- a/solution.py
+++ b/solution.py
@@ -269,12 +269,13 @@
 
     place = jnp.concatenate([jnp.stack([core, ylo]).astype(jnp.int32), tile_counts])
 
+    sent = lax.dynamic_slice_in_dim(out_weight, (1 - core) * HD, HD, axis=1)
+    sent, out_weight = lax.optimization_barrier((sent, out_weight))
+    kept = lax.dynamic_slice_in_dim(out_weight, core * HD, HD, axis=1)
+    kept, got = lax.optimization_barrier((kept, swapped(sent, "core")))
+    pair = jnp.concatenate([kept, got], axis=0)
+    pair, queries = lax.optimization_barrier((pair, queries))
     query = prepare(queries, q_gain, spans)
-
-    kept = lax.dynamic_slice_in_dim(out_weight, core * HD, HD, axis=1)
-    sent = lax.dynamic_slice_in_dim(out_weight, (1 - core) * HD, HD, axis=1)
-    got, query = lax.optimization_barrier((swapped(sent, "core"), query))
-    pair = jnp.concatenate([kept, got], axis=0)
     far = swapped(query, "ylo")
     weight = lax.all_gather(pair, "z", axis=0, tiled=False)
 

time: 143 us -> 143 us (level)
  transfers between devices with their start and end apart: 8 -> 8, of which waited for: 8 -> 8; matrix products, arithmetic and copies ran while one was open for 2% -> 3% of each run, Pallas kernels for 5% -> 5%
where the time goes in v13:
time: 143 us; the launch traced here: 142 us
  blocking collectives  69.8 us (49%)
  waiting for transfers between devices  22.3 us (16%)
  starting transfers between devices  18.5 us (13%)
  between operations  13.5 us (9%)
  Pallas kernels  11.3 us (8%)
  local copies, waits for them, and re-layouts  2.65 us (2%)
  matrix products  2.65 us (2%)
    all_gather x1, blocking collectives, local(): mine = lax.all_gather(local_pair, 'z', axis=0, tiled=False)  47.7 us
    all_to_all x1, blocking collectives, local(): parts = lax.all_to_all(product, ('x', 'yhi', 'core'), 0, 0, tiled=True)  22.1 us
    ppermute x6, waiting for transfers between devices, swapped(): return lax.ppermute(value, axis, [(0, 1), (1, 0)])  16.4 us
    ppermute x6, starting transfers between devices, swapped(): return lax.ppermute(value, axis, [(0, 1), (1, 0)])  13.8 us
    pallas_call x1, Pallas kernels, attend(): pl.pallas_call(attend_kernel, in_specs=[smem(), vmem(), vmem(), vmem(), v...  5.21 us
    ppermute x1, starting transfers between devices, placed(): return lax.ppermute(value, AXES, pairs)  4.74 us
    ppermute x1, waiting for transfers between devices, placed(): return lax.ppermute(value, AXES, pairs)  4.23 us
    pallas_call x1, Pallas kernels, project(): pl.pallas_call(project_kernel, in_specs=[smem(), vmem(), hbm, hbm], out_s...  3.66 us
  transfers between devices with their start and end apart: 8, of which 8 were waited for; matrix products, arithmetic and copies ran while one was open for 3% of the time, Pallas kernels for 5%

profile of v13, /device:TPU:6, one launch (start us, length us, event | category | flops | bytes accessed | tf_op | source)
XLA Modules:
  0.0 141.7 jit_solution(16179894224068420204)
XLA Ops:
  6.5 1.1 constant_dynamic-slice_fusion.1
  7.6 1.9 %collective-permute-start = (bf16[512,128]{1,0:T(8,128)(2,1)S(1)}, bf16[512,128]{1,0:T(8,128)(2,1)S(1)}, u32[]{:S(2)}, u32[]{:S(2)}) collective-permute-start(bf16[512,128]{1,0:T(8,128)(2,1)S(1)} %constant_dynamic-slice_fusion.1), channel_id=1, source_target_pairs={{0,1},{1,0},{2,3},{3,2},{4,5},{5,4},{6,7},{7,6},{8,9},{9,8},{10,11... | collective-permute-start | bytes 393224 | tf_op jit(solution)/shard_map/ppermute | solution.py:31
  9.5 0.9 constant_dynamic-slice_fusion
  10.5 0.4 collective-permute-done
  10.8 0.7 pad_maximum_fusion
  11.6 0.0 all-gather.4.cloned.1.call-update
  11.6 1.2 prepare.1.q_ref
  12.8 0.0 copy-start.2
  12.8 3.5 %collective-permute-start.1 = (bf16[128,640]{1,0:T(8,128)(2,1)S(1)}, bf16[128,640]{1,0:T(8,128)(2,1)}, u32[]{:S(2)}, u32[]{:S(2)}) collective-permute-start(bf16[128,640]{1,0:T(8,128)(2,1)S(1)} %prepare.1.q_ref), channel_id=1, source_target_pairs={{0,256},{256,0},{1,257},{257,1},{2,258},{258,2},{3,259},{259,3},{4... | collective-permute-start | bytes 491528 | tf_op jit(solution)/shard_map/ppermute | solution.py:31
  16.3 2.7 %fusion.x_ref = f32[200,128]{1,0:T(8,128)S(1)} fusion(bf16[200,8192]{1,0:T(8,128)(2,1)S(1)} %copy-done, bf16[128,8192]{1,0:T(8,128)(2,1)} %bitcast.22), kind=kOutput, calls=%fused_computation.5 | convolution fusion | flops 419430400 | bytes 5476352 | tf_op jit(solution)/shard_map/dot_general | solution.py:283
  19.0 2.1 %collective-permute-done.1.far_ref = bf16[128,640]{1,0:T(8,128)(2,1)} collective-permute-done((bf16[128,640]{1,0:T(8,128)(2,1)S(1)}, bf16[128,640]{1,0:T(8,128)(2,1)}, u32[]{:S(2)}, u32[]{:S(2)}) %collective-permute-start.1) | collective-permute-done | bytes 163872 | tf_op jit(solution)/shard_map/ppermute | solution.py:31
  21.1 0.1 multiply_reduce_fusion
  21.2 1.9 %collective-permute-start.2 = (f32[200]{0:T(256)S(1)}, f32[200]{0:T(256)S(1)}, u32[]{:S(2)}, u32[]{:S(2)}) collective-permute-start(f32[200]{0:T(256)S(1)} %multiply_reduce_fusion), channel_id=1, source_target_pairs={{0,1},{1,0},{2,3},{3,2},{4,5},{5,4},{6,7},{7,6},{8,9},{9,8},{10,11... | collective-permute-start | bytes 2408 | tf_op jit(solution)/shard_map/ppermute | solution.py:31
  23.1 0.1 pad_add_fusion.place_ref
  23.2 1.0 collective-permute-done.2
  24.2 0.7 pack.1
  24.9 47.7 %all-gather = bf16[3200,128]{1,0:T(8,128)(2,1)S(1)} all-gather(bf16[200,128]{1,0:T(8,128)(2,1)S(1)} %pack.1), channel_id=2, replica_groups=mesh['ylo'=2,'z'=16,'x'=4,'yhi'=2,'core'=2] {'z'}, dimensions={0}, use_global_device_ids=true | all-gather | bytes 870400 | tf_op jit(solution)/shard_map/all_gather | solution.py:290
  72.6 1.9 %collective-permute-start.3 = (bf16[16,200,128]{2,1,0:T(8,128)(2,1)S(1)}, bf16[16,200,128]{2,1,0:T(8,128)(2,1)S(1)}, u32[]{:S(2)}, u32[]{:S(2)}) collective-permute-start(bf16[16,200,128]{2,1,0:T(8,128)(2,1)S(1)} %bitcast.16), channel_id=1, source_target_pairs={{0,1},{1,0},{2,3},{3,2},{4,5},{5,4},{6,7},{7,6},{8,9},{9,8},{10,11... | collective-permute-start | bytes 2457608 | tf_op jit(solution)/shard_map/ppermute | solution.py:31
  74.5 2.3 %collective-permute-done.3.theirs_ref = bf16[16,200,128]{2,1,0:T(8,128)(2,1)S(1)} collective-permute-done((bf16[16,200,128]{2,1,0:T(8,128)(2,1)S(1)}, bf16[16,200,128]{2,1,0:T(8,128)(2,1)S(1)}, u32[]{:S(2)}, u32[]{:S(2)}) %collective-permute-start.3) | collective-permute-done | bytes 819232 | tf_op jit(solution)/shard_map/ppermute | solution.py:31
  76.8 5.2 %attend.1.near_ref = bf16[2,128,640]{2,1,0:T(8,128)(2,1)S(1)} custom-call(s32[6]{0:T(128)S(1)} %pad_add_fusion.place_ref, bf16[128,640]{1,0:T(8,128)(2,1)S(1)} %prepare.1.q_ref, bf16[128,640]{1,0:T(8,128)(2,1)} %collective-permute-done.1.far_ref, bf16[16,200,128]{2,1,0:T(8,128)(2,1)S(1)} %bitcast.17, bf16[16,200,128]{2,1,0:T(8,128)(2,1)S(1)} %collective-permute-done.3.theirs_ref), custom_call_target="tpu_custom_call" | custom-call | tf_op jit(solution)/shard_map/attend/pallas_call | solution.py:163
  82.0 2.6 %collective-permute-start.4 = (bf16[2,128,640]{2,1,0:T(8,128)(2,1)S(1)}, bf16[2,128,640]{2,1,0:T(8,128)(2,1)S(1)}, u32[]{:S(2)}, u32[]{:S(2)}) collective-permute-start(bf16[2,128,640]{2,1,0:T(8,128)(2,1)S(1)} %attend.1.near_ref), channel_id=1, source_target_pairs={{0,256},{256,0},{1,257},{257,1},{2,258},{258,2},{3,259},{259,3},{4... | collective-permute-start | bytes 983048 | tf_op jit(solution)/shard_map/ppermute | solution.py:31
  84.7 9.0 %collective-permute-done.4.far_ref = bf16[2,128,640]{2,1,0:T(8,128)(2,1)S(1)} collective-permute-done((bf16[2,128,640]{2,1,0:T(8,128)(2,1)S(1)}, bf16[2,128,640]{2,1,0:T(8,128)(2,1)S(1)}, u32[]{:S(2)}, u32[]{:S(2)}) %collective-permute-start.4) | collective-permute-done | bytes 327712 | tf_op jit(solution)/shard_map/ppermute | solution.py:31
  93.7 0.4 combine.1.own_ref
  94.1 1.9 %collective-permute-start.5 = (bf16[256,512]{1,0:T(8,128)(2,1)S(1)}, bf16[256,512]{1,0:T(8,128)(2,1)}, u32[]{:S(2)}, u32[]{:S(2)}) collective-permute-start(bf16[256,512]{1,0:T(8,128)(2,1)S(1)} %combine.1.own_ref), channel_id=1, source_target_pairs={{0,1},{1,0},{2,3},{3,2},{4,5},{5,4},{6,7},{7,6},{8,9},{9,8},{10,11... | collective-permute-start | bytes 786440 | tf_op jit(solution)/shard_map/ppermute | solution.py:31
  96.0 1.6 %collective-permute-done.5.other_hbm = bf16[256,512]{1,0:T(8,128)(2,1)} collective-permute-done((bf16[256,512]{1,0:T(8,128)(2,1)S(1)}, bf16[256,512]{1,0:T(8,128)(2,1)}, u32[]{:S(2)}, u32[]{:S(2)}) %collective-permute-start.5) | collective-permute-done | bytes 262176 | tf_op jit(solution)/shard_map/ppermute | solution.py:31
  97.6 1.6 %all-gather.4.cloned.1.call-done = bf16[16384,128]{1,0:T(8,128)(2,1)} async-done(((bf16[1024,128]{1,0:T(8,128)(2,1)}), bf16[16384,128]{1,0:T(8,128)(2,1)}) %all-gather.4.cloned.1.call-update) | async-done | bytes 4194320 | tf_op jit(solution)/shard_map/all_gather | solution.py:280
  99.3 3.7 %project.1 = bf16[2,8,128,256]{3,2,1,0:T(8,128)(2,1)S(1)} custom-call(s32[6]{0:T(128)S(1)} %pad_add_fusion.place_ref, bf16[256,512]{1,0:T(8,128)(2,1)S(1)} %combine.1.own_ref, bf16[256,512]{1,0:T(8,128)(2,1)} %collective-permute-done.5.other_hbm, bf16[16,1024,128]{2,1,0:T(8,128)(2,1)} %bitcast.21), custom_call_target="tpu_custom_call" | custom-call | tf_op jit(solution)/shard_map/project/pallas_call | solution.py:224
  103.0 22.1 %all_to_all.5.x_ref = bf16[16,128,256]{2,1,0:T(8,128)(2,1)S(1)} all-to-all(bf16[16,128,256]{2,1,0:T(8,128)(2,1)S(1)} %bitcast.15), channel_id=1, replica_groups=mesh['ylo'=2,'z'=16,'x'=4,'yhi'=2,'core'=2] {'x','yhi','core'}, dimensions={0} | all-to-all | bytes 2097152 | tf_op jit(solution)/shard_map/all_to_all | solution.py:298
  125.1 0.1 reduce.1
  125.2 4.7 %collective-permute-start.6 = (bf16[128,512]{1,0:T(8,128)(2,1)S(1)}, bf16[128,512]{1,0:T(8,128)(2,1)S(1)}, u32[]{:S(2)}, u32[]{:S(2)}) collective-permute-start(bf16[128,512]{1,0:T(8,128)(2,1)S(1)} %reduce.1), channel_id=1, source_target_pairs={{0,0},{1,1},{2,2},{3,3},{4,4},{5,5},{6,6},{7,7},{8,260},{9,261},{1... | collective-permute-start | bytes 393224 | tf_op jit(solution)/shard_map/ppermute | solution.py:42
  130.0 4.2 %collective-permute-done.6 = bf16[128,512]{1,0:T(8,128)(2,1)S(1)} collective-permute-done((bf16[128,512]{1,0:T(8,128)(2,1)S(1)}, bf16[128,512]{1,0:T(8,128)(2,1)S(1)}, u32[]{:S(2)}, u32[]{:S(2)}) %collective-permute-start.6) | collective-permute-done | bytes 131104 | tf_op jit(solution)/shard_map/ppermute | solution.py:42
  134.2 0.7 copy.10
  (6 shorter events, 0.0 us)
Async XLA Ops:
  6.5 9.8 %copy-start = (bf16[200,8192]{1,0:T(8,128)(2,1)S(1)}, bf16[200,8192]{1,0:T(8,128)(2,1)}, u32[]{:S(2)}) copy-start(bf16[200,8192]{1,0:T(8,128)(2,1)} %param.9) | copy-start | bytes 9830404
  6.5 92.7 %all-gather.4.cloned.1.call-start = ((), (), s32[]{:S(2)}) async-start(), calls=%async_computation.1 | async-start | bytes 4456448 | tf_op jit(solution)/shard_map/all_gather | solution.py:280
  7.6 3.2 %collective-permute-start = (bf16[512,128]{1,0:T(8,128)(2,1)S(1)}, bf16[512,128]{1,0:T(8,128)(2,1)S(1)}, u32[]{:S(2)}, u32[]{:S(2)}) collective-permute-start(bf16[512,128]{1,0:T(8,128)(2,1)S(1)} %constant_dynamic-slice_fusion.1), channel_id=1, source_target_pairs={{0,1},{1,0},{2,3},{3,2},{4,5},{5,4},{6,7},{7,6},{8,9},{9,8},{10,11... | collective-permute-start | bytes 393224 | tf_op jit(solution)/shard_map/ppermute | solution.py:31
  12.8 10.3 %copy-start.2 = (s32[4]{0:T(128)S(1)}, s32[4]{0:T(128)}, u32[]{:S(2)}) copy-start(s32[4]{0:T(128)} %param.14) | copy-start | bytes 52
  12.8 11.4 %copy-start.1 = (f32[128]{0:T(128)S(1)}, f32[128]{0:T(128)}, u32[]{:S(2)}) copy-start(f32[128]{0:T(128)} %param.13) | copy-start | bytes 1540
  12.8 8.3 %collective-permute-start.1 = (bf16[128,640]{1,0:T(8,128)(2,1)S(1)}, bf16[128,640]{1,0:T(8,128)(2,1)}, u32[]{:S(2)}, u32[]{:S(2)}) collective-permute-start(bf16[128,640]{1,0:T(8,128)(2,1)S(1)} %prepare.1.q_ref), channel_id=1, source_target_pairs={{0,256},{256,0},{1,257},{257,1},{2,258},{258,2},{3,259},{259,3},{4... | collective-permute-start | bytes 491528 | tf_op jit(solution)/shard_map/ppermute | solution.py:31
  21.2 3.0 %collective-permute-start.2 = (f32[200]{0:T(256)S(1)}, f32[200]{0:T(256)S(1)}, u32[]{:S(2)}, u32[]{:S(2)}) collective-permute-start(f32[200]{0:T(256)S(1)} %multiply_reduce_fusion), channel_id=1, source_target_pairs={{0,1},{1,0},{2,3},{3,2},{4,5},{5,4},{6,7},{7,6},{8,9},{9,8},{10,11... | collective-permute-start | bytes 2408 | tf_op jit(solution)/shard_map/ppermute | solution.py:31
  72.6 4.2 %collective-permute-start.3 = (bf16[16,200,128]{2,1,0:T(8,128)(2,1)S(1)}, bf16[16,200,128]{2,1,0:T(8,128)(2,1)S(1)}, u32[]{:S(2)}, u32[]{:S(2)}) collective-permute-start(bf16[16,200,128]{2,1,0:T(8,128)(2,1)S(1)} %bitcast.16), channel_id=1, source_target_pairs={{0,1},{1,0},{2,3},{3,2},{4,5},{5,4},{6,7},{7,6},{8,9},{9,8},{10,11... | collective-permute-start | bytes 2457608 | tf_op jit(solution)/shard_map/ppermute | solution.py:31
  82.0 11.6 %collective-permute-start.4 = (bf16[2,128,640]{2,1,0:T(8,128)(2,1)S(1)}, bf16[2,128,640]{2,1,0:T(8,128)(2,1)S(1)}, u32[]{:S(2)}, u32[]{:S(2)}) collective-permute-start(bf16[2,128,640]{2,1,0:T(8,128)(2,1)S(1)} %attend.1.near_ref), channel_id=1, source_target_pairs={{0,256},{256,0},{1,257},{257,1},{2,258},{258,2},{3,259},{259,3},{4... | collective-permute-start | bytes 983048 | tf_op jit(solution)/shard_map/ppermute | solution.py:31
  94.1 3.6 %collective-permute-start.5 = (bf16[256,512]{1,0:T(8,128)(2,1)S(1)}, bf16[256,512]{1,0:T(8,128)(2,1)}, u32[]{:S(2)}, u32[]{:S(2)}) collective-permute-start(bf16[256,512]{1,0:T(8,128)(2,1)S(1)} %combine.1.own_ref), channel_id=1, source_target_pairs={{0,1},{1,0},{2,3},{3,2},{4,5},{5,4},{6,7},{7,6},{8,9},{9,8},{10,11... | collective-permute-start | bytes 786440 | tf_op jit(solution)/shard_map/ppermute | solution.py:31
  125.2 9.0 %collective-permute-start.6 = (bf16[128,512]{1,0:T(8,128)(2,1)S(1)}, bf16[128,512]{1,0:T(8,128)(2,1)S(1)}, u32[]{:S(2)}, u32[]{:S(2)}) collective-permute-start(bf16[128,512]{1,0:T(8,128)(2,1)S(1)} %reduce.1), channel_id=1, source_target_pairs={{0,0},{1,1},{2,2},{3,3},{4,4},{5,5},{6,6},{7,7},{8,260},{9,261},{1... | collective-permute-start | bytes 393224 | tf_op jit(solution)/shard_map/ppermute | solution.py:42
Sparse Core Ops, SparseCore 0:
  11.7 87.5 all-gather.3
